TPU v7x, 512 devices: a whole 4x4x16 slice. The times are simulated.
512 devices in a mesh: row: 16 (over z_lo, y), col: 32 (over x, z_hi, core).
Axes of the slice: x: 4, y: 4, z: 16 (z_hi: 4, z_lo: 4; z = z_hi * 4 + z_lo), core: 2. Of those that a mesh axis runs over, the one named last changes fastest.
Arguments:
- tiles: bfloat16 [16, 32, 32, 128, 128], P('row', 'col'), may hold values from -0.5 to 0.5
- tile_slots: int32 [16, 32, 32], P('row', 'col'), may hold values from 0 to 191, as said below
- tile_counts: int32 [16, 32], P('row', 'col'), may hold values from 8 to 32, as said below
- user_degree: int32 [32768], P('row'), may hold values from 1 to 64
- item_degree: int32 [49152], P('col'), may hold values from 1 to 64
- start_panel: float32 [64, 49152], P(None, ('col', 'row')), may hold values from -6 to 6
Outputs:
- left_panel: float32 [64, 32768], P(None, ('row', 'col'))
- right_panel: float32 [64, 49152], P(None, ('col', 'row'))
- left_factors: float32 [3, 64, 64], replicated
- right_factors: float32 [3, 64, 64], replicated
Inputs may be any that keep to these rules, and one draw needn't show every extreme that they name: `tile_slots`: within one grid cell the 32 slot numbers are distinct; slot s is local tile row s // 12 and local tile column s % 12; entries from position tile_counts on are padding. `tile_counts`: some grid cell holds 32 live tiles.
All inputs are finite; a program needn't handle non-finite values.
Results may differ from a plain program's by a relative error of at most 0.0005.
Values sent between devices are 32-bit elements; how exact they have to be, the bound alone decides.
No kernel may reach another device: no remote copies, remote signals or barrier semaphores. Data moves between devices by JAX's collectives and lax.ppermute only.
A program may use at most 64 MiB of HBM per device.

v0:
```python
import math

import jax
import jax.numpy as jnp
from jax import lax
from jax.sharding import PartitionSpec as P

STEPS = 3


HIGH = lax.Precision.HIGHEST


def gram_of(vectors):
    return jnp.einsum("bn,cn->bc", vectors, vectors, precision=HIGH)


def solve_lower(factor, vectors):
    return lax.linalg.triangular_solve(factor, vectors, left_side=True, lower=True)


def per_device(tiles, tile_slots, tile_counts, user_degree, item_degree, start_panel):
    tile_stack = tiles[0, 0].astype(jnp.float32)
    slot_list = tile_slots[0, 0]
    tile_total = tile_counts[0, 0]
    slot_count = tile_stack.shape[0]
    tile_width = tile_stack.shape[1]
    row_blocks = user_degree.shape[0] // tile_width
    col_blocks = item_degree.shape[0] // tile_width
    block_width = start_panel.shape[0]
    live_mask = jnp.arange(slot_count) < tile_total
    local_rows = slot_list // col_blocks
    local_cols = slot_list % col_blocks
    row_select = (
        (local_rows[:, None] == jnp.arange(row_blocks)[None, :]) & live_mask[:, None]
    ).astype(jnp.float32)
    col_select = (
        (local_cols[:, None] == jnp.arange(col_blocks)[None, :]) & live_mask[:, None]
    ).astype(jnp.float32)
    user_scale = lax.rsqrt(user_degree.astype(jnp.float32))
    item_scale = lax.rsqrt(item_degree.astype(jnp.float32))
    user_group = row_blocks * tile_width // lax.axis_size("col")
    item_group = col_blocks * tile_width // lax.axis_size("row")
    user_offset = lax.axis_index("col") * user_group
    item_offset = lax.axis_index("row") * item_group
    user_scale_own = lax.dynamic_slice_in_dim(user_scale, user_offset, user_group)
    item_scale_own = lax.dynamic_slice_in_dim(item_scale, item_offset, item_group)
    start_total = lax.psum(gram_of(start_panel), ("row", "col"))
    start_factor = jnp.linalg.cholesky(start_total)
    item_basis = solve_lower(start_factor, start_panel)
    user_basis = start_panel[:, :0]
    item_factor = start_factor
    user_list = []
    item_list = []
    for iteration in range(STEPS):
        scaled = item_basis * item_scale_own[None, :]
        item_full = lax.all_gather(scaled, "row", axis=1, tiled=True)
        forward_panel_blocks = item_full.reshape(block_width, col_blocks, tile_width)
        forward_chosen = jnp.take(forward_panel_blocks, local_cols, axis=1)
        forward_partial_value = jnp.einsum(
            "mrc,bmc->bmr", tile_stack, forward_chosen, precision=HIGH
        )
        forward_summed = jnp.einsum(
            "bmr,mk->bkr", forward_partial_value, row_select, precision=HIGH
        )
        forward = (
            lax.psum_scatter(
                forward_summed.reshape(block_width, row_blocks * tile_width),
                "col",
                scatter_dimension=1,
                tiled=True,
            )
            * user_scale_own[None, :]
        )
        if iteration > 0:
            forward = forward - jnp.dot(item_factor.T, user_basis, precision=HIGH)
        user_factor = jnp.linalg.cholesky(lax.psum(gram_of(forward), ("row", "col")))
        user_basis = solve_lower(user_factor, forward)
        scaled = user_basis * user_scale_own[None, :]
        user_full = lax.all_gather(scaled, "col", axis=1, tiled=True)
        panel_blocks = user_full.reshape(block_width, row_blocks, tile_width)
        chosen = jnp.take(panel_blocks, local_rows, axis=1)
        partial_value = jnp.einsum("mrc,bmr->bmc", tile_stack, chosen, precision=HIGH)
        summed = jnp.einsum("bmc,mk->bkc", partial_value, col_select, precision=HIGH)
        backward = (
            lax.psum_scatter(
                summed.reshape(block_width, col_blocks * tile_width),
                "row",
                scatter_dimension=1,
                tiled=True,
            )
            * item_scale_own[None, :]
        )
        backward = backward - jnp.dot(user_factor.T, item_basis, precision=HIGH)
        item_factor = jnp.linalg.cholesky(lax.psum(gram_of(backward), ("row", "col")))
        item_basis = solve_lower(item_factor, backward)
        user_list.append(user_factor)
        item_list.append(item_factor)
    user_total = row_blocks * tile_width * lax.axis_size("row")
    item_total = col_blocks * tile_width * lax.axis_size("col")
    return (
        math.sqrt(user_total) * user_basis,
        math.sqrt(item_total) * item_basis,
        jnp.stack(user_list),
        jnp.stack(item_list),
    )


def solution(mesh):
    in_specs = (
        P("row", "col", None, None, None),
        P("row", "col", None),
        P("row", "col"),
        P("row"),
        P("col"),
        P(None, ("col", "row")),
    )
    out_specs = (P(None, ("row", "col")), P(None, ("col", "row")), P(), P())
    return jax.shard_map(
        per_device, mesh=mesh, in_specs=in_specs, out_specs=out_specs, check_vma=False
    )
```

profile of v0, /device:TPU:1, one launch (start us, length us, event | category | flops | bytes accessed | tf_op | source)
XLA Modules:
  0.0 1727.9 jit_solution(9248479124465914468)
XLA Ops:
  9.7 111.2 %psum.49 = f32[64,64]{0,1:T(8,128)S(1)} all-reduce(f32[64,64]{0,1:T(8,128)S(1)} %fusion.153), channel_id=1, replica_groups=mesh['row'=16,'col'=32] {'row','col'}, use_global_device_ids=true, to_apply=%region_0.1 | all-reduce | flops 4096 | bytes 32768 | tf_op jit(solution)/shard_map/psum | solution.py:48
  120.9 5.8 cholesky.119
  128.1 4.9 custom-call.13
  134.1 33.8 %all-gather = f32[16,96,64]{1,2,0:T(8,128)S(1)} all-gather(f32[1,96,64]{1,2,0:T(8,128)S(1)} %multiply_bitcast_fusion.2), channel_id=1, replica_groups=mesh['row'=16,'col'=32] {'row'}, dimensions={0}, use_global_device_ids=true | all-gather | bytes 417792 | tf_op jit(solution)/shard_map/all_gather | solution.py:57
  169.1 2.2 convolution_bitcast_fusion.5
  171.3 1.1 convolution_bitcast_fusion.11
  172.4 1.4 copy.162
  174.6 110.4 %reduce-scatter.19.cloned.1.call-done = f32[64,64]{1,0:T(8,128)} async-done(((f32[2048,64]{1,0:T(8,128)}), f32[64,64]{1,0:T(8,128)}) %reduce-scatter.19.cloned.1.call-update) | async-done | bytes 16400
  286.0 101.8 %psum.50 = f32[64,64]{0,1:T(8,128)S(1)} all-reduce(f32[64,64]{0,1:T(8,128)S(1)} %fusion.81), channel_id=1, replica_groups=mesh['row'=16,'col'=32] {'row','col'}, use_global_device_ids=true, to_apply=%region_4.8 | all-reduce | flops 4096 | bytes 32768 | tf_op jit(solution)/shard_map/psum | solution.py:77
  388.0 5.8 cholesky.130
  395.1 4.9 custom-call.14
  400.4 57.0 %all_gather.19 = f32[64,2048]{0,1:T(8,128)S(1)} all-gather(f32[64,64]{0,1:T(8,128)S(1)} %copy.109), channel_id=1, replica_groups=mesh['row'=16,'col'=32] {'col'}, dimensions={1}, use_global_device_ids=true | all-gather | bytes 540672 | tf_op jit(solution)/shard_map/all_gather | solution.py:80
  459.3 1.1 convolution_bitcast_fusion.10
  460.4 1.2 copy.163
  461.6 71.2 %reduce-scatter.21.cloned.1.call-done = f32[96,64]{1,0:T(8,128)} async-done(((f32[1536,64]{1,0:T(8,128)}), f32[96,64]{1,0:T(8,128)}) %reduce-scatter.21.cloned.1.call-update) | async-done | bytes 24592
  534.8 112.8 %psum.51 = f32[64,64]{0,1:T(8,128)S(1)} all-reduce(f32[64,64]{0,1:T(8,128)S(1)} %fusion.154), channel_id=1, replica_groups=mesh['row'=16,'col'=32] {'row','col'}, use_global_device_ids=true, to_apply=%region_6.12 | all-reduce | flops 4096 | bytes 32768 | tf_op jit(solution)/shard_map/psum | solution.py:95
  647.7 5.8 cholesky.141
  654.9 4.9 custom-call.15
  660.0 36.4 %all-gather.1 = f32[16,96,64]{1,2,0:T(8,128)S(1)} all-gather(f32[1,96,64]{1,2,0:T(8,128)S(1)} %multiply_bitcast_fusion.1), channel_id=1, replica_groups=mesh['row'=16,'col'=32] {'row'}, dimensions={0}, use_global_device_ids=true | all-gather | bytes 417792 | tf_op jit(solution)/shard_map/all_gather | solution.py:57
  697.6 2.2 convolution_bitcast_fusion.3
  699.8 1.1 convolution_bitcast_fusion.9
  700.9 1.4 copy.164
  702.3 110.1 %reduce-scatter.23.cloned.1.call-done = f32[64,64]{1,0:T(8,128)} async-done(((f32[2048,64]{1,0:T(8,128)}), f32[64,64]{1,0:T(8,128)}) %reduce-scatter.23.cloned.1.call-update) | async-done | bytes 16400
  814.3 102.0 %psum.52 = f32[64,64]{0,1:T(8,128)S(1)} all-reduce(f32[64,64]{0,1:T(8,128)S(1)} %fusion.155), channel_id=1, replica_groups=mesh['row'=16,'col'=32] {'row','col'}, use_global_device_ids=true, to_apply=%region_8.14 | all-reduce | flops 4096 | bytes 32768 | tf_op jit(solution)/shard_map/psum | solution.py:77
  916.4 5.8 cholesky.152
  923.6 4.9 custom-call.16
  928.9 56.4 %all_gather.21 = f32[64,2048]{0,1:T(8,128)S(1)} all-gather(f32[64,64]{0,1:T(8,128)S(1)} %copy.120), channel_id=1, replica_groups=mesh['row'=16,'col'=32] {'col'}, dimensions={1}, use_global_device_ids=true | all-gather | bytes 540672 | tf_op jit(solution)/shard_map/all_gather | solution.py:80
  987.2 1.1 convolution_bitcast_fusion.8
  988.3 1.2 copy.165
  989.6 70.9 %reduce-scatter.25.cloned.1.call-done = f32[96,64]{1,0:T(8,128)} async-done(((f32[1536,64]{1,0:T(8,128)}), f32[96,64]{1,0:T(8,128)}) %reduce-scatter.25.cloned.1.call-update) | async-done | bytes 24592
  1062.5 113.1 %psum.53 = f32[64,64]{0,1:T(8,128)S(1)} all-reduce(f32[64,64]{0,1:T(8,128)S(1)} %fusion.156), channel_id=1, replica_groups=mesh['row'=16,'col'=32] {'row','col'}, use_global_device_ids=true, to_apply=%region_10.16 | all-reduce | flops 4096 | bytes 32768 | tf_op jit(solution)/shard_map/psum | solution.py:95
  1175.6 5.8 cholesky.163
  1182.8 4.9 custom-call.17
  1188.0 36.7 %all-gather.2 = f32[16,96,64]{1,2,0:T(8,128)S(1)} all-gather(f32[1,96,64]{1,2,0:T(8,128)S(1)} %multiply_bitcast_fusion), channel_id=1, replica_groups=mesh['row'=16,'col'=32] {'row'}, dimensions={0}, use_global_device_ids=true | all-gather | bytes 417792 | tf_op jit(solution)/shard_map/all_gather | solution.py:57
  1225.9 2.2 convolution_bitcast_fusion.1
  1228.0 1.1 convolution_bitcast_fusion.7
  1229.1 1.4 copy.166
  1230.5 110.1 %reduce-scatter.27.cloned.1.call-done = f32[64,64]{1,0:T(8,128)} async-done(((f32[2048,64]{1,0:T(8,128)}), f32[64,64]{1,0:T(8,128)}) %reduce-scatter.27.cloned.1.call-update) | async-done | bytes 16400
  1342.5 101.8 %psum.54 = f32[64,64]{0,1:T(8,128)S(1)} all-reduce(f32[64,64]{0,1:T(8,128)S(1)} %fusion.157), channel_id=1, replica_groups=mesh['row'=16,'col'=32] {'row','col'}, use_global_device_ids=true, to_apply=%region_12.18 | all-reduce | flops 4096 | bytes 32768 | tf_op jit(solution)/shard_map/psum | solution.py:77
  1444.4 5.8 cholesky.174
  1451.6 4.9 custom-call.18
  1457.5 56.3 %all_gather.23 = f32[64,2048]{0,1:T(8,128)S(1)} all-gather(f32[64,64]{0,1:T(8,128)S(1)} %copy.131), channel_id=1, replica_groups=mesh['row'=16,'col'=32] {'col'}, dimensions={1}, use_global_device_ids=true | all-gather | bytes 540672 | tf_op jit(solution)/shard_map/all_gather | solution.py:80
  1515.7 1.1 convolution_bitcast_fusion.6
  1516.8 1.2 copy.167
  1518.7 73.4 %reduce-scatter.29.cloned.1.call-done = f32[96,64]{1,0:T(8,128)} async-done(((f32[1536,64]{1,0:T(8,128)}), f32[96,64]{1,0:T(8,128)}) %reduce-scatter.29.cloned.1.call-update) | async-done | bytes 24592
  1594.0 113.0 %psum.55 = f32[64,64]{0,1:T(8,128)S(1)} all-reduce(f32[64,64]{0,1:T(8,128)S(1)} %fusion.158), channel_id=1, replica_groups=mesh['row'=16,'col'=32] {'row','col'}, use_global_device_ids=true, to_apply=%region_14.20 | all-reduce | flops 4096 | bytes 32768 | tf_op jit(solution)/shard_map/psum | solution.py:95
  1707.1 5.8 cholesky.185
  1714.3 4.9 custom-call.19
  (114 shorter events, 38.1 us)
Async XLA Ops:
  7.2 161.9 %copy-start = (bf16[1,1,32,128,128]{4,3,2,1,0:T(8,128)(2,1)S(1)}, bf16[1,1,32,128,128]{4,3,2,1,0:T(8,128)(2,1)}, u32[]{:S(2)}) copy-start(bf16[1,1,32,128,128]{4,3,2,1,0:T(8,128)(2,1)} %param.15) | copy-start | bytes 3145732
  7.2 277.8 %reduce-scatter.19.cloned.1.call-start = ((), (), s32[]{:S(2)}) async-start(), calls=%async_computation.6 | async-start | bytes 1081344
  8.0 0.7 copy-start.2
  127.5 5.6 copy-start.1
  173.7 359.1 %reduce-scatter.21.cloned.1.call-start = ((), (), s32[]{:S(2)}) async-start(), calls=%async_computation.7 | async-start | bytes 835584
  461.6 350.8 %reduce-scatter.23.cloned.1.call-start = ((), (), s32[]{:S(2)}) async-start(), calls=%async_computation.8 | async-start | bytes 1081344
  702.3 358.2 %reduce-scatter.25.cloned.1.call-start = ((), (), s32[]{:S(2)}) async-start(), calls=%async_computation.9 | async-start | bytes 835584
  989.5 351.1 %reduce-scatter.27.cloned.1.call-start = ((), (), s32[]{:S(2)}) async-start(), calls=%async_computation.10 | async-start | bytes 1081344
  1230.5 361.6 %reduce-scatter.29.cloned.1.call-start = ((), (), s32[]{:S(2)}) async-start(), calls=%async_computation.11 | async-start | bytes 835584
Sparse Core Ops, SparseCore 0:
  173.9 111.0 reduce-scatter.18
  461.7 71.0 reduce-scatter.20
  702.4 109.9 reduce-scatter.22
  989.6 70.8 reduce-scatter.24
  1230.6 109.9 reduce-scatter.26
  1518.1 73.8 reduce-scatter.28
where the time goes:
time: 1740 us; the launch traced here: 1730 us
  blocking collectives  1030 us (59%)
  waiting for transfers between devices  546 us (31%)
  other arithmetic  87.5 us (5%)
  matrix products  25.6 us (1%)
  local copies, waits for them, and re-layouts  20.4 us (1%)
    unnamed x12, waiting for transfers between devices  546 us
    psum x3, blocking collectives, per_device(): lax.psum(gram_of(backward), ('row', 'col'))  339 us
    psum x3, blocking collectives, per_device(): lax.psum(gram_of(forward), ('row', 'col'))  306 us
    all_gather x3, blocking collectives, per_device(): user_full = lax.all_gather(scaled, 'col', axis=1, tiled=True)  170 us
    psum x1, blocking collectives, per_device(): start_total = lax.psum(gram_of(start_panel), ('row', 'col'))  111 us
    all_gather x3, blocking collectives, per_device(): item_full = lax.all_gather(scaled, 'row', axis=1, tiled=True)  107 us
    another operation x8, other arithmetic, solve_lower(): lax.linalg.triangular_solve(factor, vectors, left_side=True, lower=True)  34.9 us
  transfers between devices with their start and end apart: 6, of which 6 were waited for; matrix products, arithmetic and copies ran while one was open for 0% of the time, Pallas kernels for 0%

commit v1 on v0

v1 whole, which is shorter than its diff:
```python
import functools
import math

import jax
import jax.numpy as jnp
from jax import lax
from jax.experimental import pallas as pl
from jax.experimental.pallas import tpu as pltpu
from jax.sharding import Mesh
from jax.sharding import PartitionSpec as P

STEPS = 3
TILE = 128
BLOCK = 64
HIGH = lax.Precision.HIGHEST

ROW = ("zl", "y")
COL = ("x", "zh", "core")
NEAR = ("x", "core")


def factor_rows(gram_ref, out_ref):
    gram = gram_ref[:, :BLOCK]
    eye = (
        lax.broadcasted_iota(jnp.int32, (BLOCK, BLOCK), 0)
        == lax.broadcasted_iota(jnp.int32, (BLOCK, BLOCK), 1)
    ).astype(jnp.float32)
    whole = jnp.concatenate([gram, eye], axis=1)
    groups = [whole[8 * i : 8 * i + 8] for i in range(BLOCK // 8)]
    for j in range(BLOCK):
        first = j // 8
        k = j % 8
        row = groups[first][k : k + 1]
        root = lax.rsqrt(row[:, j : j + 1])
        scaled = row * root
        out_ref[j : j + 1, :] = scaled
        for i in range(first, BLOCK // 8):
            groups[i] = groups[i] - (groups[i][:, j : j + 1] * root) * scaled


def split_three(value):
    high = value.astype(jnp.bfloat16)
    rest = value - high.astype(jnp.float32)
    middle = rest.astype(jnp.bfloat16)
    low = (rest - middle.astype(jnp.float32)).astype(jnp.bfloat16)
    return jnp.concatenate([high, middle, low], axis=0)


def product(slots_ref, count_ref, tiles_ref, parts_ref, sent_ref, forward, cb):
    count = count_ref[0]
    group = 4

    def visit(step, carry):
        added = []
        for g in range(group):
            t = step * group + g
            slot = slots_ref[t]
            local_row = slot // cb
            local_col = slot - local_row * cb
            source, target = (
                (local_col, local_row) if forward else (local_row, local_col)
            )
            tile = tiles_ref[t]
            tile = jnp.where(t < count, tile, jnp.zeros_like(tile))
            parts = parts_ref[pl.ds(pl.multiple_of(source * 192, 64), 192), :]
            dims = (((1,), (1 if forward else 0,)), ((), ()))
            value = lax.dot_general(
                parts, tile, dims, preferred_element_type=jnp.float32
            )
            added.append((target, value[:64] + value[64:128] + value[128:]))
        for target, value in added:
            where = pl.ds(pl.multiple_of(target * 64, 64), 64)
            sent_ref[where, :] += value
        return carry

    lax.fori_loop(0, (count + group - 1) // group, visit, 0)


def send_panel(
    slots_ref, count_ref, tiles_ref, panel_ref, scale_ref, parts_ref, sent_ref, *,
    forward, cb, blocks, targets,
):
    sent_ref[...] = jnp.zeros_like(sent_ref)
    gram = jnp.zeros((BLOCK, BLOCK), jnp.float32)
    for b in range(blocks):
        value = panel_ref[64 * b : 64 * b + 64, :]
        gram += lax.dot_general(
            value, value, (((1,), (1,)), ((), ())), precision=HIGH,
            preferred_element_type=jnp.float32,
        )
        parts_ref[192 * b : 192 * b + 192, :] = split_three(
            value * scale_ref[b : b + 1, :]
        )
    product(slots_ref, count_ref, tiles_ref, parts_ref, sent_ref, forward, cb)
    sent_ref[64 * targets : 64 * targets + 64, :BLOCK] = gram


def start_kernel(
    slots_ref, count_ref, tiles_ref, panel_ref, scale_ref, sent_ref, parts_ref, *, blocks, targets, cb
):
    send_panel(
        slots_ref, count_ref, tiles_ref, panel_ref, scale_ref, parts_ref, sent_ref,
        forward=True, cb=cb, blocks=blocks, targets=targets,
    )


def mix(got_ref, old_ref, old_factor_ref, scale_ref, panel_ref, factor_ref, blocks):
    factor_rows(got_ref.at[64 * blocks : 64 * blocks + 64, :], factor_ref)
    inverse = factor_ref[:, BLOCK:]
    if old_ref is not None:
        upper_mask = lax.broadcasted_iota(
            jnp.int32, (BLOCK, BLOCK), 0
        ) <= lax.broadcasted_iota(jnp.int32, (BLOCK, BLOCK), 1)
        upper = jnp.where(upper_mask, factor_ref[:, :BLOCK], 0.0)
        back = jnp.dot(
            upper, old_factor_ref[:, BLOCK:], precision=HIGH,
            preferred_element_type=jnp.float32,
        )
        weights = jnp.concatenate([inverse, -back], axis=1)
    else:
        weights = inverse
    for b in range(blocks):
        value = got_ref[64 * b : 64 * b + 64, :] * scale_ref[b : b + 1, :]
        if old_ref is not None:
            value = jnp.concatenate([value, old_ref[64 * b : 64 * b + 64, :]], axis=0)
        panel_ref[64 * b : 64 * b + 64, :] = jnp.dot(
            weights, value, precision=HIGH, preferred_element_type=jnp.float32
        )


def step_kernel(*refs, forward, cb, blocks, targets, with_old, last):
    refs = list(refs)
    if not last:
        slots_ref, count_ref, tiles_ref = refs[:3]
        refs = refs[3:]
    got_ref, scale_ref = refs[:2]
    refs = refs[2:]
    old_ref = old_factor_ref = None
    if with_old:
        old_ref, old_factor_ref = refs[:2]
        refs = refs[2:]
    panel_ref, factor_ref, sent_ref = refs[:3]
    mix(got_ref, old_ref, old_factor_ref, scale_ref, panel_ref, factor_ref, blocks)
    if last:
        gram = jnp.zeros((BLOCK, BLOCK), jnp.float32)
        for b in range(blocks):
            value = panel_ref[64 * b : 64 * b + 64, :]
            gram += lax.dot_general(
                value, value, (((1,), (1,)), ((), ())), precision=HIGH,
                preferred_element_type=jnp.float32,
            )
        sent_ref[...] = jnp.concatenate([gram, jnp.zeros_like(gram)], axis=1)
    else:
        send_panel(
            slots_ref, count_ref, tiles_ref, panel_ref, scale_ref, refs[3], sent_ref,
            forward=forward, cb=cb, blocks=blocks, targets=targets,
        )


def end_kernel(gram_ref, right_ref, left_ref, left_factor_ref, out_right_ref, out_left_ref, factor_ref, *, left_size, right_size):
    factor_rows(gram_ref, factor_ref)
    out_right_ref[...] = math.sqrt(right_size) * jnp.dot(
        factor_ref[:, BLOCK:], right_ref[...], precision=HIGH,
        preferred_element_type=jnp.float32,
    )
    out_left_ref[...] = math.sqrt(left_size) * jnp.dot(
        left_factor_ref[:, BLOCK:], left_ref[...], precision=HIGH,
        preferred_element_type=jnp.float32,
    )


SMEM = pl.BlockSpec(memory_space=pltpu.SMEM)
VMEM = pl.BlockSpec(memory_space=pltpu.VMEM)
PARAMS = pltpu.CompilerParams(vmem_limit_bytes=32 * 1024 * 1024)


def f32(*shape):
    return jax.ShapeDtypeStruct(shape, jnp.float32)


def gather_whole(value, axes, count):
    copies = jnp.broadcast_to(value[None], (count,) + value.shape)
    return lax.all_to_all(copies, axes, 0, 0, tiled=True)


def sum_col(sent):
    near = lax.axis_size(NEAR)
    rows = sent.shape[0] // near
    own = jnp.sum(
        lax.all_to_all(sent.reshape(near, rows, TILE), NEAR, 0, 0, tiled=True), axis=0
    )
    own = jnp.sum(lax.all_gather(own, "zh", axis=0, tiled=False), axis=0)
    return gather_whole(own, NEAR, near).reshape(sent.shape)


def sum_row(sent):
    count = lax.axis_size(ROW)
    rows = sent.shape[0] // count
    own = jnp.sum(
        lax.all_to_all(sent.reshape(count, rows, TILE), ROW, 0, 0, tiled=True), axis=0
    )
    return gather_whole(own, ROW, count).reshape(sent.shape)


def per_device(tiles, tile_slots, tile_counts, user_degree, item_degree, start_panel):
    tile_stack = tiles[0, 0]
    slots = tile_slots[0, 0]
    count = tile_counts[0]
    rb = user_degree.shape[0] // TILE
    cb = item_degree.shape[0] // TILE
    rows = lax.axis_size(ROW)
    cols = lax.axis_size(COL)
    user_rows = BLOCK * (rb + 1)
    item_rows = -(-BLOCK * (cb + 1) // (8 * rows)) * (8 * rows)
    user_scale = lax.rsqrt(user_degree.astype(jnp.float32)).reshape(rb, TILE)
    item_scale = lax.rsqrt(item_degree.astype(jnp.float32)).reshape(cb, TILE)

    start = gather_whole(start_panel, ROW, rows)
    start = jnp.transpose(start, (1, 0, 2)).reshape(BLOCK, cb, TILE)
    start = jnp.transpose(start, (1, 0, 2)).reshape(cb * BLOCK, TILE)

    sent = pl.pallas_call(
        functools.partial(start_kernel, blocks=cb, targets=rb, cb=cb),
        out_shape=f32(user_rows, TILE),
        in_specs=[SMEM, SMEM, VMEM, VMEM, VMEM],
        out_specs=VMEM,
        scratch_shapes=[pltpu.VMEM((cb * 192, TILE), jnp.bfloat16)],
        compiler_params=PARAMS,
        name="start",
    )(slots, count, tile_stack, start, item_scale)

    panels = [start]
    factors = []
    for half in range(1, 2 * STEPS + 1):
        users = half % 2 == 1
        last = half == 2 * STEPS
        got = sum_col(sent) if users else sum_row(sent)
        blocks, targets = (rb, cb) if users else (cb, rb)
        sent_rows = item_rows if users else user_rows
        with_old = half > 1
        operands = [] if last else [slots, count, tile_stack]
        specs = [] if last else [SMEM, SMEM, VMEM]
        operands += [got, user_scale if users else item_scale]
        specs += [VMEM, VMEM]
        if with_old:
            operands += [panels[half - 2], factors[half - 2]]
            specs += [VMEM, VMEM]
        panel, factor, sent = pl.pallas_call(
            functools.partial(
                step_kernel, forward=not users, cb=cb, blocks=blocks, targets=targets,
                with_old=with_old, last=last,
            ),
            out_shape=[
                f32(blocks * BLOCK, TILE),
                f32(BLOCK, 2 * BLOCK),
                f32(BLOCK, TILE) if last else f32(sent_rows, TILE),
            ],
            in_specs=specs,
            out_specs=[VMEM, VMEM, VMEM],
            scratch_shapes=[]
            if last
            else [pltpu.VMEM((blocks * 192, TILE), jnp.bfloat16)],
            compiler_params=PARAMS,
            name=f"half{half}",
        )(*operands)
        panels.append(panel)
        factors.append(factor)

    gram = jnp.sum(gather_whole(sent, NEAR, lax.axis_size(NEAR)), axis=0)
    gram = jnp.sum(lax.all_gather(gram, "zh", axis=0, tiled=False), axis=0)

    user_group = rb * TILE // cols
    item_group = cb * TILE // rows
    left = jnp.transpose(panels[-2].reshape(rb, BLOCK, TILE), (1, 0, 2))
    left = lax.dynamic_slice_in_dim(
        left.reshape(BLOCK, rb * TILE), lax.axis_index(COL) * user_group, user_group, 1
    )
    right = jnp.transpose(panels[-1].reshape(cb, BLOCK, TILE), (1, 0, 2))
    right = lax.dynamic_slice_in_dim(
        right.reshape(BLOCK, cb * TILE), lax.axis_index(ROW) * item_group, item_group, 1
    )
    right_panel, left_panel, factor = pl.pallas_call(
        functools.partial(
            end_kernel, left_size=rb * TILE * rows, right_size=cb * TILE * cols
        ),
        out_shape=[
            f32(BLOCK, item_group),
            f32(BLOCK, user_group),
            f32(BLOCK, 2 * BLOCK),
        ],
        in_specs=[VMEM] * 4,
        out_specs=[VMEM] * 3,
        compiler_params=PARAMS,
        name="end",
    )(gram, right, left, factors[-1])
    factors.append(factor)
    lower = [jnp.tril(jnp.transpose(f[:, :BLOCK])) for f in factors]
    return (
        left_panel,
        right_panel,
        jnp.stack(lower[1::2]),
        jnp.stack(lower[2::2]),
    )


def solution(mesh):
    split = Mesh(mesh.devices.reshape(4, 4, 4, 4, 2), ROW + COL)
    in_specs = (
        P(ROW, COL, None, None, None),
        P(ROW, COL, None),
        P(ROW, COL),
        P(ROW),
        P(COL),
        P(None, COL + ROW),
    )
    out_specs = (P(None, ROW + COL), P(None, COL + ROW), P(), P())
    return jax.shard_map(
        per_device, mesh=split, in_specs=in_specs, out_specs=out_specs, check_vma=False
    )
```

time: 1740 us -> 379 us (0.22)
  blocking collectives: 1030 us -> 240 us
  waiting for transfers between devices: 546 us -> 39.5 us
  other arithmetic: 87.5 us -> 0.34 us
  Pallas kernels: 0 us -> 57.9 us
  starting transfers between devices: 0.25 us -> 28.7 us
  matrix products: 25.6 us -> 0 us
    psum x7 -> x0, blocking collectives: 756 us -> none  [the longest x3 339 us: per_device(): lax.psum(gram_of(backward), ('row', 'col'))]
    unnamed x12 -> x0, waiting for transfers between devices: 546 us -> none
    all_gather x6 -> x4, blocking collectives: 277 us -> 68.9 us  [the longest x3 53.9 us: sum_col(): own = jnp.sum(lax.all_gather(own, 'zh', axis=0, tiled=False), axis=0)]
    all_to_all x0 -> x10, blocking collectives: none -> 171 us  [the longest x4 70.3 us: gather_whole(): return lax.all_to_all(copies, axes, 0, 0, tiled=True)]
    another operation x37 -> x8, other arithmetic: 85.8 us -> 0.07 us  [the longest x4 0.03 us: per_device(): jnp.stack(lower[1::2])]
    pallas_call x0 -> x8, Pallas kernels: none -> 57.9 us  [the longest x6 49.7 us: per_device(): pl.pallas_call(functools.partial(step_kernel, forward=not users, cb=cb, b...]
    all_to_all x0 -> x4, waiting for transfers between devices: none -> 39.5 us  [gather_whole(): return lax.all_to_all(copies, axes, 0, 0, tiled=True)]
    all_to_all x0 -> x4, starting transfers between devices: none -> 28.7 us  [gather_whole(): return lax.all_to_all(copies, axes, 0, 0, tiled=True)]
  transfers between devices with their start and end apart: 6 -> 4, of which waited for: 6 -> 4; matrix products, arithmetic and copies ran while one was open for 0% -> 0% of each run, Pallas kernels for 0% -> 0%
where the time goes in v1:
time: 379 us; the launch traced here: 376 us
  blocking collectives  240 us (63%)
  Pallas kernels  57.9 us (15%)
  waiting for transfers between devices  39.5 us (10%)
  starting transfers between devices  28.7 us (8%)
  local copies, waits for them, and re-layouts  8.09 us (2%)
    all_to_all x4, blocking collectives, gather_whole(): return lax.all_to_all(copies, axes, 0, 0, tiled=True)  70.3 us
    all_gather x3, blocking collectives, sum_col(): own = jnp.sum(lax.all_gather(own, 'zh', axis=0, tiled=False), axis=0)  53.9 us
    all_to_all x3, blocking collectives, sum_row(): lax.all_to_all(sent.reshape(count, rows, TILE), ROW, 0, 0, tiled=True)  51.2 us
    all_to_all x3, blocking collectives, sum_col(): lax.all_to_all(sent.reshape(near, rows, TILE), NEAR, 0, 0, tiled=True)  49.7 us
    pallas_call x6, Pallas kernels, per_device(): pl.pallas_call(functools.partial(step_kernel, forward=not users, cb=cb, b...  49.7 us
    all_to_all x4, waiting for transfers between devices, gather_whole(): return lax.all_to_all(copies, axes, 0, 0, tiled=True)  39.5 us
    all_to_all x4, starting transfers between devices, gather_whole(): return lax.all_to_all(copies, axes, 0, 0, tiled=True)  28.7 us
    all_gather x1, blocking collectives, per_device(): gram = jnp.sum(lax.all_gather(gram, 'zh', axis=0, tiled=False), axis=0)  14.9 us
  transfers between devices with their start and end apart: 4, of which 4 were waited for; matrix products, arithmetic and copies ran while one was open for 0% of the time, Pallas kernels for 0%

profile of v1, /device:TPU:1, one launch (start us, length us, event | category | flops | bytes accessed | tf_op | source)
XLA Modules:
  0.0 376.2 jit_solution(17599052859757913481)
XLA Ops:
  0.6 1.6 broadcast_in_dim.24
  2.2 9.3 %all-to-all-start = ((f32[16,64,96]{2,1,0:T(8,128)}), f32[16,64,96]{2,1,0:T(8,128)S(1)}, u32[]{:S(2)}, u32[]{:S(2)}) async-start(f32[16,64,96]{2,1,0:T(8,128)} %broadcast_in_dim.24), calls=%async_computation | async-start | bytes 1048576 | tf_op jit(solution)/shard_map/all_to_all | solution.py:183
  12.2 13.0 %all-to-all-done = f32[16,64,96]{2,1,0:T(8,128)S(1)} async-done(((f32[16,64,96]{2,1,0:T(8,128)}), f32[16,64,96]{2,1,0:T(8,128)S(1)}, u32[]{:S(2)}, u32[]{:S(2)}) %all-to-all-start) | async-done | bytes 393248 | tf_op jit(solution)/shard_map/all_to_all | solution.py:183
  25.2 0.3 copy.25
  25.5 0.0 copy-start
  25.5 0.2 reshape.76
  25.7 0.1 copy.26
  25.8 0.0 copy-start.1
  25.8 0.9 copy-done
  26.7 2.0 start.1
  28.7 17.3 %all_to_all.70 = f32[8,136,128]{2,1,0:T(8,128)S(1)} all-to-all(f32[8,136,128]{2,1,0:T(8,128)S(1)} %bitcast.91), channel_id=1, replica_groups=mesh['zl'=4,'y'=4,'x'=4,'zh'=4,'core'=2] {'x','core'}, dimensions={0} | all-to-all | bytes 1114112 | tf_op jit(solution)/shard_map/all_to_all | solution.py:190
  46.1 21.7 %all-gather = f32[544,128]{1,0:T(8,128)S(1)} all-gather(f32[136,128]{1,0:T(8,128)S(1)} %reduce_sum.99), channel_id=2, replica_groups=mesh['zl'=4,'y'=4,'x'=4,'zh'=4,'core'=2] {'zh'}, dimensions={0}, use_global_device_ids=true | all-gather | bytes 348160 | tf_op jit(solution)/shard_map/all_gather | solution.py:192
  67.8 0.8 broadcast_in_dim.25
  68.7 7.7 %all-to-all-start.2 = ((f32[8,136,128]{2,1,0:T(8,128)}), f32[8,136,128]{2,1,0:T(8,128)S(1)}, u32[]{:S(2)}, u32[]{:S(2)}) async-start(f32[8,136,128]{2,1,0:T(8,128)} %broadcast_in_dim.25), calls=%async_computation.2 | async-start | bytes 1114112 | tf_op jit(solution)/shard_map/all_to_all | solution.py:183
  76.4 9.8 %all-to-all-done.2 = f32[8,136,128]{2,1,0:T(8,128)S(1)} async-done(((f32[8,136,128]{2,1,0:T(8,128)}), f32[8,136,128]{2,1,0:T(8,128)S(1)}, u32[]{:S(2)}, u32[]{:S(2)}) %all-to-all-start.2) | async-done | bytes 557088 | tf_op jit(solution)/shard_map/all_to_all | solution.py:183
  86.2 8.0 %half1.1 = (f32[1024,128]{1,0:T(8,128)S(1)}, f32[64,128]{1,0:T(8,128)S(1)}, f32[896,128]{1,0:T(8,128)S(1)}) custom-call(s32[32]{0:T(128)S(1)} %bitcast.103, s32[1]{0:T(128)} %bitcast.75.refs_1_, bf16[32,128,128]{2,1,0:T(8,128)(2,1)S(1)} %bitcast.81, f32[1088,128]{1,0:T(8,128)S(1)} %bitcast.88, f32[16,128]{1,0:T(8,128)S(1)} %rsqrt_bitcast_fusion.refs_4_), custom_call_target="tpu_custom_call" | custom-call | tf_op jit(solution)/shard_map/half1/pallas_call | solution.py:248
  94.2 16.9 %all_to_all.71 = f32[16,56,128]{2,1,0:T(8,128)S(1)} all-to-all(f32[16,56,128]{2,1,0:T(8,128)S(1)} %bitcast.100), channel_id=1, replica_groups=mesh['zl'=4,'y'=4,'x'=4,'zh'=4,'core'=2] {'zl','y'}, dimensions={0} | all-to-all | bytes 917504 | tf_op jit(solution)/shard_map/all_to_all | solution.py:200
  111.2 16.6 %all_to_all.72 = f32[16,56,128]{2,1,0:T(8,128)S(1)} all-to-all(f32[16,56,128]{2,1,0:T(8,128)S(1)} %broadcast_in_dim.26), channel_id=1, replica_groups=mesh['zl'=4,'y'=4,'x'=4,'zh'=4,'core'=2] {'zl','y'}, dimensions={0} | all-to-all | bytes 917504 | tf_op jit(solution)/shard_map/all_to_all | solution.py:183
  127.9 8.5 %half2.1 = (f32[768,128]{1,0:T(8,128)S(1)}, f32[64,128]{1,0:T(8,128)S(1)}, f32[1088,128]{1,0:T(8,128)S(1)}) custom-call(s32[32]{0:T(128)S(1)} %bitcast.104, s32[1]{0:T(128)} %bitcast.76.refs_1_, bf16[32,128,128]{2,1,0:T(8,128)(2,1)S(1)} %bitcast.82, f32[896,128]{1,0:T(8,128)S(1)} %bitcast.93, f32[12,128]{1,0:T(8,128)S(1)} %rsqrt_bitcast_fusion.1.scale_ref.refs_4_.refs_1_, ...), custom_call_target="tpu_custom_call" | custom-call | tf_op jit(solution)/shard_map/half2/pallas_call | solution.py:248
  136.3 16.4 %all_to_all.73 = f32[8,136,128]{2,1,0:T(8,128)S(1)} all-to-all(f32[8,136,128]{2,1,0:T(8,128)S(1)} %bitcast.95), channel_id=1, replica_groups=mesh['zl'=4,'y'=4,'x'=4,'zh'=4,'core'=2] {'x','core'}, dimensions={0} | all-to-all | bytes 1114112 | tf_op jit(solution)/shard_map/all_to_all | solution.py:190
  152.8 16.6 %all-gather.1 = f32[544,128]{1,0:T(8,128)S(1)} all-gather(f32[136,128]{1,0:T(8,128)S(1)} %reduce_sum.102), channel_id=3, replica_groups=mesh['zl'=4,'y'=4,'x'=4,'zh'=4,'core'=2] {'zh'}, dimensions={0}, use_global_device_ids=true | all-gather | bytes 348160 | tf_op jit(solution)/shard_map/all_gather | solution.py:192
  169.5 16.5 %all_to_all.74 = f32[8,136,128]{2,1,0:T(8,128)S(1)} all-to-all(f32[8,136,128]{2,1,0:T(8,128)S(1)} %broadcast_in_dim.27), channel_id=1, replica_groups=mesh['zl'=4,'y'=4,'x'=4,'zh'=4,'core'=2] {'x','core'}, dimensions={0} | all-to-all | bytes 1114112 | tf_op jit(solution)/shard_map/all_to_all | solution.py:183
  186.0 8.8 %half3.1 = (f32[1024,128]{1,0:T(8,128)S(1)}, f32[64,128]{1,0:T(8,128)S(1)}, f32[896,128]{1,0:T(8,128)S(1)}) custom-call(s32[32]{0:T(128)S(1)} %bitcast.105, s32[1]{0:T(128)} %bitcast.77.refs_1_, bf16[32,128,128]{2,1,0:T(8,128)(2,1)S(1)} %bitcast.83, f32[1088,128]{1,0:T(8,128)S(1)} %bitcast.90, f32[16,128]{1,0:T(8,128)S(1)} %rsqrt_bitcast_fusion.refs_4_, ...), custom_call_target="tpu_custom_call" | custom-call | tf_op jit(solution)/shard_map/half3/pallas_call | solution.py:248
  194.8 18.4 %all_to_all.75 = f32[16,56,128]{2,1,0:T(8,128)S(1)} all-to-all(f32[16,56,128]{2,1,0:T(8,128)S(1)} %bitcast.99), channel_id=1, replica_groups=mesh['zl'=4,'y'=4,'x'=4,'zh'=4,'core'=2] {'zl','y'}, dimensions={0} | all-to-all | bytes 917504 | tf_op jit(solution)/shard_map/all_to_all | solution.py:200
  213.3 16.7 %all_to_all.76 = f32[16,56,128]{2,1,0:T(8,128)S(1)} all-to-all(f32[16,56,128]{2,1,0:T(8,128)S(1)} %broadcast_in_dim.28), channel_id=1, replica_groups=mesh['zl'=4,'y'=4,'x'=4,'zh'=4,'core'=2] {'zl','y'}, dimensions={0} | all-to-all | bytes 917504 | tf_op jit(solution)/shard_map/all_to_all | solution.py:183
  229.9 8.5 %half4.1 = (f32[768,128]{1,0:T(8,128)S(1)}, f32[64,128]{1,0:T(8,128)S(1)}, f32[1088,128]{1,0:T(8,128)S(1)}) custom-call(s32[32]{0:T(128)S(1)} %bitcast.106, s32[1]{0:T(128)} %bitcast.78.refs_1_, bf16[32,128,128]{2,1,0:T(8,128)(2,1)S(1)} %bitcast.84, f32[896,128]{1,0:T(8,128)S(1)} %bitcast.94, f32[12,128]{1,0:T(8,128)S(1)} %rsqrt_bitcast_fusion.1.scale_ref.refs_4_.refs_1_, ...), custom_call_target="tpu_custom_call" | custom-call | tf_op jit(solution)/shard_map/half4/pallas_call | solution.py:248
  238.4 16.0 %all_to_all.77 = f32[8,136,128]{2,1,0:T(8,128)S(1)} all-to-all(f32[8,136,128]{2,1,0:T(8,128)S(1)} %bitcast.96), channel_id=1, replica_groups=mesh['zl'=4,'y'=4,'x'=4,'zh'=4,'core'=2] {'x','core'}, dimensions={0} | all-to-all | bytes 1114112 | tf_op jit(solution)/shard_map/all_to_all | solution.py:190
  254.5 15.6 %all-gather.2 = f32[544,128]{1,0:T(8,128)S(1)} all-gather(f32[136,128]{1,0:T(8,128)S(1)} %reduce_sum.105), channel_id=4, replica_groups=mesh['zl'=4,'y'=4,'x'=4,'zh'=4,'core'=2] {'zh'}, dimensions={0}, use_global_device_ids=true | all-gather | bytes 348160 | tf_op jit(solution)/shard_map/all_gather | solution.py:192
  270.1 20.5 %all_to_all.78 = f32[8,136,128]{2,1,0:T(8,128)S(1)} all-to-all(f32[8,136,128]{2,1,0:T(8,128)S(1)} %broadcast_in_dim.29), channel_id=1, replica_groups=mesh['zl'=4,'y'=4,'x'=4,'zh'=4,'core'=2] {'x','core'}, dimensions={0} | all-to-all | bytes 1114112 | tf_op jit(solution)/shard_map/all_to_all | solution.py:183
  290.6 8.8 %half5.1 = (f32[1024,128]{1,0:T(8,128)S(1)}, f32[64,128]{1,0:T(8,128)S(1)}, f32[896,128]{1,0:T(8,128)S(1)}) custom-call(s32[32]{0:T(128)S(1)} %bitcast.107, s32[1]{0:T(128)} %bitcast.79.refs_1_, bf16[32,128,128]{2,1,0:T(8,128)(2,1)S(1)} %bitcast.85, f32[1088,128]{1,0:T(8,128)S(1)} %bitcast.89, f32[16,128]{1,0:T(8,128)S(1)} %rsqrt_bitcast_fusion.refs_4_, ...), custom_call_target="tpu_custom_call" | custom-call | tf_op jit(solution)/shard_map/half5/pallas_call | solution.py:248
  299.4 15.9 %all_to_all.79 = f32[16,56,128]{2,1,0:T(8,128)S(1)} all-to-all(f32[16,56,128]{2,1,0:T(8,128)S(1)} %bitcast.98), channel_id=1, replica_groups=mesh['zl'=4,'y'=4,'x'=4,'zh'=4,'core'=2] {'zl','y'}, dimensions={0} | all-to-all | bytes 917504 | tf_op jit(solution)/shard_map/all_to_all | solution.py:200
  315.4 0.8 broadcast_in_dim.30
  316.2 5.1 %all-to-all-start.12 = ((f32[16,56,128]{2,1,0:T(8,128)}), f32[16,56,128]{2,1,0:T(8,128)S(1)}, u32[]{:S(2)}, u32[]{:S(2)}) async-start(f32[16,56,128]{2,1,0:T(8,128)} %broadcast_in_dim.30), calls=%async_computation.12 | async-start | bytes 917504 | tf_op jit(solution)/shard_map/all_to_all | solution.py:183
  321.3 0.3 copy.28
  321.6 0.2 copy.35
  321.8 0.1 constant_dynamic-slice_fusion.left_ref
  321.9 11.4 %all-to-all-done.12 = f32[16,56,128]{2,1,0:T(8,128)S(1)} async-done(((f32[16,56,128]{2,1,0:T(8,128)}), f32[16,56,128]{2,1,0:T(8,128)S(1)}, u32[]{:S(2)}, u32[]{:S(2)}) %all-to-all-start.12) | async-done | bytes 458784 | tf_op jit(solution)/shard_map/all_to_all | solution.py:183
  333.3 7.2 %half6.1 = (f32[768,128]{1,0:T(8,128)S(1)}, f32[64,128]{1,0:T(8,128)S(1)}, f32[64,128]{1,0:T(8,128)S(1)}) custom-call(f32[896,128]{1,0:T(8,128)S(1)} %bitcast.92, f32[12,128]{1,0:T(8,128)S(1)} %rsqrt_bitcast_fusion.1.scale_ref.refs_4_.refs_1_, f32[768,128]{1,0:T(8,128)S(1)} %get-tuple-element.37.refs_2_, f32[64,128]{1,0:T(8,128)S(1)} %get-tuple-element.38.refs_3_), custom_call_target="tpu_custom_call" | custom-call | tf_op jit(solution)/shard_map/half6/pallas_call | solution.py:248
  340.5 0.7 broadcast_in_dim.31
  341.2 6.6 %all-to-all-start.13 = ((f32[8,64,128]{2,1,0:T(8,128)}), f32[8,64,128]{2,1,0:T(8,128)S(1)}, u32[]{:S(2)}, u32[]{:S(2)}) async-start(f32[8,64,128]{2,1,0:T(8,128)} %broadcast_in_dim.31), calls=%async_computation.13 | async-start | bytes 524288 | tf_op jit(solution)/shard_map/all_to_all | solution.py:183
  347.8 0.2 copy.27
  348.0 0.1 copy.36
  348.2 0.7 copy.29
  348.9 0.1 constant_dynamic-slice_fusion.1.right_ref
  349.0 5.3 %all-to-all-done.13 = f32[8,64,128]{2,1,0:T(8,128)S(1)} async-done(((f32[8,64,128]{2,1,0:T(8,128)}), f32[8,64,128]{2,1,0:T(8,128)S(1)}, u32[]{:S(2)}, u32[]{:S(2)}) %all-to-all-start.13) | async-done | bytes 262176 | tf_op jit(solution)/shard_map/all_to_all | solution.py:183
  354.3 14.9 %all-gather.3 = f32[256,128]{1,0:T(8,128)S(1)} all-gather(f32[64,128]{1,0:T(8,128)S(1)} %reduce_sum.108), channel_id=5, replica_groups=mesh['zl'=4,'y'=4,'x'=4,'zh'=4,'core'=2] {'zh'}, dimensions={0}, use_global_device_ids=true | all-gather | bytes 163840 | tf_op jit(solution)/shard_map/all_gather | solution.py:270
  369.3 6.2 %end.1 = (f32[64,96]{1,0:T(8,128)}, f32[64,64]{1,0:T(8,128)}, f32[64,128]{1,0:T(8,128)S(1)}) custom-call(f32[64,128]{1,0:T(8,128)S(1)} %reduce_sum.109.gram_ref, f32[64,96]{1,0:T(8,128)S(1)} %constant_dynamic-slice_fusion.1.right_ref, f32[64,64]{1,0:T(8,128)S(1)} %constant_dynamic-slice_fusion.left_ref, f32[64,128]{1,0:T(8,128)S(1)} %get-tuple-element.42.left_factor_ref), custom_call_target="tpu_custom_call" | custom-call | tf_op jit(solution)/shard_map/end/pallas_call | solution.py:282
  375.5 0.7 copy.30
  (30 shorter events, 0.5 us)
Async XLA Ops:
  2.2 10.0 %copy-start.2 = (s32[1536]{0:T(1024)S(1)}, s32[1536]{0:T(1024)}, u32[]{:S(2)}) copy-start(s32[1536]{0:T(1024)} %param.10) | copy-start | bytes 18436
  2.2 23.0 %all-to-all-start = ((f32[16,64,96]{2,1,0:T(8,128)}), f32[16,64,96]{2,1,0:T(8,128)S(1)}, u32[]{:S(2)}, u32[]{:S(2)}) async-start(f32[16,64,96]{2,1,0:T(8,128)} %broadcast_in_dim.24), calls=%async_computation | async-start | bytes 1048576 | tf_op jit(solution)/shard_map/all_to_all | solution.py:183
  25.5 1.2 copy-start
  25.8 0.9 copy-start.1
  68.6 7.7 %copy-start.3 = (s32[2048]{0:T(1024)S(1)}, s32[2048]{0:T(1024)}, u32[]{:S(2)}) copy-start(s32[2048]{0:T(1024)} %param.9) | copy-start | bytes 24580
  68.7 17.6 %all-to-all-start.2 = ((f32[8,136,128]{2,1,0:T(8,128)}), f32[8,136,128]{2,1,0:T(8,128)S(1)}, u32[]{:S(2)}, u32[]{:S(2)}) async-start(f32[8,136,128]{2,1,0:T(8,128)} %broadcast_in_dim.25), calls=%async_computation.2 | async-start | bytes 1114112 | tf_op jit(solution)/shard_map/all_to_all | solution.py:183
  316.2 17.1 %all-to-all-start.12 = ((f32[16,56,128]{2,1,0:T(8,128)}), f32[16,56,128]{2,1,0:T(8,128)S(1)}, u32[]{:S(2)}, u32[]{:S(2)}) async-start(f32[16,56,128]{2,1,0:T(8,128)} %broadcast_in_dim.30), calls=%async_computation.12 | async-start | bytes 917504 | tf_op jit(solution)/shard_map/all_to_all | solution.py:183
  341.2 13.1 %all-to-all-start.13 = ((f32[8,64,128]{2,1,0:T(8,128)}), f32[8,64,128]{2,1,0:T(8,128)S(1)}, u32[]{:S(2)}, u32[]{:S(2)}) async-start(f32[8,64,128]{2,1,0:T(8,128)} %broadcast_in_dim.31), calls=%async_computation.13 | async-start | bytes 524288 | tf_op jit(solution)/shard_map/all_to_all | solution.py:183

commit v2 on v1

v2 whole, which is shorter than its diff:
```python
import functools
import math

import jax
import jax.numpy as jnp
from jax import lax
from jax.experimental import pallas as pl
from jax.experimental.pallas import tpu as pltpu
from jax.sharding import Mesh
from jax.sharding import PartitionSpec as P

STEPS = 3
TILE = 128
BLOCK = 64
GRAM_ROWS = 24
HIGH = lax.Precision.HIGHEST

ROW = ("zl", "y")
COL = ("x", "zh", "core")
NEAR = ("x", "core")


def pack_gram(gram):
    half = BLOCK // 2

    def rows(block):
        return jnp.concatenate([block[8 * i : 8 * i + 8] for i in range(4)], axis=1)

    return jnp.concatenate(
        [
            rows(gram[:half, :half]),
            rows(gram[half:, half:]),
            rows(gram[half:, :half]),
        ],
        axis=0,
    )


def unpack_gram(packed):
    half = BLOCK // 2

    def block(rows):
        return jnp.concatenate(
            [rows[:, half * i : half * i + half] for i in range(4)], axis=0
        )

    upper, lower, cross = (block(packed[8 * i : 8 * i + 8]) for i in range(3))
    return jnp.concatenate(
        [
            jnp.concatenate([upper, jnp.transpose(cross)], axis=1),
            jnp.concatenate([cross, lower], axis=1),
        ],
        axis=0,
    )


def factor_rows(gram, out_ref):
    eye = (
        lax.broadcasted_iota(jnp.int32, (BLOCK, BLOCK), 0)
        == lax.broadcasted_iota(jnp.int32, (BLOCK, BLOCK), 1)
    ).astype(jnp.float32)
    whole = jnp.concatenate([gram, eye], axis=1)
    groups = [whole[8 * i : 8 * i + 8] for i in range(BLOCK // 8)]
    for j in range(BLOCK):
        first = j // 8
        k = j % 8
        row = groups[first][k : k + 1]
        root = lax.rsqrt(row[:, j : j + 1])
        scaled = row * root
        out_ref[j : j + 1, :] = scaled
        for i in range(first, BLOCK // 8):
            groups[i] = groups[i] - (groups[i][:, j : j + 1] * root) * scaled


def split_three(value):
    high = value.astype(jnp.bfloat16)
    rest = value - high.astype(jnp.float32)
    middle = rest.astype(jnp.bfloat16)
    low = (rest - middle.astype(jnp.float32)).astype(jnp.bfloat16)
    return jnp.concatenate([high, middle, low], axis=0)


def product(slots_ref, count_ref, tiles_ref, parts_ref, sums_ref, forward, cb):
    count = count_ref[0]
    group = 4

    def visit(step, carry):
        added = []
        for g in range(group):
            t = step * group + g
            slot = slots_ref[t]
            local_row = slot // cb
            local_col = slot - local_row * cb
            source, target = (
                (local_col, local_row) if forward else (local_row, local_col)
            )
            tile = tiles_ref[t]
            tile = jnp.where(t < count, tile, jnp.zeros_like(tile))
            parts = parts_ref[pl.ds(pl.multiple_of(source * 192, 64), 192), :]
            dims = (((1,), (1 if forward else 0,)), ((), ()))
            value = lax.dot_general(
                parts, tile, dims, preferred_element_type=jnp.float32
            )
            added.append((target, value[:64] + value[64:128] + value[128:]))
        for target, value in added:
            where = pl.ds(pl.multiple_of(target * 64, 64), 64)
            sums_ref[where, :] += value
        return carry

    lax.fori_loop(0, (count + group - 1) // group, visit, 0)


def add_gram(gram, value):
    return gram + lax.dot_general(
        value, value, (((1,), (1,)), ((), ())), precision=HIGH,
        preferred_element_type=jnp.float32,
    )


def send_panel(
    slots_ref, count_ref, tiles_ref, panel_ref, scale_ref, sent_ref, parts_ref, sums_ref, *, forward, cb
):
    sums_ref[...] = jnp.zeros_like(sums_ref)
    gram = jnp.zeros((BLOCK, BLOCK), jnp.float32)
    for b in range(panel_ref.shape[0] // BLOCK):
        value = panel_ref[64 * b : 64 * b + 64, :]
        gram = add_gram(gram, value)
        parts_ref[192 * b : 192 * b + 192, :] = split_three(
            value * scale_ref[b : b + 1, :]
        )
    product(slots_ref, count_ref, tiles_ref, parts_ref, sums_ref, forward, cb)
    packed = pack_gram(gram)
    count = sent_ref.shape[0]
    rows = sums_ref.shape[0] // count
    for k in range(count):
        sent_ref[k, :rows, :] = sums_ref[rows * k : rows * k + rows, :]
        sent_ref[k, rows:, :] = packed


def start_kernel(slots_ref, count_ref, tiles_ref, panel_ref, scale_ref, sent_ref, parts_ref, sums_ref, *, cb):
    send_panel(
        slots_ref, count_ref, tiles_ref, panel_ref, scale_ref, sent_ref, parts_ref, sums_ref,
        forward=True, cb=cb,
    )


def fold_kernel(got_ref, out_ref):
    rows = out_ref.shape[-2]
    total = got_ref[0, :rows, :]
    for k in range(1, got_ref.shape[0]):
        total += got_ref[k, :rows, :]
    for k in range(out_ref.shape[0]):
        out_ref[k] = total


def sum_gram(got_ref):
    packed = got_ref[0, -GRAM_ROWS:, :]
    for k in range(1, got_ref.shape[0]):
        packed += got_ref[k, -GRAM_ROWS:, :]
    return unpack_gram(packed)


def factor_kernel(*refs, with_old):
    if not with_old:
        got_ref, factor_ref = refs
        factor_rows(sum_gram(got_ref), factor_ref)
        return
    got_ref, old_ref, old_factor_ref, factor_ref, part_ref = refs
    factor_rows(sum_gram(got_ref), factor_ref)
    upper_mask = lax.broadcasted_iota(
        jnp.int32, (BLOCK, BLOCK), 0
    ) <= lax.broadcasted_iota(jnp.int32, (BLOCK, BLOCK), 1)
    upper = jnp.where(upper_mask, factor_ref[:, :BLOCK], 0.0)
    back = jnp.dot(
        upper, -old_factor_ref[:, BLOCK:], precision=HIGH,
        preferred_element_type=jnp.float32,
    )
    for b in range(old_ref.shape[0] // BLOCK):
        part_ref[64 * b : 64 * b + 64, :] = jnp.dot(
            back, old_ref[64 * b : 64 * b + 64, :], precision=HIGH,
            preferred_element_type=jnp.float32,
        )


def step_kernel(*refs, forward, cb, with_old, last):
    refs = list(refs)
    tables = []
    if not last:
        tables, refs = refs[:3], refs[3:]
    got_ref, scale_ref, factor_ref = refs[:3]
    refs = refs[3:]
    if with_old:
        part_ref, refs = refs[0], refs[1:]
    panel_ref, sent_ref = refs[:2]
    inverse = factor_ref[:, BLOCK:]
    gram = jnp.zeros((BLOCK, BLOCK), jnp.float32)
    for b in range(panel_ref.shape[0] // BLOCK):
        where = slice(64 * b, 64 * b + 64)
        value = jnp.dot(
            inverse, got_ref[where, :] * scale_ref[b : b + 1, :], precision=HIGH,
            preferred_element_type=jnp.float32,
        )
        if with_old:
            value += part_ref[where, :]
        panel_ref[where, :] = value
        if last:
            gram = add_gram(gram, value)
    if last:
        sent_ref[...] = pack_gram(gram)
    else:
        send_panel(
            *tables, panel_ref, scale_ref, sent_ref, refs[2], refs[3],
            forward=forward, cb=cb,
        )


def end_kernel(
    got_ref, right_ref, left_ref, left_factor_ref, out_right_ref, out_left_ref, factor_ref, *,
    left_size, right_size,
):
    factor_rows(sum_gram(got_ref), factor_ref)
    out_right_ref[...] = math.sqrt(right_size) * jnp.dot(
        factor_ref[:, BLOCK:], right_ref[...], precision=HIGH,
        preferred_element_type=jnp.float32,
    )
    out_left_ref[...] = math.sqrt(left_size) * jnp.dot(
        left_factor_ref[:, BLOCK:], left_ref[...], precision=HIGH,
        preferred_element_type=jnp.float32,
    )


SMEM = pl.BlockSpec(memory_space=pltpu.SMEM)
VMEM = pl.BlockSpec(memory_space=pltpu.VMEM)
PARAMS = pltpu.CompilerParams(vmem_limit_bytes=8 * 1024 * 1024)


def f32(*shape):
    return jax.ShapeDtypeStruct(shape, jnp.float32)


def gather_whole(value, axes, count):
    copies = jnp.broadcast_to(value[None], (count,) + value.shape)
    return lax.all_to_all(copies, axes, 0, 0, tiled=True)


def fold(got, copies, rows):
    return pl.pallas_call(
        fold_kernel,
        out_shape=f32(copies, rows, TILE),
        in_specs=[VMEM],
        out_specs=VMEM,
        compiler_params=PARAMS,
        name="fold",
    )(got)


def exchange(messages, axes):
    return lax.all_to_all(messages, axes, 0, 0, tiled=True)


def sum_col(sent):
    near = lax.axis_size(NEAR)
    own = fold(exchange(sent, NEAR), 1, sent.shape[1])[0]
    got = lax.all_gather(own, "zh", axis=0, tiled=False)
    rows = sent.shape[1] - GRAM_ROWS
    return got, exchange(fold(got, near, rows), NEAR).reshape(near * rows, TILE)


def sum_row(sent):
    count = lax.axis_size(ROW)
    got = exchange(sent, ROW)
    rows = sent.shape[1] - GRAM_ROWS
    return got, exchange(fold(got, count, rows), ROW).reshape(count * rows, TILE)


def per_device(tiles, tile_slots, tile_counts, user_degree, item_degree, start_panel):
    tile_stack = tiles[0, 0]
    slots = tile_slots[0, 0]
    count = tile_counts[0]
    rb = user_degree.shape[0] // TILE
    cb = item_degree.shape[0] // TILE
    rows = lax.axis_size(ROW)
    cols = lax.axis_size(COL)
    near = lax.axis_size(NEAR)
    user_scale = lax.rsqrt(user_degree.astype(jnp.float32)).reshape(rb, TILE)
    item_scale = lax.rsqrt(item_degree.astype(jnp.float32)).reshape(cb, TILE)

    start = gather_whole(start_panel, ROW, rows)
    start = jnp.transpose(start, (1, 0, 2)).reshape(BLOCK, cb, TILE)
    start = jnp.transpose(start, (1, 0, 2)).reshape(cb * BLOCK, TILE)

    user_messages = f32(near, rb * BLOCK // near + GRAM_ROWS, TILE)
    item_messages = f32(rows, cb * BLOCK // rows + GRAM_ROWS, TILE)
    user_sums = pltpu.VMEM((rb * BLOCK, TILE), jnp.float32)
    item_sums = pltpu.VMEM((cb * BLOCK, TILE), jnp.float32)
    user_parts = pltpu.VMEM((rb * 192, TILE), jnp.bfloat16)
    item_parts = pltpu.VMEM((cb * 192, TILE), jnp.bfloat16)
    sent = pl.pallas_call(
        functools.partial(start_kernel, cb=cb),
        out_shape=user_messages,
        in_specs=[SMEM, SMEM, VMEM, VMEM, VMEM],
        out_specs=VMEM,
        scratch_shapes=[item_parts, user_sums],
        compiler_params=PARAMS,
        name="start",
    )(slots, count, tile_stack, start, item_scale)

    panels = [start]
    factors = []
    for half in range(1, 2 * STEPS + 1):
        users = half % 2 == 1
        last = half == 2 * STEPS
        with_old = half > 1
        got, whole = sum_col(sent) if users else sum_row(sent)
        panel_shape = f32((rb if users else cb) * BLOCK, TILE)
        old = [panels[half - 2], factors[half - 2]] if with_old else []
        factored = pl.pallas_call(
            functools.partial(factor_kernel, with_old=with_old),
            out_shape=[f32(BLOCK, 2 * BLOCK)] + ([panel_shape] if with_old else []),
            in_specs=[VMEM] * (1 + len(old)),
            out_specs=[VMEM] * (2 if with_old else 1),
            compiler_params=PARAMS,
            name=f"factor{half}",
        )(got, *old)
        factors.append(factored[0])
        tables = [] if last else [slots, count, tile_stack]
        operands = [whole, user_scale if users else item_scale, *factored]
        panel, sent = pl.pallas_call(
            functools.partial(
                step_kernel, forward=not users, cb=cb, with_old=with_old, last=last
            ),
            out_shape=[
                panel_shape,
                f32(GRAM_ROWS, TILE)
                if last
                else (item_messages if users else user_messages),
            ],
            in_specs=([] if last else [SMEM, SMEM, VMEM]) + [VMEM] * len(operands),
            out_specs=[VMEM, VMEM],
            scratch_shapes=[]
            if last
            else ([user_parts, item_sums] if users else [item_parts, user_sums]),
            compiler_params=PARAMS,
            name=f"half{half}",
        )(*tables, *operands)
        panels.append(panel)

    gram = fold(gather_whole(sent, NEAR, near), 1, GRAM_ROWS)[0]
    gram = lax.all_gather(gram, "zh", axis=0, tiled=False)

    user_group = rb * TILE // cols
    item_group = cb * TILE // rows
    left = jnp.transpose(panels[-2].reshape(rb, BLOCK, TILE), (1, 0, 2))
    left = lax.dynamic_slice_in_dim(
        left.reshape(BLOCK, rb * TILE), lax.axis_index(COL) * user_group, user_group, 1
    )
    right = jnp.transpose(panels[-1].reshape(cb, BLOCK, TILE), (1, 0, 2))
    right = lax.dynamic_slice_in_dim(
        right.reshape(BLOCK, cb * TILE), lax.axis_index(ROW) * item_group, item_group, 1
    )
    right_panel, left_panel, factor = pl.pallas_call(
        functools.partial(
            end_kernel, left_size=rb * TILE * rows, right_size=cb * TILE * cols
        ),
        out_shape=[
            f32(BLOCK, item_group),
            f32(BLOCK, user_group),
            f32(BLOCK, 2 * BLOCK),
        ],
        in_specs=[VMEM] * 4,
        out_specs=[VMEM] * 3,
        compiler_params=PARAMS,
        name="end",
    )(gram, right, left, factors[-1])
    factors.append(factor)
    lower = [jnp.tril(jnp.transpose(f[:, :BLOCK])) for f in factors]
    return (
        left_panel,
        right_panel,
        jnp.stack(lower[1::2]),
        jnp.stack(lower[2::2]),
    )


def solution(mesh):
    split = Mesh(mesh.devices.reshape(4, 4, 4, 4, 2), ROW + COL)
    in_specs = (
        P(ROW, COL, None, None, None),
        P(ROW, COL, None),
        P(ROW, COL),
        P(ROW),
        P(COL),
        P(None, COL + ROW),
    )
    out_specs = (P(None, ROW + COL), P(None, COL + ROW), P(), P())
    return jax.shard_map(
        per_device, mesh=split, in_specs=in_specs, out_specs=out_specs, check_vma=False
    )
```

time: 379 us -> 357 us (0.942)
  blocking collectives: 240 us -> 183 us
  starting transfers between devices: 28.7 us -> 51.5 us
  Pallas kernels: 57.9 us -> 66 us
  local copies, waits for them, and re-layouts: 8.09 us -> 12 us
    all_to_all x10 -> x6, blocking collectives: 171 us -> 111 us  [exchange(): return lax.all_to_all(messages, axes, 0, 0, tiled=True)]
    all_to_all x0 -> x6, starting transfers between devices: none -> 36.1 us  [exchange(): return lax.all_to_all(messages, axes, 0, 0, tiled=True)]
    all_to_all x0 -> x6, waiting for transfers between devices: none -> 22.3 us  [exchange(): return lax.all_to_all(messages, axes, 0, 0, tiled=True)]
    all_to_all x4 -> x2, waiting for transfers between devices: 39.5 us -> 17.9 us  [gather_whole(): return lax.all_to_all(copies, axes, 0, 0, tiled=True)]
    all_to_all x4 -> x2, starting transfers between devices: 28.7 us -> 15.3 us  [gather_whole(): return lax.all_to_all(copies, axes, 0, 0, tiled=True)]
    pallas_call x7 -> x23, Pallas kernels: 51.7 us -> 59.7 us  [the longest x6 35.8 us: per_device(): pl.pallas_call(functools.partial(factor_kernel, with_old=with_old), out_s...]
    unnamed x12 -> x32, local copies, waits for them, and re-layouts: 2.68 us -> 8.46 us
  transfers between devices with their start and end apart: 4 -> 8, of which waited for: 4 -> 8; matrix products, arithmetic and copies ran while one was open for 0% -> 0% of each run, Pallas kernels for 0% -> 10%
where the time goes in v2:
time: 357 us; the launch traced here: 354 us
  blocking collectives  183 us (51%)
  Pallas kernels  66 us (18%)
  starting transfers between devices  51.5 us (14%)
  waiting for transfers between devices  40.1 us (11%)
  local copies, waits for them, and re-layouts  12 us (3%)
    all_to_all x6, blocking collectives, exchange(): return lax.all_to_all(messages, axes, 0, 0, tiled=True)  111 us
    all_gather x3, blocking collectives, sum_col(): got = lax.all_gather(own, 'zh', axis=0, tiled=False)  57.5 us
    all_to_all x6, starting transfers between devices, exchange(): return lax.all_to_all(messages, axes, 0, 0, tiled=True)  36.1 us
    pallas_call x6, Pallas kernels, per_device(): pl.pallas_call(functools.partial(factor_kernel, with_old=with_old), out_s...  35.8 us
    all_to_all x6, waiting for transfers between devices, exchange(): return lax.all_to_all(messages, axes, 0, 0, tiled=True)  22.3 us
    all_to_all x2, waiting for transfers between devices, gather_whole(): return lax.all_to_all(copies, axes, 0, 0, tiled=True)  17.9 us
    pallas_call x6, Pallas kernels, per_device(): pl.pallas_call(functools.partial(step_kernel, forward=not users, cb=cb, w...  16.6 us
    all_to_all x2, starting transfers between devices, gather_whole(): return lax.all_to_all(copies, axes, 0, 0, tiled=True)  15.3 us
  transfers between devices with their start and end apart: 8, of which 8 were waited for; matrix products, arithmetic and copies ran while one was open for 0% of the time, Pallas kernels for 10%

profile of v2, /device:TPU:1, one launch (start us, length us, event | category | flops | bytes accessed | tf_op | source)
XLA Modules:
  0.0 354.3 jit_solution(9623918797465190262)
XLA Ops:
  0.6 1.6 broadcast_in_dim.21
  2.2 9.3 %all-to-all-start = ((f32[16,64,96]{2,1,0:T(8,128)}), f32[16,64,96]{2,1,0:T(8,128)S(1)}, u32[]{:S(2)}, u32[]{:S(2)}) async-start(f32[16,64,96]{2,1,0:T(8,128)} %broadcast_in_dim.21), calls=%async_computation | async-start | bytes 1048576 | tf_op jit(solution)/shard_map/all_to_all | solution.py:243
  12.2 13.0 %all-to-all-done = f32[16,64,96]{2,1,0:T(8,128)S(1)} async-done(((f32[16,64,96]{2,1,0:T(8,128)}), f32[16,64,96]{2,1,0:T(8,128)S(1)}, u32[]{:S(2)}, u32[]{:S(2)}) %all-to-all-start) | async-done | bytes 393248 | tf_op jit(solution)/shard_map/all_to_all | solution.py:243
  25.8 0.9 copy-done
  26.7 2.3 start.1
  29.0 17.5 %all_to_all.70.got_ref = f32[8,152,128]{2,1,0:T(8,128)S(1)} all-to-all(f32[8,152,128]{2,1,0:T(8,128)S(1)} %start.1), channel_id=1, replica_groups=mesh['zl'=4,'y'=4,'x'=4,'zh'=4,'core'=2] {'x','core'}, dimensions={0} | all-to-all | bytes 1245184 | tf_op jit(solution)/shard_map/all_to_all | solution.py:258
  46.6 22.1 %all_gather.12.got_ref.refs_0_ = f32[4,152,128]{2,1,0:T(8,128)S(1)} all-gather(f32[1,152,128]{2,1,0:T(8,128)S(1)} %fold.10), channel_id=1, replica_groups=mesh['zl'=4,'y'=4,'x'=4,'zh'=4,'core'=2] {'zh'}, dimensions={0}, use_global_device_ids=true | all-gather | bytes 389120 | tf_op jit(solution)/shard_map/all_gather | solution.py:264
  68.6 0.8 fold.11
  69.5 7.9 %all-to-all-start.2 = ((f32[8,128,128]{2,1,0:T(8,128)}), f32[8,128,128]{2,1,0:T(8,128)S(1)}, u32[]{:S(2)}, u32[]{:S(2)}) async-start(f32[8,128,128]{2,1,0:T(8,128)} %fold.11), calls=%async_computation.2 | async-start | bytes 1048576 | tf_op jit(solution)/shard_map/all_to_all | solution.py:258
  77.4 5.4 %factor1.1.refs_5_.refs_2_ = f32[64,128]{1,0:T(8,128)S(1)} custom-call(f32[4,152,128]{2,1,0:T(8,128)S(1)} %all_gather.12.got_ref.refs_0_), custom_call_target="tpu_custom_call" | custom-call | tf_op jit(solution)/shard_map/factor1/pallas_call | solution.py:317
  82.7 4.1 %all-to-all-done.2 = f32[8,128,128]{2,1,0:T(8,128)S(1)} async-done(((f32[8,128,128]{2,1,0:T(8,128)}), f32[8,128,128]{2,1,0:T(8,128)S(1)}, u32[]{:S(2)}, u32[]{:S(2)}) %all-to-all-start.2) | async-done | bytes 524320 | tf_op jit(solution)/shard_map/all_to_all | solution.py:258
  86.8 3.0 half1.1
  89.8 20.9 %all_to_all.71.got_ref.refs_0_ = f32[16,72,128]{2,1,0:T(8,128)S(1)} all-to-all(f32[16,72,128]{2,1,0:T(8,128)S(1)} %get-tuple-element.29), channel_id=1, replica_groups=mesh['zl'=4,'y'=4,'x'=4,'zh'=4,'core'=2] {'zl','y'}, dimensions={0} | all-to-all | bytes 1179648 | tf_op jit(solution)/shard_map/all_to_all | solution.py:258
  111.5 4.5 %all-to-all-start.4 = ((f32[16,48,128]{2,1,0:T(8,128)}), f32[16,48,128]{2,1,0:T(8,128)S(1)}, u32[]{:S(2)}, u32[]{:S(2)}) async-start(f32[16,48,128]{2,1,0:T(8,128)} %fold.12), calls=%async_computation.4 | async-start | bytes 786432 | tf_op jit(solution)/shard_map/all_to_all | solution.py:258
  116.0 6.1 %factor2.1 = (f32[64,128]{1,0:T(8,128)S(1)}, f32[768,128]{1,0:T(8,128)S(1)}) custom-call(f32[16,72,128]{2,1,0:T(8,128)S(1)} %all_to_all.71.got_ref.refs_0_, f32[768,128]{1,0:T(8,128)S(1)} %bitcast.77, f32[64,128]{1,0:T(8,128)S(1)} %factor1.1.refs_5_.refs_2_), custom_call_target="tpu_custom_call" | custom-call | tf_op jit(solution)/shard_map/factor2/pallas_call | solution.py:317
  122.8 4.6 %all-to-all-done.4 = f32[16,48,128]{2,1,0:T(8,128)S(1)} async-done(((f32[16,48,128]{2,1,0:T(8,128)}), f32[16,48,128]{2,1,0:T(8,128)S(1)}, u32[]{:S(2)}, u32[]{:S(2)}) %all-to-all-start.4) | async-done | bytes 393248 | tf_op jit(solution)/shard_map/all_to_all | solution.py:258
  127.4 1.0 copy-done.4
  128.4 2.8 half2.1
  131.1 15.6 %all_to_all.72.got_ref = f32[8,152,128]{2,1,0:T(8,128)S(1)} all-to-all(f32[8,152,128]{2,1,0:T(8,128)S(1)} %get-tuple-element.32), channel_id=1, replica_groups=mesh['zl'=4,'y'=4,'x'=4,'zh'=4,'core'=2] {'x','core'}, dimensions={0} | all-to-all | bytes 1245184 | tf_op jit(solution)/shard_map/all_to_all | solution.py:258
  146.8 17.1 %all_gather.13.got_ref.refs_0_ = f32[4,152,128]{2,1,0:T(8,128)S(1)} all-gather(f32[1,152,128]{2,1,0:T(8,128)S(1)} %fold.13), channel_id=1, replica_groups=mesh['zl'=4,'y'=4,'x'=4,'zh'=4,'core'=2] {'zh'}, dimensions={0}, use_global_device_ids=true | all-gather | bytes 389120 | tf_op jit(solution)/shard_map/all_gather | solution.py:264
  163.9 0.8 fold.14
  164.7 8.3 %all-to-all-start.6 = ((f32[8,128,128]{2,1,0:T(8,128)}), f32[8,128,128]{2,1,0:T(8,128)S(1)}, u32[]{:S(2)}, u32[]{:S(2)}) async-start(f32[8,128,128]{2,1,0:T(8,128)} %fold.14), calls=%async_computation.6 | async-start | bytes 1048576 | tf_op jit(solution)/shard_map/all_to_all | solution.py:258
  173.0 6.1 %factor3.1 = (f32[64,128]{1,0:T(8,128)S(1)}, f32[1024,128]{1,0:T(8,128)S(1)}) custom-call(f32[4,152,128]{2,1,0:T(8,128)S(1)} %all_gather.13.got_ref.refs_0_, f32[1024,128]{1,0:T(8,128)S(1)} %get-tuple-element.33.refs_1_, f32[64,128]{1,0:T(8,128)S(1)} %get-tuple-element.30.refs_5_.refs_2_), custom_call_target="tpu_custom_call" | custom-call | tf_op jit(solution)/shard_map/factor3/pallas_call | solution.py:317
  179.2 0.8 copy-done.1
  180.0 2.5 all-to-all-done.6
  182.5 1.0 copy-done.2
  183.6 3.0 half3.1
  186.6 20.5 %all_to_all.73.got_ref.refs_0_ = f32[16,72,128]{2,1,0:T(8,128)S(1)} all-to-all(f32[16,72,128]{2,1,0:T(8,128)S(1)} %get-tuple-element.36), channel_id=1, replica_groups=mesh['zl'=4,'y'=4,'x'=4,'zh'=4,'core'=2] {'zl','y'}, dimensions={0} | all-to-all | bytes 1179648 | tf_op jit(solution)/shard_map/all_to_all | solution.py:258
  207.8 4.5 %all-to-all-start.8 = ((f32[16,48,128]{2,1,0:T(8,128)}), f32[16,48,128]{2,1,0:T(8,128)S(1)}, u32[]{:S(2)}, u32[]{:S(2)}) async-start(f32[16,48,128]{2,1,0:T(8,128)} %fold.15), calls=%async_computation.8 | async-start | bytes 786432 | tf_op jit(solution)/shard_map/all_to_all | solution.py:258
  212.3 6.1 %factor4.1 = (f32[64,128]{1,0:T(8,128)S(1)}, f32[768,128]{1,0:T(8,128)S(1)}) custom-call(f32[16,72,128]{2,1,0:T(8,128)S(1)} %all_to_all.73.got_ref.refs_0_, f32[768,128]{1,0:T(8,128)S(1)} %get-tuple-element.37.refs_1_, f32[64,128]{1,0:T(8,128)S(1)} %get-tuple-element.34.refs_5_.refs_2_), custom_call_target="tpu_custom_call" | custom-call | tf_op jit(solution)/shard_map/factor4/pallas_call | solution.py:317
  218.4 5.3 %all-to-all-done.8 = f32[16,48,128]{2,1,0:T(8,128)S(1)} async-done(((f32[16,48,128]{2,1,0:T(8,128)}), f32[16,48,128]{2,1,0:T(8,128)S(1)}, u32[]{:S(2)}, u32[]{:S(2)}) %all-to-all-start.8) | async-done | bytes 393248 | tf_op jit(solution)/shard_map/all_to_all | solution.py:258
  223.7 2.8 half4.1
  226.5 15.6 %all_to_all.74.got_ref = f32[8,152,128]{2,1,0:T(8,128)S(1)} all-to-all(f32[8,152,128]{2,1,0:T(8,128)S(1)} %get-tuple-element.40), channel_id=1, replica_groups=mesh['zl'=4,'y'=4,'x'=4,'zh'=4,'core'=2] {'x','core'}, dimensions={0} | all-to-all | bytes 1245184 | tf_op jit(solution)/shard_map/all_to_all | solution.py:258
  242.1 18.3 %all_gather.14.got_ref.refs_0_ = f32[4,152,128]{2,1,0:T(8,128)S(1)} all-gather(f32[1,152,128]{2,1,0:T(8,128)S(1)} %fold.16), channel_id=1, replica_groups=mesh['zl'=4,'y'=4,'x'=4,'zh'=4,'core'=2] {'zh'}, dimensions={0}, use_global_device_ids=true | all-gather | bytes 389120 | tf_op jit(solution)/shard_map/all_gather | solution.py:264
  260.4 0.8 fold.17
  261.2 6.5 %all-to-all-start.10 = ((f32[8,128,128]{2,1,0:T(8,128)}), f32[8,128,128]{2,1,0:T(8,128)S(1)}, u32[]{:S(2)}, u32[]{:S(2)}) async-start(f32[8,128,128]{2,1,0:T(8,128)} %fold.17), calls=%async_computation.10 | async-start | bytes 1048576 | tf_op jit(solution)/shard_map/all_to_all | solution.py:258
  267.7 6.1 %factor5.1 = (f32[64,128]{1,0:T(8,128)S(1)}, f32[1024,128]{1,0:T(8,128)S(1)}) custom-call(f32[4,152,128]{2,1,0:T(8,128)S(1)} %all_gather.14.got_ref.refs_0_, f32[1024,128]{1,0:T(8,128)S(1)} %get-tuple-element.41.refs_1_, f32[64,128]{1,0:T(8,128)S(1)} %copy-done.8), custom_call_target="tpu_custom_call" | custom-call | tf_op jit(solution)/shard_map/factor5/pallas_call | solution.py:317
  273.9 3.4 all-to-all-done.10
  277.9 3.0 half5.1
  280.9 20.9 %all_to_all.75.got_ref.refs_0_ = f32[16,72,128]{2,1,0:T(8,128)S(1)} all-to-all(f32[16,72,128]{2,1,0:T(8,128)S(1)} %get-tuple-element.44), channel_id=1, replica_groups=mesh['zl'=4,'y'=4,'x'=4,'zh'=4,'core'=2] {'zl','y'}, dimensions={0} | all-to-all | bytes 1179648 | tf_op jit(solution)/shard_map/all_to_all | solution.py:258
  302.5 4.5 %all-to-all-start.12 = ((f32[16,48,128]{2,1,0:T(8,128)}), f32[16,48,128]{2,1,0:T(8,128)S(1)}, u32[]{:S(2)}, u32[]{:S(2)}) async-start(f32[16,48,128]{2,1,0:T(8,128)} %fold.18), calls=%async_computation.12 | async-start | bytes 786432 | tf_op jit(solution)/shard_map/all_to_all | solution.py:258
  309.1 6.1 %factor6.1 = (f32[64,128]{1,0:T(8,128)S(1)}, f32[768,128]{1,0:T(8,128)S(1)}) custom-call(f32[16,72,128]{2,1,0:T(8,128)S(1)} %all_to_all.75.got_ref.refs_0_, f32[768,128]{1,0:T(8,128)S(1)} %get-tuple-element.45.refs_1_, f32[64,128]{1,0:T(8,128)S(1)} %get-tuple-element.42.refs_5_.refs_2_), custom_call_target="tpu_custom_call" | custom-call | tf_op jit(solution)/shard_map/factor6/pallas_call | solution.py:317
  315.9 2.4 all-to-all-done.12
  318.4 2.1 half6.1
  321.5 6.0 %all-to-all-start.13 = ((f32[8,24,128]{2,1,0:T(8,128)}), f32[8,24,128]{2,1,0:T(8,128)S(1)}, u32[]{:S(2)}, u32[]{:S(2)}) async-start(f32[8,24,128]{2,1,0:T(8,128)} %broadcast_in_dim.22), calls=%async_computation.13 | async-start | bytes 196608 | tf_op jit(solution)/shard_map/all_to_all | solution.py:243
  327.6 4.9 %all-to-all-done.13.got_ref = f32[8,24,128]{2,1,0:T(8,128)S(1)} async-done(((f32[8,24,128]{2,1,0:T(8,128)}), f32[8,24,128]{2,1,0:T(8,128)S(1)}, u32[]{:S(2)}, u32[]{:S(2)}) %all-to-all-start.13) | async-done | bytes 98336 | tf_op jit(solution)/shard_map/all_to_all | solution.py:243
  332.5 14.6 %all_gather.15.got_ref = f32[4,24,128]{2,1,0:T(8,128)S(1)} all-gather(f32[1,24,128]{2,1,0:T(8,128)S(1)} %fold.19), channel_id=1, replica_groups=mesh['zl'=4,'y'=4,'x'=4,'zh'=4,'core'=2] {'zh'}, dimensions={0}, use_global_device_ids=true | all-gather | bytes 61440 | tf_op jit(solution)/shard_map/all_gather | solution.py:349
  347.2 6.3 %end.1 = (f32[64,96]{1,0:T(8,128)}, f32[64,64]{1,0:T(8,128)}, f32[64,128]{1,0:T(8,128)S(1)}) custom-call(f32[4,24,128]{2,1,0:T(8,128)S(1)} %all_gather.15.got_ref, f32[64,96]{1,0:T(8,128)S(1)} %constant_dynamic-slice_fusion.1.right_ref, f32[64,64]{1,0:T(8,128)S(1)} %constant_dynamic-slice_fusion.left_ref, f32[64,128]{1,0:T(8,128)S(1)} %get-tuple-element.46.refs_2_.left_factor_ref), custom_call_target="tpu_custom_call" | custom-call | tf_op jit(solution)/shard_map/end/pallas_call | solution.py:361
  (53 shorter events, 9.2 us)
Async XLA Ops:
  2.2 10.0 %copy-start.12 = (s32[1536]{0:T(1024)S(1)}, s32[1536]{0:T(1024)}, u32[]{:S(2)}) copy-start(s32[1536]{0:T(1024)} %param.10) | copy-start | bytes 18436
  2.2 23.0 %all-to-all-start = ((f32[16,64,96]{2,1,0:T(8,128)}), f32[16,64,96]{2,1,0:T(8,128)S(1)}, u32[]{:S(2)}, u32[]{:S(2)}) async-start(f32[16,64,96]{2,1,0:T(8,128)} %broadcast_in_dim.21), calls=%async_computation | async-start | bytes 1048576 | tf_op jit(solution)/shard_map/all_to_all | solution.py:243
  25.5 1.2 copy-start
  25.8 0.9 copy-start.10
  69.5 7.9 %copy-start.13 = (s32[2048]{0:T(1024)S(1)}, s32[2048]{0:T(1024)}, u32[]{:S(2)}) copy-start(s32[2048]{0:T(1024)} %param.9) | copy-start | bytes 24580
  69.5 17.4 %all-to-all-start.2 = ((f32[8,128,128]{2,1,0:T(8,128)}), f32[8,128,128]{2,1,0:T(8,128)S(1)}, u32[]{:S(2)}, u32[]{:S(2)}) async-start(f32[8,128,128]{2,1,0:T(8,128)} %fold.11), calls=%async_computation.2 | async-start | bytes 1048576 | tf_op jit(solution)/shard_map/all_to_all | solution.py:258
  111.5 15.9 %all-to-all-start.4 = ((f32[16,48,128]{2,1,0:T(8,128)}), f32[16,48,128]{2,1,0:T(8,128)S(1)}, u32[]{:S(2)}, u32[]{:S(2)}) async-start(f32[16,48,128]{2,1,0:T(8,128)} %fold.12), calls=%async_computation.4 | async-start | bytes 786432 | tf_op jit(solution)/shard_map/all_to_all | solution.py:258
  122.1 0.8 copy-start.3
  122.8 50.2 %copy-start.5 = (f32[64,128]{1,0:T(8,128)}, f32[64,128]{1,0:T(8,128)S(1)}, u32[]{:S(2)}) copy-start(f32[64,128]{1,0:T(8,128)S(1)} %get-tuple-element.30.refs_5_.refs_2_) | copy-start | bytes 98308
  127.4 1.0 copy-start.4
  164.7 17.8 %all-to-all-start.6 = ((f32[8,128,128]{2,1,0:T(8,128)}), f32[8,128,128]{2,1,0:T(8,128)S(1)}, u32[]{:S(2)}, u32[]{:S(2)}) async-start(f32[8,128,128]{2,1,0:T(8,128)} %fold.14), calls=%async_computation.6 | async-start | bytes 1048576 | tf_op jit(solution)/shard_map/all_to_all | solution.py:258
  179.2 0.8 copy-start.1
  182.5 1.0 copy-start.2
  207.8 15.9 %all-to-all-start.8 = ((f32[16,48,128]{2,1,0:T(8,128)}), f32[16,48,128]{2,1,0:T(8,128)S(1)}, u32[]{:S(2)}, u32[]{:S(2)}) async-start(f32[16,48,128]{2,1,0:T(8,128)} %fold.15), calls=%async_computation.8 | async-start | bytes 786432 | tf_op jit(solution)/shard_map/all_to_all | solution.py:258
  218.4 8.1 %copy-start.7 = (f32[64,128]{1,0:T(8,128)}, f32[64,128]{1,0:T(8,128)S(1)}, u32[]{:S(2)}) copy-start(f32[64,128]{1,0:T(8,128)S(1)} %get-tuple-element.38.refs_5_.refs_2_) | copy-start | bytes 98308
  261.2 6.5 %copy-start.8 = (f32[64,128]{1,0:T(8,128)S(1)}, f32[64,128]{1,0:T(8,128)}, u32[]{:S(2)}) copy-start(f32[64,128]{1,0:T(8,128)} %copy-done.7) | copy-start | bytes 98308
  261.2 16.0 %all-to-all-start.10 = ((f32[8,128,128]{2,1,0:T(8,128)}), f32[8,128,128]{2,1,0:T(8,128)S(1)}, u32[]{:S(2)}, u32[]{:S(2)}) async-start(f32[8,128,128]{2,1,0:T(8,128)} %fold.17), calls=%async_computation.10 | async-start | bytes 1048576 | tf_op jit(solution)/shard_map/all_to_all | solution.py:258
  277.2 0.7 copy-start.11
  302.5 15.9 %all-to-all-start.12 = ((f32[16,48,128]{2,1,0:T(8,128)}), f32[16,48,128]{2,1,0:T(8,128)S(1)}, u32[]{:S(2)}, u32[]{:S(2)}) async-start(f32[16,48,128]{2,1,0:T(8,128)} %fold.18), calls=%async_computation.12 | async-start | bytes 786432 | tf_op jit(solution)/shard_map/all_to_all | solution.py:258
  307.0 0.8 copy-start.6
  307.8 0.8 copy-start.9
  321.5 11.0 %all-to-all-start.13 = ((f32[8,24,128]{2,1,0:T(8,128)}), f32[8,24,128]{2,1,0:T(8,128)S(1)}, u32[]{:S(2)}, u32[]{:S(2)}) async-start(f32[8,24,128]{2,1,0:T(8,128)} %broadcast_in_dim.22), calls=%async_computation.13 | async-start | bytes 196608 | tf_op jit(solution)/shard_map/all_to_all | solution.py:243

commit v3 on v2

--- a/solution.py
+++ b/solution.py
@@ -13,6 +13,7 @@
 TILE = 128
 BLOCK = 64
 GRAM_ROWS = 24
+HALF_ROWS = 16
 HIGH = lax.Precision.HIGHEST
 
 ROW = ("zl", "y")
@@ -61,15 +62,26 @@
     ).astype(jnp.float32)
     whole = jnp.concatenate([gram, eye], axis=1)
     groups = [whole[8 * i : 8 * i + 8] for i in range(BLOCK // 8)]
-    for j in range(BLOCK):
-        first = j // 8
-        k = j % 8
-        row = groups[first][k : k + 1]
-        root = lax.rsqrt(row[:, j : j + 1])
-        scaled = row * root
-        out_ref[j : j + 1, :] = scaled
-        for i in range(first, BLOCK // 8):
-            groups[i] = groups[i] - (groups[i][:, j : j + 1] * root) * scaled
+    for first in range(BLOCK // 8):
+        base = 8 * first
+        below = range(first, BLOCK // 8)
+        spread = {
+            i: [
+                jnp.broadcast_to(groups[i][:, base + m : base + m + 1], groups[i].shape)
+                for m in range(8)
+            ]
+            for i in below
+        }
+        for k in range(8):
+            root = lax.rsqrt(spread[first][k][k : k + 1])
+            scaled = groups[first][k : k + 1] * root
+            out_ref[base + k : base + k + 1, :] = scaled
+            across = {m: spread[first][m][k : k + 1] * root for m in range(k + 1, 8)}
+            for i in below:
+                times = spread[i][k] * root
+                groups[i] = groups[i] - times * scaled
+                for m in across:
+                    spread[i][m] = spread[i][m] - times * across[m]
 
 
 def split_three(value):
@@ -77,12 +89,21 @@
     rest = value - high.astype(jnp.float32)
     middle = rest.astype(jnp.bfloat16)
     low = (rest - middle.astype(jnp.float32)).astype(jnp.bfloat16)
-    return jnp.concatenate([high, middle, low], axis=0)
+    return high, middle, low
+
+
+def exact_dot(left, right):
+    high, middle, low = left
+    first = jnp.concatenate([high, high, middle, high, middle, low], axis=1)
+    high, middle, low = right
+    second = jnp.concatenate([high, middle, high, low, middle, high], axis=0)
+    return jnp.dot(first, second, preferred_element_type=jnp.float32)
 
 
 def product(slots_ref, count_ref, tiles_ref, parts_ref, sums_ref, forward, cb):
     count = count_ref[0]
-    group = 4
+    spare = sums_ref.shape[0] // BLOCK - 1
+    group = 16
 
     def visit(step, carry):
         added = []
@@ -95,7 +116,7 @@
                 (local_col, local_row) if forward else (local_row, local_col)
             )
             tile = tiles_ref[t]
-            tile = jnp.where(t < count, tile, jnp.zeros_like(tile))
+            target = jnp.where(t < count, target, spare)
             parts = parts_ref[pl.ds(pl.multiple_of(source * 192, 64), 192), :]
             dims = (((1,), (1 if forward else 0,)), ((), ()))
             value = lax.dot_general(
@@ -111,27 +132,49 @@
 
 
 def add_gram(gram, value):
-    return gram + lax.dot_general(
-        value, value, (((1,), (1,)), ((), ())), precision=HIGH,
+    same, cross = gram
+    high, middle, low = split_three(value)
+    dims = (((1,), (1,)), ((), ()))
+    same += lax.dot_general(
+        jnp.concatenate([high, middle], axis=1), jnp.concatenate([high, middle], axis=1), dims,
         preferred_element_type=jnp.float32,
     )
+    cross += lax.dot_general(
+        jnp.concatenate([high, high], axis=1), jnp.concatenate([middle, low], axis=1), dims,
+        preferred_element_type=jnp.float32,
+    )
+    return same, cross
+
+
+def no_gram():
+    return (jnp.zeros((BLOCK, BLOCK), jnp.float32),) * 2
+
+
+def whole_gram(gram):
+    same, cross = gram
+    return same + cross + jnp.transpose(cross)
 
 
 def send_panel(
-    slots_ref, count_ref, tiles_ref, panel_ref, scale_ref, sent_ref, parts_ref, sums_ref, *, forward, cb
+    slots_ref, count_ref, tiles_ref, panel_ref, scale_ref, sent_ref, parts_ref, sums_ref, *, forward, cb, core=None
 ):
     sums_ref[...] = jnp.zeros_like(sums_ref)
-    gram = jnp.zeros((BLOCK, BLOCK), jnp.float32)
+    gram = no_gram()
     for b in range(panel_ref.shape[0] // BLOCK):
         value = panel_ref[64 * b : 64 * b + 64, :]
         gram = add_gram(gram, value)
-        parts_ref[192 * b : 192 * b + 192, :] = split_three(
-            value * scale_ref[b : b + 1, :]
+        parts_ref[192 * b : 192 * b + 192, :] = jnp.concatenate(
+            split_three(value * scale_ref[b : b + 1, :]), axis=0
         )
     product(slots_ref, count_ref, tiles_ref, parts_ref, sums_ref, forward, cb)
-    packed = pack_gram(gram)
+    packed = pack_gram(whole_gram(gram))
+    if core is not None:
+        cross = packed[HALF_ROWS:]
+        packed = jnp.where(
+            core == 0, packed[:HALF_ROWS], jnp.concatenate([cross, cross], axis=0)
+        )
     count = sent_ref.shape[0]
-    rows = sums_ref.shape[0] // count
+    rows = (sums_ref.shape[0] - BLOCK) // count
     for k in range(count):
         sent_ref[k, :rows, :] = sums_ref[rows * k : rows * k + rows, :]
         sent_ref[k, rows:, :] = packed
@@ -144,13 +187,18 @@
     )
 
 
-def fold_kernel(got_ref, out_ref):
+def fold_kernel(got_ref, out_ref, *rest):
     rows = out_ref.shape[-2]
     total = got_ref[0, :rows, :]
     for k in range(1, got_ref.shape[0]):
         total += got_ref[k, :rows, :]
     for k in range(out_ref.shape[0]):
         out_ref[k] = total
+    if rest:
+        other = got_ref[0, rows:, :]
+        for k in range(1, got_ref.shape[0]):
+            other += got_ref[k, rows:, :]
+        rest[0][...] = other
 
 
 def sum_gram(got_ref):
@@ -160,13 +208,31 @@
     return unpack_gram(packed)
 
 
-def factor_kernel(*refs, with_old):
+def join_gram(core_ref, own_ref, other_ref):
+    first = core_ref[0] == 0
+    own, other = own_ref[...], other_ref[...]
+    return unpack_gram(
+        jnp.concatenate(
+            [
+                jnp.where(first, own, other),
+                jnp.where(first, other, own)[: GRAM_ROWS - HALF_ROWS],
+            ],
+            axis=0,
+        )
+    )
+
+
+def factor_kernel(*refs, with_old, halves):
+    refs = list(refs)
+    if halves:
+        gram, refs = join_gram(*refs[:3]), refs[3:]
+    else:
+        gram, refs = sum_gram(refs[0]), refs[1:]
     if not with_old:
-        got_ref, factor_ref = refs
-        factor_rows(sum_gram(got_ref), factor_ref)
+        factor_rows(gram, refs[0])
         return
-    got_ref, old_ref, old_factor_ref, factor_ref, part_ref = refs
-    factor_rows(sum_gram(got_ref), factor_ref)
+    old_ref, old_factor_ref, factor_ref, part_ref = refs
+    factor_rows(gram, factor_ref)
     upper_mask = lax.broadcasted_iota(
         jnp.int32, (BLOCK, BLOCK), 0
     ) <= lax.broadcasted_iota(jnp.int32, (BLOCK, BLOCK), 1)
@@ -187,18 +253,20 @@
     tables = []
     if not last:
         tables, refs = refs[:3], refs[3:]
+    core = None
+    if not (forward or last):
+        core, refs = refs[0][0], refs[1:]
     got_ref, scale_ref, factor_ref = refs[:3]
     refs = refs[3:]
     if with_old:
         part_ref, refs = refs[0], refs[1:]
     panel_ref, sent_ref = refs[:2]
-    inverse = factor_ref[:, BLOCK:]
-    gram = jnp.zeros((BLOCK, BLOCK), jnp.float32)
+    inverse = split_three(factor_ref[:, BLOCK:])
+    gram = no_gram()
     for b in range(panel_ref.shape[0] // BLOCK):
         where = slice(64 * b, 64 * b + 64)
-        value = jnp.dot(
-            inverse, got_ref[where, :] * scale_ref[b : b + 1, :], precision=HIGH,
-            preferred_element_type=jnp.float32,
+        value = exact_dot(
+            inverse, split_three(got_ref[where, :] * scale_ref[b : b + 1, :])
         )
         if with_old:
             value += part_ref[where, :]
@@ -206,11 +274,11 @@
         if last:
             gram = add_gram(gram, value)
     if last:
-        sent_ref[...] = pack_gram(gram)
+        sent_ref[...] = pack_gram(whole_gram(gram))
     else:
         send_panel(
             *tables, panel_ref, scale_ref, sent_ref, refs[2], refs[3],
-            forward=forward, cb=cb,
+            forward=forward, cb=cb, core=core,
         )
 
 
@@ -243,12 +311,15 @@
     return lax.all_to_all(copies, axes, 0, 0, tiled=True)
 
 
-def fold(got, copies, rows):
+def fold(got, copies, rows, rest=False):
+    shapes = [f32(copies, rows, TILE)]
+    if rest:
+        shapes.append(f32(got.shape[1] - rows, TILE))
     return pl.pallas_call(
         fold_kernel,
-        out_shape=f32(copies, rows, TILE),
+        out_shape=shapes,
         in_specs=[VMEM],
-        out_specs=VMEM,
+        out_specs=[VMEM] * len(shapes),
         compiler_params=PARAMS,
         name="fold",
     )(got)
@@ -260,17 +331,19 @@
 
 def sum_col(sent):
     near = lax.axis_size(NEAR)
-    own = fold(exchange(sent, NEAR), 1, sent.shape[1])[0]
+    own = fold(exchange(sent, NEAR), 1, sent.shape[1])[0][0]
     got = lax.all_gather(own, "zh", axis=0, tiled=False)
     rows = sent.shape[1] - GRAM_ROWS
-    return got, exchange(fold(got, near, rows), NEAR).reshape(near * rows, TILE)
-
-
-def sum_row(sent):
+    return [got], exchange(fold(got, near, rows)[0], NEAR).reshape(near * rows, TILE)
+
+
+def sum_row(sent, core):
     count = lax.axis_size(ROW)
-    got = exchange(sent, ROW)
-    rows = sent.shape[1] - GRAM_ROWS
-    return got, exchange(fold(got, count, rows), ROW).reshape(count * rows, TILE)
+    rows = sent.shape[1] - HALF_ROWS
+    copies, own = fold(exchange(sent, ROW), count, rows, rest=True)
+    whole = exchange(copies, ROW).reshape(count * rows, TILE)
+    other = lax.ppermute(own, "core", [(0, 1), (1, 0)])
+    return [core, own, other], whole
 
 
 def per_device(tiles, tile_slots, tile_counts, user_degree, item_degree, start_panel):
@@ -282,6 +355,7 @@
     rows = lax.axis_size(ROW)
     cols = lax.axis_size(COL)
     near = lax.axis_size(NEAR)
+    core = lax.axis_index("core").astype(jnp.int32).reshape(1)
     user_scale = lax.rsqrt(user_degree.astype(jnp.float32)).reshape(rb, TILE)
     item_scale = lax.rsqrt(item_degree.astype(jnp.float32)).reshape(cb, TILE)
 
@@ -290,9 +364,9 @@
     start = jnp.transpose(start, (1, 0, 2)).reshape(cb * BLOCK, TILE)
 
     user_messages = f32(near, rb * BLOCK // near + GRAM_ROWS, TILE)
-    item_messages = f32(rows, cb * BLOCK // rows + GRAM_ROWS, TILE)
-    user_sums = pltpu.VMEM((rb * BLOCK, TILE), jnp.float32)
-    item_sums = pltpu.VMEM((cb * BLOCK, TILE), jnp.float32)
+    item_messages = f32(rows, cb * BLOCK // rows + HALF_ROWS, TILE)
+    user_sums = pltpu.VMEM((rb * BLOCK + BLOCK, TILE), jnp.float32)
+    item_sums = pltpu.VMEM((cb * BLOCK + BLOCK, TILE), jnp.float32)
     user_parts = pltpu.VMEM((rb * 192, TILE), jnp.bfloat16)
     item_parts = pltpu.VMEM((cb * 192, TILE), jnp.bfloat16)
     sent = pl.pallas_call(
@@ -311,19 +385,23 @@
         users = half % 2 == 1
         last = half == 2 * STEPS
         with_old = half > 1
-        got, whole = sum_col(sent) if users else sum_row(sent)
+        gram, whole = sum_col(sent) if users else sum_row(sent, core)
         panel_shape = f32((rb if users else cb) * BLOCK, TILE)
         old = [panels[half - 2], factors[half - 2]] if with_old else []
         factored = pl.pallas_call(
-            functools.partial(factor_kernel, with_old=with_old),
+            functools.partial(factor_kernel, with_old=with_old, halves=not users),
             out_shape=[f32(BLOCK, 2 * BLOCK)] + ([panel_shape] if with_old else []),
-            in_specs=[VMEM] * (1 + len(old)),
+            in_specs=([VMEM] if users else [SMEM, VMEM, VMEM]) + [VMEM] * len(old),
             out_specs=[VMEM] * (2 if with_old else 1),
             compiler_params=PARAMS,
             name=f"factor{half}",
-        )(got, *old)
+        )(*gram, *old)
         factors.append(factored[0])
         tables = [] if last else [slots, count, tile_stack]
+        table_specs = [] if last else [SMEM, SMEM, VMEM]
+        if users:
+            tables.append(core)
+            table_specs.append(SMEM)
         operands = [whole, user_scale if users else item_scale, *factored]
         panel, sent = pl.pallas_call(
             functools.partial(
@@ -335,7 +413,7 @@
                 if last
                 else (item_messages if users else user_messages),
             ],
-            in_specs=([] if last else [SMEM, SMEM, VMEM]) + [VMEM] * len(operands),
+            in_specs=table_specs + [VMEM] * len(operands),
             out_specs=[VMEM, VMEM],
             scratch_shapes=[]
             if last
@@ -345,7 +423,7 @@
         )(*tables, *operands)
         panels.append(panel)
 
-    gram = fold(gather_whole(sent, NEAR, near), 1, GRAM_ROWS)[0]
+    gram = fold(gather_whole(sent, NEAR, near), 1, GRAM_ROWS)[0][0]
     gram = lax.all_gather(gram, "zh", axis=0, tiled=False)
 
     user_group = rb * TILE // cols

time: 357 us -> 338 us (0.947)
  Pallas kernels: 66 us -> 33.2 us
  starting transfers between devices: 51.5 us -> 68.3 us
  waiting for transfers between devices: 40.1 us -> 51.9 us
  blocking collectives: 183 us -> 174 us
  local copies, waits for them, and re-layouts: 12 us -> 6.25 us
    pallas_call x16, Pallas kernels: 40.8 us -> 18.6 us  [the longest x6 13.6 us: per_device(): pl.pallas_call(functools.partial(factor_kernel, with_old=with_old, halves...]
    ppermute x0 -> x3, starting transfers between devices: none -> 11.4 us  [sum_row(): other = lax.ppermute(own, 'core', [(0, 1), (1, 0)])]
    all_to_all x6, waiting for transfers between devices: 22.3 us -> 31.9 us  [exchange(): return lax.all_to_all(messages, axes, 0, 0, tiled=True)]
    all_to_all x6, blocking collectives: 111 us -> 104 us  [exchange(): return lax.all_to_all(messages, axes, 0, 0, tiled=True)]
    pallas_call x6, Pallas kernels: 16.6 us -> 10.4 us  [per_device(): pl.pallas_call(functools.partial(step_kernel, forward=not users, cb=cb, w...]
    unnamed x32 -> x12, local copies, waits for them, and re-layouts: 8.46 us -> 2.68 us
    all_to_all x6, starting transfers between devices: 36.1 us -> 40.9 us  [exchange(): return lax.all_to_all(messages, axes, 0, 0, tiled=True)]
    pallas_call x1, Pallas kernels: 6.31 us -> 2.59 us  [per_device(): pl.pallas_call(functools.partial(end_kernel, left_size=rb * TILE * rows,...]
  transfers between devices with their start and end apart: 8 -> 11, of which waited for: 8 -> 11; matrix products, arithmetic and copies ran while one was open for 0% -> 0% of each run, Pallas kernels for 10% -> 4%
where the time goes in v3:
time: 338 us; the launch traced here: 335 us
  blocking collectives  174 us (51%)
  starting transfers between devices  68.3 us (20%)
  waiting for transfers between devices  51.9 us (15%)
  Pallas kernels  33.2 us (10%)
  local copies, waits for them, and re-layouts  6.25 us (2%)
    all_to_all x6, blocking collectives, exchange(): return lax.all_to_all(messages, axes, 0, 0, tiled=True)  104 us
    all_gather x3, blocking collectives, sum_col(): got = lax.all_gather(own, 'zh', axis=0, tiled=False)  55.5 us
    all_to_all x6, starting transfers between devices, exchange(): return lax.all_to_all(messages, axes, 0, 0, tiled=True)  40.9 us
    all_to_all x6, waiting for transfers between devices, exchange(): return lax.all_to_all(messages, axes, 0, 0, tiled=True)  31.9 us
    all_to_all x2, waiting for transfers between devices, gather_whole(): return lax.all_to_all(copies, axes, 0, 0, tiled=True)  17.9 us
    all_to_all x2, starting transfers between devices, gather_whole(): return lax.all_to_all(copies, axes, 0, 0, tiled=True)  16 us
    all_gather x1, blocking collectives, per_device(): gram = lax.all_gather(gram, 'zh', axis=0, tiled=False)  14.4 us
    pallas_call x6, Pallas kernels, per_device(): pl.pallas_call(functools.partial(factor_kernel, with_old=with_old, halves...  13.6 us
  transfers between devices with their start and end apart: 11, of which 11 were waited for; matrix products, arithmetic and copies ran while one was open for 0% of the time, Pallas kernels for 4%

profile of v3, /device:TPU:1, one launch (start us, length us, event | category | flops | bytes accessed | tf_op | source)
XLA Modules:
  0.0 335.3 jit_solution(8367097965090149590)
XLA Ops:
  0.6 1.6 broadcast_in_dim.21
  2.2 9.3 %all-to-all-start = ((f32[16,64,96]{2,1,0:T(8,128)}), f32[16,64,96]{2,1,0:T(8,128)S(1)}, u32[]{:S(2)}, u32[]{:S(2)}) async-start(f32[16,64,96]{2,1,0:T(8,128)} %broadcast_in_dim.21), calls=%async_computation | async-start | bytes 1048576 | tf_op jit(solution)/shard_map/all_to_all | solution.py:311
  12.2 13.0 %all-to-all-done = f32[16,64,96]{2,1,0:T(8,128)S(1)} async-done(((f32[16,64,96]{2,1,0:T(8,128)}), f32[16,64,96]{2,1,0:T(8,128)S(1)}, u32[]{:S(2)}, u32[]{:S(2)}) %all-to-all-start) | async-done | bytes 393248 | tf_op jit(solution)/shard_map/all_to_all | solution.py:311
  25.8 0.9 copy-done
  26.7 1.5 start.1
  28.3 17.5 %all_to_all.70.got_ref = f32[8,152,128]{2,1,0:T(8,128)S(1)} all-to-all(f32[8,152,128]{2,1,0:T(8,128)S(1)} %start.1), channel_id=1, replica_groups=mesh['zl'=4,'y'=4,'x'=4,'zh'=4,'core'=2] {'x','core'}, dimensions={0} | all-to-all | bytes 1245184 | tf_op jit(solution)/shard_map/all_to_all | solution.py:329
  45.8 22.8 %all_gather.12.got_ref.refs_0_ = f32[4,152,128]{2,1,0:T(8,128)S(1)} all-gather(f32[1,152,128]{2,1,0:T(8,128)S(1)} %fold.10), channel_id=1, replica_groups=mesh['zl'=4,'y'=4,'x'=4,'zh'=4,'core'=2] {'zh'}, dimensions={0}, use_global_device_ids=true | all-gather | bytes 389120 | tf_op jit(solution)/shard_map/all_gather | solution.py:335
  68.6 0.8 fold.11
  69.5 6.1 %all-to-all-start.2 = ((f32[8,128,128]{2,1,0:T(8,128)}), f32[8,128,128]{2,1,0:T(8,128)S(1)}, u32[]{:S(2)}, u32[]{:S(2)}) async-start(f32[8,128,128]{2,1,0:T(8,128)} %fold.11), calls=%async_computation.2 | async-start | bytes 1048576 | tf_op jit(solution)/shard_map/all_to_all | solution.py:329
  75.6 1.7 factor1.1.refs_6_.refs_4_
  77.3 7.8 %all-to-all-done.2 = f32[8,128,128]{2,1,0:T(8,128)S(1)} async-done(((f32[8,128,128]{2,1,0:T(8,128)}), f32[8,128,128]{2,1,0:T(8,128)S(1)}, u32[]{:S(2)}, u32[]{:S(2)}) %all-to-all-start.2) | async-done | bytes 524320 | tf_op jit(solution)/shard_map/all_to_all | solution.py:329
  85.1 1.9 half1.1
  87.0 19.0 %all_to_all.71.got_ref = f32[16,64,128]{2,1,0:T(8,128)S(1)} all-to-all(f32[16,64,128]{2,1,0:T(8,128)S(1)} %get-tuple-element.35), channel_id=1, replica_groups=mesh['zl'=4,'y'=4,'x'=4,'zh'=4,'core'=2] {'zl','y'}, dimensions={0} | all-to-all | bytes 1048576 | tf_op jit(solution)/shard_map/all_to_all | solution.py:329
  106.8 5.3 %all-to-all-start.4 = ((f32[16,48,128]{2,1,0:T(8,128)}), f32[16,48,128]{2,1,0:T(8,128)S(1)}, u32[]{:S(2)}, u32[]{:S(2)}) async-start(f32[16,48,128]{2,1,0:T(8,128)} %get-tuple-element.36), calls=%async_computation.4 | async-start | bytes 786432 | tf_op jit(solution)/shard_map/all_to_all | solution.py:329
  112.1 3.7 %collective-permute-start = (f32[16,128]{1,0:T(8,128)S(1)}, f32[16,128]{1,0:T(8,128)S(1)}, u32[]{:S(2)}, u32[]{:S(2)}) collective-permute-start(f32[16,128]{1,0:T(8,128)S(1)} %get-tuple-element.37.refs_1_), channel_id=1, source_target_pairs={{0,1},{1,0},{2,3},{3,2},{4,5},{5,4},{6,7},{7,6},{8,9},{9,8},{10,11... | collective-permute-start | bytes 24584 | tf_op jit(solution)/shard_map/ppermute | solution.py:345
  116.7 2.3 factor2.1
  119.0 3.8 %all-to-all-done.4 = f32[16,48,128]{2,1,0:T(8,128)S(1)} async-done(((f32[16,48,128]{2,1,0:T(8,128)}), f32[16,48,128]{2,1,0:T(8,128)S(1)}, u32[]{:S(2)}, u32[]{:S(2)}) %all-to-all-start.4) | async-done | bytes 393248 | tf_op jit(solution)/shard_map/all_to_all | solution.py:329
  122.8 1.9 half2.1
  124.7 16.4 %all_to_all.72.got_ref = f32[8,152,128]{2,1,0:T(8,128)S(1)} all-to-all(f32[8,152,128]{2,1,0:T(8,128)S(1)} %get-tuple-element.40), channel_id=1, replica_groups=mesh['zl'=4,'y'=4,'x'=4,'zh'=4,'core'=2] {'x','core'}, dimensions={0} | all-to-all | bytes 1245184 | tf_op jit(solution)/shard_map/all_to_all | solution.py:329
  141.2 16.5 %all_gather.13.got_ref.refs_0_ = f32[4,152,128]{2,1,0:T(8,128)S(1)} all-gather(f32[1,152,128]{2,1,0:T(8,128)S(1)} %fold.13), channel_id=1, replica_groups=mesh['zl'=4,'y'=4,'x'=4,'zh'=4,'core'=2] {'zh'}, dimensions={0}, use_global_device_ids=true | all-gather | bytes 389120 | tf_op jit(solution)/shard_map/all_gather | solution.py:335
  157.7 0.8 fold.14
  158.5 8.1 %all-to-all-start.6 = ((f32[8,128,128]{2,1,0:T(8,128)}), f32[8,128,128]{2,1,0:T(8,128)S(1)}, u32[]{:S(2)}, u32[]{:S(2)}) async-start(f32[8,128,128]{2,1,0:T(8,128)} %fold.14), calls=%async_computation.6 | async-start | bytes 1048576 | tf_op jit(solution)/shard_map/all_to_all | solution.py:329
  166.6 2.4 factor3.1
  169.1 7.1 %all-to-all-done.6 = f32[8,128,128]{2,1,0:T(8,128)S(1)} async-done(((f32[8,128,128]{2,1,0:T(8,128)}), f32[8,128,128]{2,1,0:T(8,128)S(1)}, u32[]{:S(2)}, u32[]{:S(2)}) %all-to-all-start.6) | async-done | bytes 524320 | tf_op jit(solution)/shard_map/all_to_all | solution.py:329
  176.1 1.9 half3.1
  178.0 17.3 %all_to_all.73.got_ref = f32[16,64,128]{2,1,0:T(8,128)S(1)} all-to-all(f32[16,64,128]{2,1,0:T(8,128)S(1)} %get-tuple-element.44), channel_id=1, replica_groups=mesh['zl'=4,'y'=4,'x'=4,'zh'=4,'core'=2] {'zl','y'}, dimensions={0} | all-to-all | bytes 1048576 | tf_op jit(solution)/shard_map/all_to_all | solution.py:329
  196.0 5.3 %all-to-all-start.8 = ((f32[16,48,128]{2,1,0:T(8,128)}), f32[16,48,128]{2,1,0:T(8,128)S(1)}, u32[]{:S(2)}, u32[]{:S(2)}) async-start(f32[16,48,128]{2,1,0:T(8,128)} %get-tuple-element.45), calls=%async_computation.8 | async-start | bytes 786432 | tf_op jit(solution)/shard_map/all_to_all | solution.py:329
  201.3 3.9 %collective-permute-start.1 = (f32[16,128]{1,0:T(8,128)S(1)}, f32[16,128]{1,0:T(8,128)S(1)}, u32[]{:S(2)}, u32[]{:S(2)}) collective-permute-start(f32[16,128]{1,0:T(8,128)S(1)} %get-tuple-element.46.refs_1_), channel_id=1, source_target_pairs={{0,1},{1,0},{2,3},{3,2},{4,5},{5,4},{6,7},{7,6},{8,9},{9,8},{10,11... | collective-permute-start | bytes 24584 | tf_op jit(solution)/shard_map/ppermute | solution.py:345
  205.9 2.3 factor4.1
  208.2 3.8 %all-to-all-done.8 = f32[16,48,128]{2,1,0:T(8,128)S(1)} async-done(((f32[16,48,128]{2,1,0:T(8,128)}), f32[16,48,128]{2,1,0:T(8,128)S(1)}, u32[]{:S(2)}, u32[]{:S(2)}) %all-to-all-start.8) | async-done | bytes 393248 | tf_op jit(solution)/shard_map/all_to_all | solution.py:329
  212.0 1.9 half4.1
  213.9 16.4 %all_to_all.74.got_ref = f32[8,152,128]{2,1,0:T(8,128)S(1)} all-to-all(f32[8,152,128]{2,1,0:T(8,128)S(1)} %get-tuple-element.50), channel_id=1, replica_groups=mesh['zl'=4,'y'=4,'x'=4,'zh'=4,'core'=2] {'x','core'}, dimensions={0} | all-to-all | bytes 1245184 | tf_op jit(solution)/shard_map/all_to_all | solution.py:329
  230.4 16.2 %all_gather.14.got_ref.refs_0_ = f32[4,152,128]{2,1,0:T(8,128)S(1)} all-gather(f32[1,152,128]{2,1,0:T(8,128)S(1)} %fold.16), channel_id=1, replica_groups=mesh['zl'=4,'y'=4,'x'=4,'zh'=4,'core'=2] {'zh'}, dimensions={0}, use_global_device_ids=true | all-gather | bytes 389120 | tf_op jit(solution)/shard_map/all_gather | solution.py:335
  246.6 0.8 fold.17
  247.4 10.8 %all-to-all-start.10 = ((f32[8,128,128]{2,1,0:T(8,128)}), f32[8,128,128]{2,1,0:T(8,128)S(1)}, u32[]{:S(2)}, u32[]{:S(2)}) async-start(f32[8,128,128]{2,1,0:T(8,128)} %fold.17), calls=%async_computation.10 | async-start | bytes 1048576 | tf_op jit(solution)/shard_map/all_to_all | solution.py:329
  258.2 2.4 factor5.1
  260.6 7.1 %all-to-all-done.10 = f32[8,128,128]{2,1,0:T(8,128)S(1)} async-done(((f32[8,128,128]{2,1,0:T(8,128)}), f32[8,128,128]{2,1,0:T(8,128)S(1)}, u32[]{:S(2)}, u32[]{:S(2)}) %all-to-all-start.10) | async-done | bytes 524320 | tf_op jit(solution)/shard_map/all_to_all | solution.py:329
  267.7 1.9 half5.1
  269.6 17.4 %all_to_all.75.got_ref = f32[16,64,128]{2,1,0:T(8,128)S(1)} all-to-all(f32[16,64,128]{2,1,0:T(8,128)S(1)} %get-tuple-element.54), channel_id=1, replica_groups=mesh['zl'=4,'y'=4,'x'=4,'zh'=4,'core'=2] {'zl','y'}, dimensions={0} | all-to-all | bytes 1048576 | tf_op jit(solution)/shard_map/all_to_all | solution.py:329
  287.8 5.3 %all-to-all-start.12 = ((f32[16,48,128]{2,1,0:T(8,128)}), f32[16,48,128]{2,1,0:T(8,128)S(1)}, u32[]{:S(2)}, u32[]{:S(2)}) async-start(f32[16,48,128]{2,1,0:T(8,128)} %get-tuple-element.55), calls=%async_computation.12 | async-start | bytes 786432 | tf_op jit(solution)/shard_map/all_to_all | solution.py:329
  293.6 3.7 %collective-permute-start.2 = (f32[16,128]{1,0:T(8,128)S(1)}, f32[16,128]{1,0:T(8,128)S(1)}, u32[]{:S(2)}, u32[]{:S(2)}) collective-permute-start(f32[16,128]{1,0:T(8,128)S(1)} %get-tuple-element.56.refs_1_), channel_id=1, source_target_pairs={{0,1},{1,0},{2,3},{3,2},{4,5},{5,4},{6,7},{7,6},{8,9},{9,8},{10,11... | collective-permute-start | bytes 24584 | tf_op jit(solution)/shard_map/ppermute | solution.py:345
  298.2 2.3 factor6.1
  301.3 2.4 all-to-all-done.12
  303.8 1.0 half6.1
  305.8 6.7 %all-to-all-start.13 = ((f32[8,24,128]{2,1,0:T(8,128)}), f32[8,24,128]{2,1,0:T(8,128)S(1)}, u32[]{:S(2)}, u32[]{:S(2)}) async-start(f32[8,24,128]{2,1,0:T(8,128)} %broadcast_in_dim.22), calls=%async_computation.13 | async-start | bytes 196608 | tf_op jit(solution)/shard_map/all_to_all | solution.py:311
  312.6 4.9 %all-to-all-done.13.got_ref = f32[8,24,128]{2,1,0:T(8,128)S(1)} async-done(((f32[8,24,128]{2,1,0:T(8,128)}), f32[8,24,128]{2,1,0:T(8,128)S(1)}, u32[]{:S(2)}, u32[]{:S(2)}) %all-to-all-start.13) | async-done | bytes 98336 | tf_op jit(solution)/shard_map/all_to_all | solution.py:311
  317.5 14.4 %all_gather.15.got_ref = f32[4,24,128]{2,1,0:T(8,128)S(1)} all-gather(f32[1,24,128]{2,1,0:T(8,128)S(1)} %fold.19), channel_id=1, replica_groups=mesh['zl'=4,'y'=4,'x'=4,'zh'=4,'core'=2] {'zh'}, dimensions={0}, use_global_device_ids=true | all-gather | bytes 61440 | tf_op jit(solution)/shard_map/all_gather | solution.py:427
  331.9 2.6 end.1
  (39 shorter events, 8.5 us)
Async XLA Ops:
  2.2 10.0 %copy-start.2 = (s32[1536]{0:T(1024)S(1)}, s32[1536]{0:T(1024)}, u32[]{:S(2)}) copy-start(s32[1536]{0:T(1024)} %param.10) | copy-start | bytes 18436
  2.2 23.0 %all-to-all-start = ((f32[16,64,96]{2,1,0:T(8,128)}), f32[16,64,96]{2,1,0:T(8,128)S(1)}, u32[]{:S(2)}, u32[]{:S(2)}) async-start(f32[16,64,96]{2,1,0:T(8,128)} %broadcast_in_dim.21), calls=%async_computation | async-start | bytes 1048576 | tf_op jit(solution)/shard_map/all_to_all | solution.py:311
  25.5 1.2 copy-start
  25.8 0.9 copy-start.1
  69.5 6.1 %copy-start.3 = (s32[2048]{0:T(1024)S(1)}, s32[2048]{0:T(1024)}, u32[]{:S(2)}) copy-start(s32[2048]{0:T(1024)} %param.9) | copy-start | bytes 24580
  69.5 15.6 %all-to-all-start.2 = ((f32[8,128,128]{2,1,0:T(8,128)}), f32[8,128,128]{2,1,0:T(8,128)S(1)}, u32[]{:S(2)}, u32[]{:S(2)}) async-start(f32[8,128,128]{2,1,0:T(8,128)} %fold.11), calls=%async_computation.2 | async-start | bytes 1048576 | tf_op jit(solution)/shard_map/all_to_all | solution.py:329
  106.8 16.0 %all-to-all-start.4 = ((f32[16,48,128]{2,1,0:T(8,128)}), f32[16,48,128]{2,1,0:T(8,128)S(1)}, u32[]{:S(2)}, u32[]{:S(2)}) async-start(f32[16,48,128]{2,1,0:T(8,128)} %get-tuple-element.36), calls=%async_computation.4 | async-start | bytes 786432 | tf_op jit(solution)/shard_map/all_to_all | solution.py:329
  112.1 4.6 %collective-permute-start = (f32[16,128]{1,0:T(8,128)S(1)}, f32[16,128]{1,0:T(8,128)S(1)}, u32[]{:S(2)}, u32[]{:S(2)}) collective-permute-start(f32[16,128]{1,0:T(8,128)S(1)} %get-tuple-element.37.refs_1_), channel_id=1, source_target_pairs={{0,1},{1,0},{2,3},{3,2},{4,5},{5,4},{6,7},{7,6},{8,9},{9,8},{10,11... | collective-permute-start | bytes 24584 | tf_op jit(solution)/shard_map/ppermute | solution.py:345
  158.5 17.6 %all-to-all-start.6 = ((f32[8,128,128]{2,1,0:T(8,128)}), f32[8,128,128]{2,1,0:T(8,128)S(1)}, u32[]{:S(2)}, u32[]{:S(2)}) async-start(f32[8,128,128]{2,1,0:T(8,128)} %fold.14), calls=%async_computation.6 | async-start | bytes 1048576 | tf_op jit(solution)/shard_map/all_to_all | solution.py:329
  196.0 16.0 %all-to-all-start.8 = ((f32[16,48,128]{2,1,0:T(8,128)}), f32[16,48,128]{2,1,0:T(8,128)S(1)}, u32[]{:S(2)}, u32[]{:S(2)}) async-start(f32[16,48,128]{2,1,0:T(8,128)} %get-tuple-element.45), calls=%async_computation.8 | async-start | bytes 786432 | tf_op jit(solution)/shard_map/all_to_all | solution.py:329
  201.3 4.6 %collective-permute-start.1 = (f32[16,128]{1,0:T(8,128)S(1)}, f32[16,128]{1,0:T(8,128)S(1)}, u32[]{:S(2)}, u32[]{:S(2)}) collective-permute-start(f32[16,128]{1,0:T(8,128)S(1)} %get-tuple-element.46.refs_1_), channel_id=1, source_target_pairs={{0,1},{1,0},{2,3},{3,2},{4,5},{5,4},{6,7},{7,6},{8,9},{9,8},{10,11... | collective-permute-start | bytes 24584 | tf_op jit(solution)/shard_map/ppermute | solution.py:345
  247.4 20.3 %all-to-all-start.10 = ((f32[8,128,128]{2,1,0:T(8,128)}), f32[8,128,128]{2,1,0:T(8,128)S(1)}, u32[]{:S(2)}, u32[]{:S(2)}) async-start(f32[8,128,128]{2,1,0:T(8,128)} %fold.17), calls=%async_computation.10 | async-start | bytes 1048576 | tf_op jit(solution)/shard_map/all_to_all | solution.py:329
  287.8 16.0 %all-to-all-start.12 = ((f32[16,48,128]{2,1,0:T(8,128)}), f32[16,48,128]{2,1,0:T(8,128)S(1)}, u32[]{:S(2)}, u32[]{:S(2)}) async-start(f32[16,48,128]{2,1,0:T(8,128)} %get-tuple-element.55), calls=%async_computation.12 | async-start | bytes 786432 | tf_op jit(solution)/shard_map/all_to_all | solution.py:329
  293.6 4.6 %collective-permute-start.2 = (f32[16,128]{1,0:T(8,128)S(1)}, f32[16,128]{1,0:T(8,128)S(1)}, u32[]{:S(2)}, u32[]{:S(2)}) collective-permute-start(f32[16,128]{1,0:T(8,128)S(1)} %get-tuple-element.56.refs_1_), channel_id=1, source_target_pairs={{0,1},{1,0},{2,3},{3,2},{4,5},{5,4},{6,7},{7,6},{8,9},{9,8},{10,11... | collective-permute-start | bytes 24584 | tf_op jit(solution)/shard_map/ppermute | solution.py:345
  305.8 11.7 %all-to-all-start.13 = ((f32[8,24,128]{2,1,0:T(8,128)}), f32[8,24,128]{2,1,0:T(8,128)S(1)}, u32[]{:S(2)}, u32[]{:S(2)}) async-start(f32[8,24,128]{2,1,0:T(8,128)} %broadcast_in_dim.22), calls=%async_computation.13 | async-start | bytes 196608 | tf_op jit(solution)/shard_map/all_to_all | solution.py:311

commit v4 on v3

--- a/solution.py
+++ b/solution.py
@@ -14,11 +14,12 @@
 BLOCK = 64
 GRAM_ROWS = 24
 HALF_ROWS = 16
+UNIT = 32
 HIGH = lax.Precision.HIGHEST
 
 ROW = ("zl", "y")
 COL = ("x", "zh", "core")
-NEAR = ("x", "core")
+NEAR = ("core", "x")
 
 
 def pack_gram(gram):
@@ -156,7 +157,8 @@
 
 
 def send_panel(
-    slots_ref, count_ref, tiles_ref, panel_ref, scale_ref, sent_ref, parts_ref, sums_ref, *, forward, cb, core=None
+    slots_ref, count_ref, tiles_ref, panel_ref, scale_ref, sent_ref, parts_ref, sums_ref, *, forward, cb, core=None,
+    ready=None,
 ):
     sums_ref[...] = jnp.zeros_like(sums_ref)
     gram = no_gram()
@@ -166,6 +168,8 @@
         parts_ref[192 * b : 192 * b + 192, :] = jnp.concatenate(
             split_three(value * scale_ref[b : b + 1, :]), axis=0
         )
+    if ready is not None:
+        ready.wait()
     product(slots_ref, count_ref, tiles_ref, parts_ref, sums_ref, forward, cb)
     packed = pack_gram(whole_gram(gram))
     if core is not None:
@@ -180,10 +184,50 @@
         sent_ref[k, rows:, :] = packed
 
 
-def start_kernel(slots_ref, count_ref, tiles_ref, panel_ref, scale_ref, sent_ref, parts_ref, sums_ref, *, cb):
+def unit_rows(unit, rows):
+    for piece in range(BLOCK // 16):
+        at = BLOCK * unit + 16 * piece
+        yield at % rows, UNIT * (at // rows)
+
+
+def pack_kernel(panel_ref, out_ref):
+    rows = out_ref.shape[1]
+    columns = [[] for _ in range(TILE // UNIT)]
+    for unit in range(panel_ref.shape[1] // UNIT):
+        value = panel_ref[:, UNIT * unit : UNIT * unit + UNIT]
+        for piece, (_, lane) in enumerate(unit_rows(unit, rows)):
+            columns[lane // UNIT].append(value[16 * piece : 16 * piece + 16])
+    packed = jnp.concatenate(
+        [jnp.concatenate(pieces, axis=0) for pieces in columns], axis=1
+    )
+    for k in range(out_ref.shape[0]):
+        out_ref[k] = packed
+
+
+def start_kernel(
+    slots_ref, count_ref, tiles_ref, got_ref, scale_ref, panel_ref, sent_ref,
+    parts_ref, sums_ref, near_tiles_ref, sem, *, cb, units,
+):
+    copy = pltpu.make_async_copy(tiles_ref, near_tiles_ref, sem)
+    copy.start()
+    rows = got_ref.shape[1]
+    for b in range(cb):
+        found = []
+        for c in range(TILE // UNIT):
+            device, unit = divmod(TILE // UNIT * b + c, units)
+            found.append(
+                [
+                    got_ref[device, row : row + 16, lane : lane + UNIT]
+                    for row, lane in unit_rows(unit, rows)
+                ]
+            )
+        for piece in range(BLOCK // 16):
+            panel_ref[64 * b + 16 * piece : 64 * b + 16 * piece + 16, :] = (
+                jnp.concatenate([pieces[piece] for pieces in found], axis=1)
+            )
     send_panel(
-        slots_ref, count_ref, tiles_ref, panel_ref, scale_ref, sent_ref, parts_ref, sums_ref,
-        forward=True, cb=cb,
+        slots_ref, count_ref, near_tiles_ref, panel_ref, scale_ref, sent_ref, parts_ref, sums_ref,
+        forward=True, cb=cb, ready=copy,
     )
 
 
@@ -222,6 +266,14 @@
     )
 
 
+def lower_factor(factor_ref):
+    lower = jnp.transpose(factor_ref[:, :BLOCK])
+    mask = lax.broadcasted_iota(
+        jnp.int32, (BLOCK, BLOCK), 0
+    ) >= lax.broadcasted_iota(jnp.int32, (BLOCK, BLOCK), 1)
+    return jnp.where(mask, lower, 0.0)
+
+
 def factor_kernel(*refs, with_old, halves):
     refs = list(refs)
     if halves:
@@ -231,8 +283,9 @@
     if not with_old:
         factor_rows(gram, refs[0])
         return
-    old_ref, old_factor_ref, factor_ref, part_ref = refs
+    old_ref, old_factor_ref, factor_ref, part_ref, lower_ref = refs
     factor_rows(gram, factor_ref)
+    lower_ref[...] = lower_factor(factor_ref)
     upper_mask = lax.broadcasted_iota(
         jnp.int32, (BLOCK, BLOCK), 0
     ) <= lax.broadcasted_iota(jnp.int32, (BLOCK, BLOCK), 1)
@@ -274,7 +327,9 @@
         if last:
             gram = add_gram(gram, value)
     if last:
-        sent_ref[...] = pack_gram(whole_gram(gram))
+        packed = pack_gram(whole_gram(gram))
+        for k in range(sent_ref.shape[0]):
+            sent_ref[k] = packed
     else:
         send_panel(
             *tables, panel_ref, scale_ref, sent_ref, refs[2], refs[3],
@@ -283,10 +338,13 @@
 
 
 def end_kernel(
-    got_ref, right_ref, left_ref, left_factor_ref, out_right_ref, out_left_ref, factor_ref, *,
-    left_size, right_size,
+    got_ref, right_ref, left_ref, left_factor_ref, first_ref, second_ref,
+    out_right_ref, out_left_ref, lower_ref, factor_ref, *, left_size, right_size,
 ):
+    lower_ref[0] = first_ref[...]
+    lower_ref[1] = second_ref[...]
     factor_rows(sum_gram(got_ref), factor_ref)
+    lower_ref[2] = lower_factor(factor_ref)
     out_right_ref[...] = math.sqrt(right_size) * jnp.dot(
         factor_ref[:, BLOCK:], right_ref[...], precision=HIGH,
         preferred_element_type=jnp.float32,
@@ -304,11 +362,6 @@
 
 def f32(*shape):
     return jax.ShapeDtypeStruct(shape, jnp.float32)
-
-
-def gather_whole(value, axes, count):
-    copies = jnp.broadcast_to(value[None], (count,) + value.shape)
-    return lax.all_to_all(copies, axes, 0, 0, tiled=True)
 
 
 def fold(got, copies, rows, rest=False):
@@ -334,7 +387,9 @@
     own = fold(exchange(sent, NEAR), 1, sent.shape[1])[0][0]
     got = lax.all_gather(own, "zh", axis=0, tiled=False)
     rows = sent.shape[1] - GRAM_ROWS
-    return [got], exchange(fold(got, near, rows)[0], NEAR).reshape(near * rows, TILE)
+    line = lax.axis_size("x")
+    half = exchange(fold(got, line, rows)[0], "x").reshape(line * rows, TILE)
+    return [got], lax.all_gather(half, "core", axis=0, tiled=True)
 
 
 def sum_row(sent, core):
@@ -359,9 +414,16 @@
     user_scale = lax.rsqrt(user_degree.astype(jnp.float32)).reshape(rb, TILE)
     item_scale = lax.rsqrt(item_degree.astype(jnp.float32)).reshape(cb, TILE)
 
-    start = gather_whole(start_panel, ROW, rows)
-    start = jnp.transpose(start, (1, 0, 2)).reshape(BLOCK, cb, TILE)
-    start = jnp.transpose(start, (1, 0, 2)).reshape(cb * BLOCK, TILE)
+    units = start_panel.shape[1] // UNIT
+    start = pl.pallas_call(
+        pack_kernel,
+        out_shape=f32(rows, BLOCK * units * UNIT // TILE, TILE),
+        in_specs=[VMEM],
+        out_specs=VMEM,
+        compiler_params=PARAMS,
+        name="pack",
+    )(start_panel)
+    start = exchange(start, ROW)
 
     user_messages = f32(near, rb * BLOCK // near + GRAM_ROWS, TILE)
     item_messages = f32(rows, cb * BLOCK // rows + HALF_ROWS, TILE)
@@ -369,18 +431,24 @@
     item_sums = pltpu.VMEM((cb * BLOCK + BLOCK, TILE), jnp.float32)
     user_parts = pltpu.VMEM((rb * 192, TILE), jnp.bfloat16)
     item_parts = pltpu.VMEM((cb * 192, TILE), jnp.bfloat16)
-    sent = pl.pallas_call(
-        functools.partial(start_kernel, cb=cb),
-        out_shape=user_messages,
-        in_specs=[SMEM, SMEM, VMEM, VMEM, VMEM],
-        out_specs=VMEM,
-        scratch_shapes=[item_parts, user_sums],
+    start, sent = pl.pallas_call(
+        functools.partial(start_kernel, cb=cb, units=units),
+        out_shape=[f32(cb * BLOCK, TILE), user_messages],
+        in_specs=[SMEM, SMEM, pl.BlockSpec(memory_space=pl.ANY), VMEM, VMEM],
+        out_specs=[VMEM, VMEM],
+        scratch_shapes=[
+            item_parts,
+            user_sums,
+            pltpu.VMEM(tile_stack.shape, tile_stack.dtype),
+            pltpu.SemaphoreType.DMA,
+        ],
         compiler_params=PARAMS,
         name="start",
     )(slots, count, tile_stack, start, item_scale)
 
     panels = [start]
     factors = []
+    lower = []
     for half in range(1, 2 * STEPS + 1):
         users = half % 2 == 1
         last = half == 2 * STEPS
@@ -390,26 +458,28 @@
         old = [panels[half - 2], factors[half - 2]] if with_old else []
         factored = pl.pallas_call(
             functools.partial(factor_kernel, with_old=with_old, halves=not users),
-            out_shape=[f32(BLOCK, 2 * BLOCK)] + ([panel_shape] if with_old else []),
+            out_shape=[f32(BLOCK, 2 * BLOCK)]
+            + ([panel_shape, f32(BLOCK, BLOCK)] if with_old else []),
             in_specs=([VMEM] if users else [SMEM, VMEM, VMEM]) + [VMEM] * len(old),
-            out_specs=[VMEM] * (2 if with_old else 1),
+            out_specs=[VMEM] * (3 if with_old else 1),
             compiler_params=PARAMS,
             name=f"factor{half}",
         )(*gram, *old)
         factors.append(factored[0])
+        lower += factored[2:]
         tables = [] if last else [slots, count, tile_stack]
         table_specs = [] if last else [SMEM, SMEM, VMEM]
         if users:
             tables.append(core)
             table_specs.append(SMEM)
-        operands = [whole, user_scale if users else item_scale, *factored]
+        operands = [whole, user_scale if users else item_scale, *factored[:2]]
         panel, sent = pl.pallas_call(
             functools.partial(
                 step_kernel, forward=not users, cb=cb, with_old=with_old, last=last
             ),
             out_shape=[
                 panel_shape,
-                f32(GRAM_ROWS, TILE)
+                f32(near, GRAM_ROWS, TILE)
                 if last
                 else (item_messages if users else user_messages),
             ],
@@ -423,7 +493,7 @@
         )(*tables, *operands)
         panels.append(panel)
 
-    gram = fold(gather_whole(sent, NEAR, near), 1, GRAM_ROWS)[0][0]
+    gram = fold(exchange(sent, NEAR), 1, GRAM_ROWS)[0][0]
     gram = lax.all_gather(gram, "zh", axis=0, tiled=False)
 
     user_group = rb * TILE // cols
@@ -436,28 +506,22 @@
     right = lax.dynamic_slice_in_dim(
         right.reshape(BLOCK, cb * TILE), lax.axis_index(ROW) * item_group, item_group, 1
     )
-    right_panel, left_panel, factor = pl.pallas_call(
+    right_panel, left_panel, right_factors = pl.pallas_call(
         functools.partial(
             end_kernel, left_size=rb * TILE * rows, right_size=cb * TILE * cols
         ),
         out_shape=[
             f32(BLOCK, item_group),
             f32(BLOCK, user_group),
-            f32(BLOCK, 2 * BLOCK),
+            f32(STEPS, BLOCK, BLOCK),
         ],
-        in_specs=[VMEM] * 4,
+        in_specs=[VMEM] * 6,
         out_specs=[VMEM] * 3,
+        scratch_shapes=[pltpu.VMEM((BLOCK, 2 * BLOCK), jnp.float32)],
         compiler_params=PARAMS,
         name="end",
-    )(gram, right, left, factors[-1])
-    factors.append(factor)
-    lower = [jnp.tril(jnp.transpose(f[:, :BLOCK])) for f in factors]
-    return (
-        left_panel,
-        right_panel,
-        jnp.stack(lower[1::2]),
-        jnp.stack(lower[2::2]),
-    )
+    )(gram, right, left, factors[-1], lower[1], lower[3])
+    return left_panel, right_panel, jnp.stack(lower[::2]), right_factors
 
 
 def solution(mesh):

time: 338 us -> 330 us (0.976)
  starting transfers between devices: 68.3 us -> 59.5 us
  blocking collectives: 174 us -> 180 us
  local copies, waits for them, and re-layouts: 6.25 us -> 2.5 us
    all_gather x0 -> x3, blocking collectives: none -> 22.9 us  [sum_col(): return ([got], lax.all_gather(half, 'core', axis=0, tiled=True))]
    all_to_all x6 -> x5, blocking collectives: 104 us -> 85.8 us  [exchange(): return lax.all_to_all(messages, axes, 0, 0, tiled=True)]
    all_to_all x2 -> x0, waiting for transfers between devices: 17.9 us -> none  [gather_whole(): return lax.all_to_all(copies, axes, 0, 0, tiled=True)]
    all_to_all x2 -> x0, starting transfers between devices: 16 us -> none  [gather_whole(): return lax.all_to_all(copies, axes, 0, 0, tiled=True)]
    all_to_all x6 -> x9, waiting for transfers between devices: 31.9 us -> 46.4 us  [exchange(): return lax.all_to_all(messages, axes, 0, 0, tiled=True)]
    all_to_all x6 -> x9, starting transfers between devices: 40.9 us -> 48.2 us  [exchange(): return lax.all_to_all(messages, axes, 0, 0, tiled=True)]
  transfers between devices with their start and end apart: 11 -> 12, of which waited for: 11 -> 12; matrix products, arithmetic and copies ran while one was open for 0% -> 0% of each run, Pallas kernels for 4% -> 4%
where the time goes in v4:
time: 330 us; the launch traced here: 328 us
  blocking collectives  180 us (55%)
  starting transfers between devices  59.5 us (18%)
  waiting for transfers between devices  48.6 us (15%)
  Pallas kernels  35.4 us (11%)
    all_to_all x5, blocking collectives, exchange(): return lax.all_to_all(messages, axes, 0, 0, tiled=True)  85.8 us
    all_gather x3, blocking collectives, sum_col(): got = lax.all_gather(own, 'zh', axis=0, tiled=False)  56.4 us
    all_to_all x9, starting transfers between devices, exchange(): return lax.all_to_all(messages, axes, 0, 0, tiled=True)  48.2 us
    all_to_all x9, waiting for transfers between devices, exchange(): return lax.all_to_all(messages, axes, 0, 0, tiled=True)  46.4 us
    all_gather x3, blocking collectives, sum_col(): return ([got], lax.all_gather(half, 'core', axis=0, tiled=True))  22.9 us
    all_gather x1, blocking collectives, per_device(): gram = lax.all_gather(gram, 'zh', axis=0, tiled=False)  14.5 us
    pallas_call x6, Pallas kernels, per_device(): pl.pallas_call(functools.partial(factor_kernel, with_old=with_old, halves...  13.6 us
    ppermute x3, starting transfers between devices, sum_row(): other = lax.ppermute(own, 'core', [(0, 1), (1, 0)])  11.3 us
  transfers between devices with their start and end apart: 12, of which 12 were waited for; matrix products, arithmetic and copies ran while one was open for 0% of the time, Pallas kernels for 4%

profile of v4, /device:TPU:1, one launch (start us, length us, event | category | flops | bytes accessed | tf_op | source)
XLA Modules:
  0.0 327.7 jit_solution(16816823584545538777)
XLA Ops:
  1.5 0.9 pack.1
  2.4 9.3 %all-to-all-start = ((f32[16,48,128]{2,1,0:T(8,128)}), f32[16,48,128]{2,1,0:T(8,128)S(1)}, u32[]{:S(2)}, u32[]{:S(2)}) async-start(f32[16,48,128]{2,1,0:T(8,128)} %pack.1), calls=%async_computation | async-start | bytes 786432 | tf_op jit(solution)/shard_map/all_to_all | solution.py:382
  12.4 10.7 %all-to-all-done.got_ref = f32[16,48,128]{2,1,0:T(8,128)S(1)} async-done(((f32[16,48,128]{2,1,0:T(8,128)}), f32[16,48,128]{2,1,0:T(8,128)S(1)}, u32[]{:S(2)}, u32[]{:S(2)}) %all-to-all-start) | async-done | bytes 393248 | tf_op jit(solution)/shard_map/all_to_all | solution.py:382
  23.8 2.5 start.1
  26.3 7.0 %all-to-all-start.1 = ((f32[8,152,128]{2,1,0:T(8,128)}), f32[8,152,128]{2,1,0:T(8,128)S(1)}, u32[]{:S(2)}, u32[]{:S(2)}) async-start(f32[8,152,128]{2,1,0:T(8,128)} %get-tuple-element.42), calls=%async_computation.1 | async-start | bytes 1245184 | tf_op jit(solution)/shard_map/all_to_all | solution.py:382
  33.4 10.4 %all-to-all-done.1.got_ref = f32[8,152,128]{2,1,0:T(8,128)S(1)} async-done(((f32[8,152,128]{2,1,0:T(8,128)}), f32[8,152,128]{2,1,0:T(8,128)S(1)}, u32[]{:S(2)}, u32[]{:S(2)}) %all-to-all-start.1) | async-done | bytes 622624 | tf_op jit(solution)/shard_map/all_to_all | solution.py:382
  43.8 23.0 %all_gather.21.got_ref.refs_0_ = f32[4,152,128]{2,1,0:T(8,128)S(1)} all-gather(f32[1,152,128]{2,1,0:T(8,128)S(1)} %fold.10), channel_id=1, replica_groups=mesh['zl'=4,'y'=4,'x'=4,'zh'=4,'core'=2] {'zh'}, dimensions={0}, use_global_device_ids=true | all-gather | bytes 389120 | tf_op jit(solution)/shard_map/all_gather | solution.py:388
  67.6 3.5 %all-to-all-start.2 = ((f32[4,128,128]{2,1,0:T(8,128)}), f32[4,128,128]{2,1,0:T(8,128)S(1)}, u32[]{:S(2)}, u32[]{:S(2)}) async-start(f32[4,128,128]{2,1,0:T(8,128)} %fold.11), calls=%async_computation.2 | async-start | bytes 524288 | tf_op jit(solution)/shard_map/all_to_all | solution.py:382
  71.2 1.7 factor1.1.refs_6_.refs_4_
  72.9 3.7 %all-to-all-done.2 = f32[4,128,128]{2,1,0:T(8,128)S(1)} async-done(((f32[4,128,128]{2,1,0:T(8,128)}), f32[4,128,128]{2,1,0:T(8,128)S(1)}, u32[]{:S(2)}, u32[]{:S(2)}) %all-to-all-start.2) | async-done | bytes 262176 | tf_op jit(solution)/shard_map/all_to_all | solution.py:382
  76.6 7.6 %all_gather.22.refs_4_ = f32[1024,128]{1,0:T(8,128)S(1)} all-gather(f32[512,128]{1,0:T(8,128)S(1)} %bitcast.59), channel_id=1, replica_groups=mesh['zl'=4,'y'=4,'x'=4,'zh'=4,'core'=2] {'core'}, dimensions={0}, use_global_device_ids=true | all-gather | bytes 786432 | tf_op jit(solution)/shard_map/all_gather | solution.py:392
  84.3 1.9 half1.1
  86.2 17.3 %all_to_all.70.got_ref = f32[16,64,128]{2,1,0:T(8,128)S(1)} all-to-all(f32[16,64,128]{2,1,0:T(8,128)S(1)} %get-tuple-element.43), channel_id=1, replica_groups=mesh['zl'=4,'y'=4,'x'=4,'zh'=4,'core'=2] {'zl','y'}, dimensions={0} | all-to-all | bytes 1048576 | tf_op jit(solution)/shard_map/all_to_all | solution.py:382
  104.3 4.9 %all-to-all-start.4 = ((f32[16,48,128]{2,1,0:T(8,128)}), f32[16,48,128]{2,1,0:T(8,128)S(1)}, u32[]{:S(2)}, u32[]{:S(2)}) async-start(f32[16,48,128]{2,1,0:T(8,128)} %get-tuple-element.44), calls=%async_computation.4 | async-start | bytes 786432 | tf_op jit(solution)/shard_map/all_to_all | solution.py:382
  109.2 3.7 %collective-permute-start = (f32[16,128]{1,0:T(8,128)S(1)}, f32[16,128]{1,0:T(8,128)S(1)}, u32[]{:S(2)}, u32[]{:S(2)}) collective-permute-start(f32[16,128]{1,0:T(8,128)S(1)} %get-tuple-element.45.refs_1_), channel_id=1, source_target_pairs={{0,1},{1,0},{2,3},{3,2},{4,5},{5,4},{6,7},{7,6},{8,9},{9,8},{10,11... | collective-permute-start | bytes 24584 | tf_op jit(solution)/shard_map/ppermute | solution.py:400
  113.7 2.3 factor2.1
  116.1 3.9 %all-to-all-done.4 = f32[16,48,128]{2,1,0:T(8,128)S(1)} async-done(((f32[16,48,128]{2,1,0:T(8,128)}), f32[16,48,128]{2,1,0:T(8,128)S(1)}, u32[]{:S(2)}, u32[]{:S(2)}) %all-to-all-start.4) | async-done | bytes 393248 | tf_op jit(solution)/shard_map/all_to_all | solution.py:382
  119.9 1.9 half2.1
  121.8 16.4 %all_to_all.71.got_ref = f32[8,152,128]{2,1,0:T(8,128)S(1)} all-to-all(f32[8,152,128]{2,1,0:T(8,128)S(1)} %get-tuple-element.49), channel_id=1, replica_groups=mesh['zl'=4,'y'=4,'x'=4,'zh'=4,'core'=2] {'core','x'}, dimensions={0} | all-to-all | bytes 1245184 | tf_op jit(solution)/shard_map/all_to_all | solution.py:382
  138.2 16.6 %all_gather.23.got_ref.refs_0_ = f32[4,152,128]{2,1,0:T(8,128)S(1)} all-gather(f32[1,152,128]{2,1,0:T(8,128)S(1)} %fold.13), channel_id=1, replica_groups=mesh['zl'=4,'y'=4,'x'=4,'zh'=4,'core'=2] {'zh'}, dimensions={0}, use_global_device_ids=true | all-gather | bytes 389120 | tf_op jit(solution)/shard_map/all_gather | solution.py:388
  155.6 3.4 %all-to-all-start.6 = ((f32[4,128,128]{2,1,0:T(8,128)}), f32[4,128,128]{2,1,0:T(8,128)S(1)}, u32[]{:S(2)}, u32[]{:S(2)}) async-start(f32[4,128,128]{2,1,0:T(8,128)} %fold.14), calls=%async_computation.6 | async-start | bytes 524288 | tf_op jit(solution)/shard_map/all_to_all | solution.py:382
  159.0 2.4 factor3.1
  161.5 3.0 all-to-all-done.6
  164.5 7.7 %all_gather.24.refs_4_ = f32[1024,128]{1,0:T(8,128)S(1)} all-gather(f32[512,128]{1,0:T(8,128)S(1)} %bitcast.57), channel_id=1, replica_groups=mesh['zl'=4,'y'=4,'x'=4,'zh'=4,'core'=2] {'core'}, dimensions={0}, use_global_device_ids=true | all-gather | bytes 786432 | tf_op jit(solution)/shard_map/all_gather | solution.py:392
  172.2 1.9 half3.1
  174.0 17.8 %all_to_all.72.got_ref = f32[16,64,128]{2,1,0:T(8,128)S(1)} all-to-all(f32[16,64,128]{2,1,0:T(8,128)S(1)} %get-tuple-element.53), channel_id=1, replica_groups=mesh['zl'=4,'y'=4,'x'=4,'zh'=4,'core'=2] {'zl','y'}, dimensions={0} | all-to-all | bytes 1048576 | tf_op jit(solution)/shard_map/all_to_all | solution.py:382
  192.6 4.9 %all-to-all-start.8 = ((f32[16,48,128]{2,1,0:T(8,128)}), f32[16,48,128]{2,1,0:T(8,128)S(1)}, u32[]{:S(2)}, u32[]{:S(2)}) async-start(f32[16,48,128]{2,1,0:T(8,128)} %get-tuple-element.54), calls=%async_computation.8 | async-start | bytes 786432 | tf_op jit(solution)/shard_map/all_to_all | solution.py:382
  197.6 3.9 %collective-permute-start.1 = (f32[16,128]{1,0:T(8,128)S(1)}, f32[16,128]{1,0:T(8,128)S(1)}, u32[]{:S(2)}, u32[]{:S(2)}) collective-permute-start(f32[16,128]{1,0:T(8,128)S(1)} %get-tuple-element.55.refs_1_), channel_id=1, source_target_pairs={{0,1},{1,0},{2,3},{3,2},{4,5},{5,4},{6,7},{7,6},{8,9},{9,8},{10,11... | collective-permute-start | bytes 24584 | tf_op jit(solution)/shard_map/ppermute | solution.py:400
  202.1 2.3 factor4.1
  204.4 3.9 %all-to-all-done.8 = f32[16,48,128]{2,1,0:T(8,128)S(1)} async-done(((f32[16,48,128]{2,1,0:T(8,128)}), f32[16,48,128]{2,1,0:T(8,128)S(1)}, u32[]{:S(2)}, u32[]{:S(2)}) %all-to-all-start.8) | async-done | bytes 393248 | tf_op jit(solution)/shard_map/all_to_all | solution.py:382
  208.3 1.9 half4.1
  210.2 16.4 %all_to_all.73.got_ref = f32[8,152,128]{2,1,0:T(8,128)S(1)} all-to-all(f32[8,152,128]{2,1,0:T(8,128)S(1)} %get-tuple-element.59), channel_id=1, replica_groups=mesh['zl'=4,'y'=4,'x'=4,'zh'=4,'core'=2] {'core','x'}, dimensions={0} | all-to-all | bytes 1245184 | tf_op jit(solution)/shard_map/all_to_all | solution.py:382
  226.6 16.8 %all_gather.25.got_ref.refs_0_ = f32[4,152,128]{2,1,0:T(8,128)S(1)} all-gather(f32[1,152,128]{2,1,0:T(8,128)S(1)} %fold.16), channel_id=1, replica_groups=mesh['zl'=4,'y'=4,'x'=4,'zh'=4,'core'=2] {'zh'}, dimensions={0}, use_global_device_ids=true | all-gather | bytes 389120 | tf_op jit(solution)/shard_map/all_gather | solution.py:388
  244.1 3.4 %all-to-all-start.10 = ((f32[4,128,128]{2,1,0:T(8,128)}), f32[4,128,128]{2,1,0:T(8,128)S(1)}, u32[]{:S(2)}, u32[]{:S(2)}) async-start(f32[4,128,128]{2,1,0:T(8,128)} %fold.17), calls=%async_computation.10 | async-start | bytes 524288 | tf_op jit(solution)/shard_map/all_to_all | solution.py:382
  247.5 2.4 factor5.1
  250.0 3.0 all-to-all-done.10
  253.0 7.6 %all_gather.26.refs_4_ = f32[1024,128]{1,0:T(8,128)S(1)} all-gather(f32[512,128]{1,0:T(8,128)S(1)} %bitcast.58), channel_id=1, replica_groups=mesh['zl'=4,'y'=4,'x'=4,'zh'=4,'core'=2] {'core'}, dimensions={0}, use_global_device_ids=true | all-gather | bytes 786432 | tf_op jit(solution)/shard_map/all_gather | solution.py:392
  260.6 1.9 half5.1
  262.4 17.9 %all_to_all.74.got_ref = f32[16,64,128]{2,1,0:T(8,128)S(1)} all-to-all(f32[16,64,128]{2,1,0:T(8,128)S(1)} %get-tuple-element.63), channel_id=1, replica_groups=mesh['zl'=4,'y'=4,'x'=4,'zh'=4,'core'=2] {'zl','y'}, dimensions={0} | all-to-all | bytes 1048576 | tf_op jit(solution)/shard_map/all_to_all | solution.py:382
  281.2 4.9 %all-to-all-start.12 = ((f32[16,48,128]{2,1,0:T(8,128)}), f32[16,48,128]{2,1,0:T(8,128)S(1)}, u32[]{:S(2)}, u32[]{:S(2)}) async-start(f32[16,48,128]{2,1,0:T(8,128)} %get-tuple-element.64), calls=%async_computation.12 | async-start | bytes 786432 | tf_op jit(solution)/shard_map/all_to_all | solution.py:382
  286.6 3.7 %collective-permute-start.2 = (f32[16,128]{1,0:T(8,128)S(1)}, f32[16,128]{1,0:T(8,128)S(1)}, u32[]{:S(2)}, u32[]{:S(2)}) collective-permute-start(f32[16,128]{1,0:T(8,128)S(1)} %get-tuple-element.65.refs_1_), channel_id=1, source_target_pairs={{0,1},{1,0},{2,3},{3,2},{4,5},{5,4},{6,7},{7,6},{8,9},{9,8},{10,11... | collective-permute-start | bytes 24584 | tf_op jit(solution)/shard_map/ppermute | solution.py:400
  291.1 2.3 factor6.1
  294.1 2.7 all-to-all-done.12
  296.9 1.7 half6.1
  298.9 6.7 %all-to-all-start.13 = ((f32[8,24,128]{2,1,0:T(8,128)}), f32[8,24,128]{2,1,0:T(8,128)S(1)}, u32[]{:S(2)}, u32[]{:S(2)}) async-start(f32[8,24,128]{2,1,0:T(8,128)} %get-tuple-element.69), calls=%async_computation.13 | async-start | bytes 196608 | tf_op jit(solution)/shard_map/all_to_all | solution.py:382
  305.7 4.9 %all-to-all-done.13.got_ref = f32[8,24,128]{2,1,0:T(8,128)S(1)} async-done(((f32[8,24,128]{2,1,0:T(8,128)}), f32[8,24,128]{2,1,0:T(8,128)S(1)}, u32[]{:S(2)}, u32[]{:S(2)}) %all-to-all-start.13) | async-done | bytes 98336 | tf_op jit(solution)/shard_map/all_to_all | solution.py:382
  310.6 14.5 %all_gather.27.got_ref = f32[4,24,128]{2,1,0:T(8,128)S(1)} all-gather(f32[1,24,128]{2,1,0:T(8,128)S(1)} %fold.19), channel_id=1, replica_groups=mesh['zl'=4,'y'=4,'x'=4,'zh'=4,'core'=2] {'zh'}, dimensions={0}, use_global_device_ids=true | all-gather | bytes 61440 | tf_op jit(solution)/shard_map/all_gather | solution.py:497
  325.1 2.6 end.1
  (32 shorter events, 10.0 us)
Async XLA Ops:
  0.6 22.5 %copy-start = (bf16[1,1,32,128,128]{4,3,2,1,0:T(8,128)(2,1)S(1)}, bf16[1,1,32,128,128]{4,3,2,1,0:T(8,128)(2,1)}, u32[]{:S(2)}) copy-start(bf16[1,1,32,128,128]{4,3,2,1,0:T(8,128)(2,1)} %param.6) | copy-start | bytes 3145732
  0.6 0.8 copy-start.1
  2.4 10.0 %copy-start.3 = (s32[1536]{0:T(1024)S(1)}, s32[1536]{0:T(1024)}, u32[]{:S(2)}) copy-start(s32[1536]{0:T(1024)} %param.10) | copy-start | bytes 18436
  2.4 20.7 %all-to-all-start = ((f32[16,48,128]{2,1,0:T(8,128)}), f32[16,48,128]{2,1,0:T(8,128)S(1)}, u32[]{:S(2)}, u32[]{:S(2)}) async-start(f32[16,48,128]{2,1,0:T(8,128)} %pack.1), calls=%async_computation | async-start | bytes 786432 | tf_op jit(solution)/shard_map/all_to_all | solution.py:382
  23.1 0.7 copy-start.2
  26.3 17.5 %all-to-all-start.1 = ((f32[8,152,128]{2,1,0:T(8,128)}), f32[8,152,128]{2,1,0:T(8,128)S(1)}, u32[]{:S(2)}, u32[]{:S(2)}) async-start(f32[8,152,128]{2,1,0:T(8,128)} %get-tuple-element.42), calls=%async_computation.1 | async-start | bytes 1245184 | tf_op jit(solution)/shard_map/all_to_all | solution.py:382
  67.6 3.5 %copy-start.4 = (s32[2048]{0:T(1024)S(1)}, s32[2048]{0:T(1024)}, u32[]{:S(2)}) copy-start(s32[2048]{0:T(1024)} %param.9) | copy-start | bytes 24580
  67.6 9.0 %all-to-all-start.2 = ((f32[4,128,128]{2,1,0:T(8,128)}), f32[4,128,128]{2,1,0:T(8,128)S(1)}, u32[]{:S(2)}, u32[]{:S(2)}) async-start(f32[4,128,128]{2,1,0:T(8,128)} %fold.11), calls=%async_computation.2 | async-start | bytes 524288 | tf_op jit(solution)/shard_map/all_to_all | solution.py:382
  104.3 15.7 %all-to-all-start.4 = ((f32[16,48,128]{2,1,0:T(8,128)}), f32[16,48,128]{2,1,0:T(8,128)S(1)}, u32[]{:S(2)}, u32[]{:S(2)}) async-start(f32[16,48,128]{2,1,0:T(8,128)} %get-tuple-element.44), calls=%async_computation.4 | async-start | bytes 786432 | tf_op jit(solution)/shard_map/all_to_all | solution.py:382
  109.2 4.5 %collective-permute-start = (f32[16,128]{1,0:T(8,128)S(1)}, f32[16,128]{1,0:T(8,128)S(1)}, u32[]{:S(2)}, u32[]{:S(2)}) collective-permute-start(f32[16,128]{1,0:T(8,128)S(1)} %get-tuple-element.45.refs_1_), channel_id=1, source_target_pairs={{0,1},{1,0},{2,3},{3,2},{4,5},{5,4},{6,7},{7,6},{8,9},{9,8},{10,11... | collective-permute-start | bytes 24584 | tf_op jit(solution)/shard_map/ppermute | solution.py:400
  155.6 8.9 %all-to-all-start.6 = ((f32[4,128,128]{2,1,0:T(8,128)}), f32[4,128,128]{2,1,0:T(8,128)S(1)}, u32[]{:S(2)}, u32[]{:S(2)}) async-start(f32[4,128,128]{2,1,0:T(8,128)} %fold.14), calls=%async_computation.6 | async-start | bytes 524288 | tf_op jit(solution)/shard_map/all_to_all | solution.py:382
  192.6 15.7 %all-to-all-start.8 = ((f32[16,48,128]{2,1,0:T(8,128)}), f32[16,48,128]{2,1,0:T(8,128)S(1)}, u32[]{:S(2)}, u32[]{:S(2)}) async-start(f32[16,48,128]{2,1,0:T(8,128)} %get-tuple-element.54), calls=%async_computation.8 | async-start | bytes 786432 | tf_op jit(solution)/shard_map/all_to_all | solution.py:382
  197.6 4.5 %collective-permute-start.1 = (f32[16,128]{1,0:T(8,128)S(1)}, f32[16,128]{1,0:T(8,128)S(1)}, u32[]{:S(2)}, u32[]{:S(2)}) collective-permute-start(f32[16,128]{1,0:T(8,128)S(1)} %get-tuple-element.55.refs_1_), channel_id=1, source_target_pairs={{0,1},{1,0},{2,3},{3,2},{4,5},{5,4},{6,7},{7,6},{8,9},{9,8},{10,11... | collective-permute-start | bytes 24584 | tf_op jit(solution)/shard_map/ppermute | solution.py:400
  244.1 8.9 %all-to-all-start.10 = ((f32[4,128,128]{2,1,0:T(8,128)}), f32[4,128,128]{2,1,0:T(8,128)S(1)}, u32[]{:S(2)}, u32[]{:S(2)}) async-start(f32[4,128,128]{2,1,0:T(8,128)} %fold.17), calls=%async_computation.10 | async-start | bytes 524288 | tf_op jit(solution)/shard_map/all_to_all | solution.py:382
  281.2 15.7 %all-to-all-start.12 = ((f32[16,48,128]{2,1,0:T(8,128)}), f32[16,48,128]{2,1,0:T(8,128)S(1)}, u32[]{:S(2)}, u32[]{:S(2)}) async-start(f32[16,48,128]{2,1,0:T(8,128)} %get-tuple-element.64), calls=%async_computation.12 | async-start | bytes 786432 | tf_op jit(solution)/shard_map/all_to_all | solution.py:382
  286.6 4.5 %collective-permute-start.2 = (f32[16,128]{1,0:T(8,128)S(1)}, f32[16,128]{1,0:T(8,128)S(1)}, u32[]{:S(2)}, u32[]{:S(2)}) collective-permute-start(f32[16,128]{1,0:T(8,128)S(1)} %get-tuple-element.65.refs_1_), channel_id=1, source_target_pairs={{0,1},{1,0},{2,3},{3,2},{4,5},{5,4},{6,7},{7,6},{8,9},{9,8},{10,11... | collective-permute-start | bytes 24584 | tf_op jit(solution)/shard_map/ppermute | solution.py:400
  298.9 11.7 %all-to-all-start.13 = ((f32[8,24,128]{2,1,0:T(8,128)}), f32[8,24,128]{2,1,0:T(8,128)S(1)}, u32[]{:S(2)}, u32[]{:S(2)}) async-start(f32[8,24,128]{2,1,0:T(8,128)} %get-tuple-element.69), calls=%async_computation.13 | async-start | bytes 196608 | tf_op jit(solution)/shard_map/all_to_all | solution.py:382

commit v5 on v4

--- a/solution.py
+++ b/solution.py
@@ -101,8 +101,9 @@
     return jnp.dot(first, second, preferred_element_type=jnp.float32)
 
 
-def product(slots_ref, count_ref, tiles_ref, parts_ref, sums_ref, forward, cb):
-    count = count_ref[0]
+def product(table_ref, tiles_ref, parts_ref, sums_ref, forward, cb):
+    slot_count = tiles_ref.shape[0]
+    count = table_ref[slot_count]
     spare = sums_ref.shape[0] // BLOCK - 1
     group = 16
 
@@ -110,7 +111,7 @@
         added = []
         for g in range(group):
             t = step * group + g
-            slot = slots_ref[t]
+            slot = table_ref[t]
             local_row = slot // cb
             local_col = slot - local_row * cb
             source, target = (
@@ -157,8 +158,7 @@
 
 
 def send_panel(
-    slots_ref, count_ref, tiles_ref, panel_ref, scale_ref, sent_ref, parts_ref, sums_ref, *, forward, cb, core=None,
-    ready=None,
+    table_ref, tiles_ref, panel_ref, scale_ref, sent_ref, parts_ref, sums_ref, *, forward, cb, ready=None
 ):
     sums_ref[...] = jnp.zeros_like(sums_ref)
     gram = no_gram()
@@ -170,12 +170,12 @@
         )
     if ready is not None:
         ready.wait()
-    product(slots_ref, count_ref, tiles_ref, parts_ref, sums_ref, forward, cb)
+    product(table_ref, tiles_ref, parts_ref, sums_ref, forward, cb)
     packed = pack_gram(whole_gram(gram))
-    if core is not None:
+    if not forward:
         cross = packed[HALF_ROWS:]
         packed = jnp.where(
-            core == 0, packed[:HALF_ROWS], jnp.concatenate([cross, cross], axis=0)
+            table_ref[tiles_ref.shape[0] + 1] == 0, packed[:HALF_ROWS], jnp.concatenate([cross, cross], axis=0)
         )
     count = sent_ref.shape[0]
     rows = (sums_ref.shape[0] - BLOCK) // count
@@ -205,7 +205,7 @@
 
 
 def start_kernel(
-    slots_ref, count_ref, tiles_ref, got_ref, scale_ref, panel_ref, sent_ref,
+    table_ref, tiles_ref, got_ref, scale_ref, panel_ref, sent_ref,
     parts_ref, sums_ref, near_tiles_ref, sem, *, cb, units,
 ):
     copy = pltpu.make_async_copy(tiles_ref, near_tiles_ref, sem)
@@ -226,7 +226,7 @@
                 jnp.concatenate([pieces[piece] for pieces in found], axis=1)
             )
     send_panel(
-        slots_ref, count_ref, near_tiles_ref, panel_ref, scale_ref, sent_ref, parts_ref, sums_ref,
+        table_ref, near_tiles_ref, panel_ref, scale_ref, sent_ref, parts_ref, sums_ref,
         forward=True, cb=cb, ready=copy,
     )
 
@@ -252,8 +252,8 @@
     return unpack_gram(packed)
 
 
-def join_gram(core_ref, own_ref, other_ref):
-    first = core_ref[0] == 0
+def join_gram(table_ref, own_ref, other_ref):
+    first = table_ref[table_ref.shape[0] - 1] == 0
     own, other = own_ref[...], other_ref[...]
     return unpack_gram(
         jnp.concatenate(
@@ -305,10 +305,7 @@
     refs = list(refs)
     tables = []
     if not last:
-        tables, refs = refs[:3], refs[3:]
-    core = None
-    if not (forward or last):
-        core, refs = refs[0][0], refs[1:]
+        tables, refs = refs[:2], refs[2:]
     got_ref, scale_ref, factor_ref = refs[:3]
     refs = refs[3:]
     if with_old:
@@ -333,7 +330,7 @@
     else:
         send_panel(
             *tables, panel_ref, scale_ref, sent_ref, refs[2], refs[3],
-            forward=forward, cb=cb, core=core,
+            forward=forward, cb=cb,
         )
 
 
@@ -392,25 +389,24 @@
     return [got], lax.all_gather(half, "core", axis=0, tiled=True)
 
 
-def sum_row(sent, core):
+def sum_row(sent, table):
     count = lax.axis_size(ROW)
     rows = sent.shape[1] - HALF_ROWS
     copies, own = fold(exchange(sent, ROW), count, rows, rest=True)
     whole = exchange(copies, ROW).reshape(count * rows, TILE)
     other = lax.ppermute(own, "core", [(0, 1), (1, 0)])
-    return [core, own, other], whole
+    return [table, own, other], whole
 
 
 def per_device(tiles, tile_slots, tile_counts, user_degree, item_degree, start_panel):
     tile_stack = tiles[0, 0]
-    slots = tile_slots[0, 0]
-    count = tile_counts[0]
     rb = user_degree.shape[0] // TILE
     cb = item_degree.shape[0] // TILE
     rows = lax.axis_size(ROW)
     cols = lax.axis_size(COL)
     near = lax.axis_size(NEAR)
     core = lax.axis_index("core").astype(jnp.int32).reshape(1)
+    table = jnp.concatenate([tile_slots[0, 0], tile_counts[0], core])
     user_scale = lax.rsqrt(user_degree.astype(jnp.float32)).reshape(rb, TILE)
     item_scale = lax.rsqrt(item_degree.astype(jnp.float32)).reshape(cb, TILE)
 
@@ -434,7 +430,7 @@
     start, sent = pl.pallas_call(
         functools.partial(start_kernel, cb=cb, units=units),
         out_shape=[f32(cb * BLOCK, TILE), user_messages],
-        in_specs=[SMEM, SMEM, pl.BlockSpec(memory_space=pl.ANY), VMEM, VMEM],
+        in_specs=[SMEM, pl.BlockSpec(memory_space=pltpu.HBM), VMEM, VMEM],
         out_specs=[VMEM, VMEM],
         scratch_shapes=[
             item_parts,
@@ -444,7 +440,7 @@
         ],
         compiler_params=PARAMS,
         name="start",
-    )(slots, count, tile_stack, start, item_scale)
+    )(table, tile_stack, start, item_scale)
 
     panels = [start]
     factors = []
@@ -453,7 +449,7 @@
         users = half % 2 == 1
         last = half == 2 * STEPS
         with_old = half > 1
-        gram, whole = sum_col(sent) if users else sum_row(sent, core)
+        gram, whole = sum_col(sent) if users else sum_row(sent, table)
         panel_shape = f32((rb if users else cb) * BLOCK, TILE)
         old = [panels[half - 2], factors[half - 2]] if with_old else []
         factored = pl.pallas_call(
@@ -467,11 +463,8 @@
         )(*gram, *old)
         factors.append(factored[0])
         lower += factored[2:]
-        tables = [] if last else [slots, count, tile_stack]
-        table_specs = [] if last else [SMEM, SMEM, VMEM]
-        if users:
-            tables.append(core)
-            table_specs.append(SMEM)
+        tables = [] if last else [table, tile_stack]
+        table_specs = [] if last else [SMEM, VMEM]
         operands = [whole, user_scale if users else item_scale, *factored[:2]]
         panel, sent = pl.pallas_call(
             functools.partial(
@@ -493,8 +486,8 @@
         )(*tables, *operands)
         panels.append(panel)
 
-    gram = fold(exchange(sent, NEAR), 1, GRAM_ROWS)[0][0]
-    gram = lax.all_gather(gram, "zh", axis=0, tiled=False)
+    gram = fold(exchange(sent, NEAR), lax.axis_size("zh"), GRAM_ROWS)[0]
+    gram = exchange(gram, "zh")
 
     user_group = rb * TILE // cols
     item_group = cb * TILE // rows

time: 330 us -> 331 us (level)
    all_to_all x5 -> x6, blocking collectives: 85.8 us -> 103 us  [exchange(): return lax.all_to_all(messages, axes, 0, 0, tiled=True)]
    all_gather x1 -> x0, blocking collectives: 14.5 us -> none  [per_device(): gram = lax.all_gather(gram, 'zh', axis=0, tiled=False)]
  transfers between devices with their start and end apart: 12 -> 12, of which waited for: 12 -> 12; matrix products, arithmetic and copies ran while one was open for 0% -> 1% of each run, Pallas kernels for 4% -> 5%
where the time goes in v5:
time: 331 us; the launch traced here: 329 us
  blocking collectives  182 us (55%)
  starting transfers between devices  58.6 us (18%)
  waiting for transfers between devices  47.1 us (14%)
  Pallas kernels  36.8 us (11%)
    all_to_all x6, blocking collectives, exchange(): return lax.all_to_all(messages, axes, 0, 0, tiled=True)  103 us
    all_gather x3, blocking collectives, sum_col(): got = lax.all_gather(own, 'zh', axis=0, tiled=False)  56 us
    all_to_all x9, starting transfers between devices, exchange(): return lax.all_to_all(messages, axes, 0, 0, tiled=True)  47.4 us
    all_to_all x9, waiting for transfers between devices, exchange(): return lax.all_to_all(messages, axes, 0, 0, tiled=True)  45.3 us
    all_gather x3, blocking collectives, sum_col(): return ([got], lax.all_gather(half, 'core', axis=0, tiled=True))  23.4 us
    pallas_call x6, Pallas kernels, per_device(): pl.pallas_call(functools.partial(factor_kernel, with_old=with_old, halves...  15.3 us
    ppermute x3, starting transfers between devices, sum_row(): other = lax.ppermute(own, 'core', [(0, 1), (1, 0)])  11.3 us
    pallas_call x6, Pallas kernels, per_device(): pl.pallas_call(functools.partial(step_kernel, forward=not users, cb=cb, w...  11.1 us
  transfers between devices with their start and end apart: 12, of which 12 were waited for; matrix products, arithmetic and copies ran while one was open for 1% of the time, Pallas kernels for 5%

profile of v5, /device:TPU:1, one launch (start us, length us, event | category | flops | bytes accessed | tf_op | source)
XLA Modules:
  0.0 329.3 jit_solution(4716822762662705568)
XLA Ops:
  1.5 0.9 pack.1
  2.4 9.2 %all-to-all-start = ((f32[16,48,128]{2,1,0:T(8,128)}), f32[16,48,128]{2,1,0:T(8,128)S(1)}, u32[]{:S(2)}, u32[]{:S(2)}) async-start(f32[16,48,128]{2,1,0:T(8,128)} %pack.1), calls=%async_computation | async-start | bytes 786432 | tf_op jit(solution)/shard_map/all_to_all | solution.py:379
  13.0 10.0 %all-to-all-done.got_ref = f32[16,48,128]{2,1,0:T(8,128)S(1)} async-done(((f32[16,48,128]{2,1,0:T(8,128)}), f32[16,48,128]{2,1,0:T(8,128)S(1)}, u32[]{:S(2)}, u32[]{:S(2)}) %all-to-all-start) | async-done | bytes 393248 | tf_op jit(solution)/shard_map/all_to_all | solution.py:379
  23.0 1.7 start.1
  24.7 17.4 %all_to_all.75.got_ref = f32[8,152,128]{2,1,0:T(8,128)S(1)} all-to-all(f32[8,152,128]{2,1,0:T(8,128)S(1)} %get-tuple-element.42), channel_id=1, replica_groups=mesh['zl'=4,'y'=4,'x'=4,'zh'=4,'core'=2] {'core','x'}, dimensions={0} | all-to-all | bytes 1245184 | tf_op jit(solution)/shard_map/all_to_all | solution.py:379
  42.2 22.7 %all_gather.18.got_ref.refs_0_ = f32[4,152,128]{2,1,0:T(8,128)S(1)} all-gather(f32[1,152,128]{2,1,0:T(8,128)S(1)} %fold.10), channel_id=1, replica_groups=mesh['zl'=4,'y'=4,'x'=4,'zh'=4,'core'=2] {'zh'}, dimensions={0}, use_global_device_ids=true | all-gather | bytes 389120 | tf_op jit(solution)/shard_map/all_gather | solution.py:385
  65.7 3.5 %all-to-all-start.2 = ((f32[4,128,128]{2,1,0:T(8,128)}), f32[4,128,128]{2,1,0:T(8,128)S(1)}, u32[]{:S(2)}, u32[]{:S(2)}) async-start(f32[4,128,128]{2,1,0:T(8,128)} %fold.11), calls=%async_computation.2 | async-start | bytes 524288 | tf_op jit(solution)/shard_map/all_to_all | solution.py:379
  69.2 1.7 factor1.1.refs_4_
  71.0 3.7 %all-to-all-done.2 = f32[4,128,128]{2,1,0:T(8,128)S(1)} async-done(((f32[4,128,128]{2,1,0:T(8,128)}), f32[4,128,128]{2,1,0:T(8,128)S(1)}, u32[]{:S(2)}, u32[]{:S(2)}) %all-to-all-start.2) | async-done | bytes 262176 | tf_op jit(solution)/shard_map/all_to_all | solution.py:379
  74.7 7.6 %all_gather.19.refs_2_ = f32[1024,128]{1,0:T(8,128)S(1)} all-gather(f32[512,128]{1,0:T(8,128)S(1)} %bitcast.48), channel_id=1, replica_groups=mesh['zl'=4,'y'=4,'x'=4,'zh'=4,'core'=2] {'core'}, dimensions={0}, use_global_device_ids=true | all-gather | bytes 786432 | tf_op jit(solution)/shard_map/all_gather | solution.py:389
  82.3 1.9 half1.1
  84.2 17.4 %all_to_all.76.got_ref = f32[16,64,128]{2,1,0:T(8,128)S(1)} all-to-all(f32[16,64,128]{2,1,0:T(8,128)S(1)} %get-tuple-element.43), channel_id=1, replica_groups=mesh['zl'=4,'y'=4,'x'=4,'zh'=4,'core'=2] {'zl','y'}, dimensions={0} | all-to-all | bytes 1048576 | tf_op jit(solution)/shard_map/all_to_all | solution.py:379
  102.3 4.9 %all-to-all-start.4 = ((f32[16,48,128]{2,1,0:T(8,128)}), f32[16,48,128]{2,1,0:T(8,128)S(1)}, u32[]{:S(2)}, u32[]{:S(2)}) async-start(f32[16,48,128]{2,1,0:T(8,128)} %get-tuple-element.44), calls=%async_computation.4 | async-start | bytes 786432 | tf_op jit(solution)/shard_map/all_to_all | solution.py:379
  107.3 3.7 %collective-permute-start = (f32[16,128]{1,0:T(8,128)S(1)}, f32[16,128]{1,0:T(8,128)S(1)}, u32[]{:S(2)}, u32[]{:S(2)}) collective-permute-start(f32[16,128]{1,0:T(8,128)S(1)} %get-tuple-element.45.refs_1_), channel_id=1, source_target_pairs={{0,1},{1,0},{2,3},{3,2},{4,5},{5,4},{6,7},{7,6},{8,9},{9,8},{10,11... | collective-permute-start | bytes 24584 | tf_op jit(solution)/shard_map/ppermute | solution.py:397
  111.8 2.9 factor2.1
  114.7 3.4 %all-to-all-done.4 = f32[16,48,128]{2,1,0:T(8,128)S(1)} async-done(((f32[16,48,128]{2,1,0:T(8,128)}), f32[16,48,128]{2,1,0:T(8,128)S(1)}, u32[]{:S(2)}, u32[]{:S(2)}) %all-to-all-start.4) | async-done | bytes 393248 | tf_op jit(solution)/shard_map/all_to_all | solution.py:379
  118.0 1.9 half2.1
  119.9 16.4 %all_to_all.77.got_ref = f32[8,152,128]{2,1,0:T(8,128)S(1)} all-to-all(f32[8,152,128]{2,1,0:T(8,128)S(1)} %get-tuple-element.49), channel_id=1, replica_groups=mesh['zl'=4,'y'=4,'x'=4,'zh'=4,'core'=2] {'core','x'}, dimensions={0} | all-to-all | bytes 1245184 | tf_op jit(solution)/shard_map/all_to_all | solution.py:379
  136.3 16.8 %all_gather.20.got_ref.refs_0_ = f32[4,152,128]{2,1,0:T(8,128)S(1)} all-gather(f32[1,152,128]{2,1,0:T(8,128)S(1)} %fold.13), channel_id=1, replica_groups=mesh['zl'=4,'y'=4,'x'=4,'zh'=4,'core'=2] {'zh'}, dimensions={0}, use_global_device_ids=true | all-gather | bytes 389120 | tf_op jit(solution)/shard_map/all_gather | solution.py:385
  153.8 3.4 %all-to-all-start.6 = ((f32[4,128,128]{2,1,0:T(8,128)}), f32[4,128,128]{2,1,0:T(8,128)S(1)}, u32[]{:S(2)}, u32[]{:S(2)}) async-start(f32[4,128,128]{2,1,0:T(8,128)} %fold.14), calls=%async_computation.6 | async-start | bytes 524288 | tf_op jit(solution)/shard_map/all_to_all | solution.py:379
  157.3 2.4 factor3.1
  159.7 3.0 all-to-all-done.6
  162.8 7.6 %all_gather.21.refs_2_ = f32[1024,128]{1,0:T(8,128)S(1)} all-gather(f32[512,128]{1,0:T(8,128)S(1)} %bitcast.46), channel_id=1, replica_groups=mesh['zl'=4,'y'=4,'x'=4,'zh'=4,'core'=2] {'core'}, dimensions={0}, use_global_device_ids=true | all-gather | bytes 786432 | tf_op jit(solution)/shard_map/all_gather | solution.py:389
  170.4 1.9 half3.1
  172.2 17.9 %all_to_all.78.got_ref = f32[16,64,128]{2,1,0:T(8,128)S(1)} all-to-all(f32[16,64,128]{2,1,0:T(8,128)S(1)} %get-tuple-element.53), channel_id=1, replica_groups=mesh['zl'=4,'y'=4,'x'=4,'zh'=4,'core'=2] {'zl','y'}, dimensions={0} | all-to-all | bytes 1048576 | tf_op jit(solution)/shard_map/all_to_all | solution.py:379
  190.9 4.9 %all-to-all-start.8 = ((f32[16,48,128]{2,1,0:T(8,128)}), f32[16,48,128]{2,1,0:T(8,128)S(1)}, u32[]{:S(2)}, u32[]{:S(2)}) async-start(f32[16,48,128]{2,1,0:T(8,128)} %get-tuple-element.54), calls=%async_computation.8 | async-start | bytes 786432 | tf_op jit(solution)/shard_map/all_to_all | solution.py:379
  195.8 3.9 %collective-permute-start.1 = (f32[16,128]{1,0:T(8,128)S(1)}, f32[16,128]{1,0:T(8,128)S(1)}, u32[]{:S(2)}, u32[]{:S(2)}) collective-permute-start(f32[16,128]{1,0:T(8,128)S(1)} %get-tuple-element.55.refs_1_), channel_id=1, source_target_pairs={{0,1},{1,0},{2,3},{3,2},{4,5},{5,4},{6,7},{7,6},{8,9},{9,8},{10,11... | collective-permute-start | bytes 24584 | tf_op jit(solution)/shard_map/ppermute | solution.py:397
  200.3 2.9 factor4.1
  203.2 3.4 %all-to-all-done.8 = f32[16,48,128]{2,1,0:T(8,128)S(1)} async-done(((f32[16,48,128]{2,1,0:T(8,128)}), f32[16,48,128]{2,1,0:T(8,128)S(1)}, u32[]{:S(2)}, u32[]{:S(2)}) %all-to-all-start.8) | async-done | bytes 393248 | tf_op jit(solution)/shard_map/all_to_all | solution.py:379
  206.6 1.9 half4.1
  208.5 16.4 %all_to_all.79.got_ref = f32[8,152,128]{2,1,0:T(8,128)S(1)} all-to-all(f32[8,152,128]{2,1,0:T(8,128)S(1)} %get-tuple-element.59), channel_id=1, replica_groups=mesh['zl'=4,'y'=4,'x'=4,'zh'=4,'core'=2] {'core','x'}, dimensions={0} | all-to-all | bytes 1245184 | tf_op jit(solution)/shard_map/all_to_all | solution.py:379
  224.9 16.5 %all_gather.22.got_ref.refs_0_ = f32[4,152,128]{2,1,0:T(8,128)S(1)} all-gather(f32[1,152,128]{2,1,0:T(8,128)S(1)} %fold.16), channel_id=1, replica_groups=mesh['zl'=4,'y'=4,'x'=4,'zh'=4,'core'=2] {'zh'}, dimensions={0}, use_global_device_ids=true | all-gather | bytes 389120 | tf_op jit(solution)/shard_map/all_gather | solution.py:385
  242.1 3.4 %all-to-all-start.10 = ((f32[4,128,128]{2,1,0:T(8,128)}), f32[4,128,128]{2,1,0:T(8,128)S(1)}, u32[]{:S(2)}, u32[]{:S(2)}) async-start(f32[4,128,128]{2,1,0:T(8,128)} %fold.17), calls=%async_computation.10 | async-start | bytes 524288 | tf_op jit(solution)/shard_map/all_to_all | solution.py:379
  245.5 2.4 factor5.1
  247.9 3.0 all-to-all-done.10
  251.0 8.3 %all_gather.23.refs_2_ = f32[1024,128]{1,0:T(8,128)S(1)} all-gather(f32[512,128]{1,0:T(8,128)S(1)} %bitcast.47), channel_id=1, replica_groups=mesh['zl'=4,'y'=4,'x'=4,'zh'=4,'core'=2] {'core'}, dimensions={0}, use_global_device_ids=true | all-gather | bytes 786432 | tf_op jit(solution)/shard_map/all_gather | solution.py:389
  259.2 1.9 half5.1
  261.1 17.2 %all_to_all.80.got_ref = f32[16,64,128]{2,1,0:T(8,128)S(1)} all-to-all(f32[16,64,128]{2,1,0:T(8,128)S(1)} %get-tuple-element.63), channel_id=1, replica_groups=mesh['zl'=4,'y'=4,'x'=4,'zh'=4,'core'=2] {'zl','y'}, dimensions={0} | all-to-all | bytes 1048576 | tf_op jit(solution)/shard_map/all_to_all | solution.py:379
  279.0 4.9 %all-to-all-start.12 = ((f32[16,48,128]{2,1,0:T(8,128)}), f32[16,48,128]{2,1,0:T(8,128)S(1)}, u32[]{:S(2)}, u32[]{:S(2)}) async-start(f32[16,48,128]{2,1,0:T(8,128)} %get-tuple-element.64), calls=%async_computation.12 | async-start | bytes 786432 | tf_op jit(solution)/shard_map/all_to_all | solution.py:379
  284.0 3.7 %collective-permute-start.2 = (f32[16,128]{1,0:T(8,128)S(1)}, f32[16,128]{1,0:T(8,128)S(1)}, u32[]{:S(2)}, u32[]{:S(2)}) collective-permute-start(f32[16,128]{1,0:T(8,128)S(1)} %get-tuple-element.65.refs_1_), channel_id=1, source_target_pairs={{0,1},{1,0},{2,3},{3,2},{4,5},{5,4},{6,7},{7,6},{8,9},{9,8},{10,11... | collective-permute-start | bytes 24584 | tf_op jit(solution)/shard_map/ppermute | solution.py:397
  288.5 2.9 factor6.1
  291.4 3.4 %all-to-all-done.12 = f32[16,48,128]{2,1,0:T(8,128)S(1)} async-done(((f32[16,48,128]{2,1,0:T(8,128)}), f32[16,48,128]{2,1,0:T(8,128)S(1)}, u32[]{:S(2)}, u32[]{:S(2)}) %all-to-all-start.12) | async-done | bytes 393248 | tf_op jit(solution)/shard_map/all_to_all | solution.py:379
  294.7 1.7 half6.1
  296.4 6.7 %all-to-all-start.13 = ((f32[8,24,128]{2,1,0:T(8,128)}), f32[8,24,128]{2,1,0:T(8,128)S(1)}, u32[]{:S(2)}, u32[]{:S(2)}) async-start(f32[8,24,128]{2,1,0:T(8,128)} %get-tuple-element.69), calls=%async_computation.13 | async-start | bytes 196608 | tf_op jit(solution)/shard_map/all_to_all | solution.py:379
  303.1 4.9 %all-to-all-done.13.got_ref = f32[8,24,128]{2,1,0:T(8,128)S(1)} async-done(((f32[8,24,128]{2,1,0:T(8,128)}), f32[8,24,128]{2,1,0:T(8,128)S(1)}, u32[]{:S(2)}, u32[]{:S(2)}) %all-to-all-start.13) | async-done | bytes 98336 | tf_op jit(solution)/shard_map/all_to_all | solution.py:379
  308.7 6.4 %all-to-all-start.14 = ((f32[4,24,128]{2,1,0:T(8,128)}), f32[4,24,128]{2,1,0:T(8,128)S(1)}, u32[]{:S(2)}, u32[]{:S(2)}) async-start(f32[4,24,128]{2,1,0:T(8,128)} %fold.19), calls=%async_computation.14 | async-start | bytes 98304 | tf_op jit(solution)/shard_map/all_to_all | solution.py:379
  316.2 10.5 %all-to-all-done.14.got_ref = f32[4,24,128]{2,1,0:T(8,128)S(1)} async-done(((f32[4,24,128]{2,1,0:T(8,128)}), f32[4,24,128]{2,1,0:T(8,128)S(1)}, u32[]{:S(2)}, u32[]{:S(2)}) %all-to-all-start.14) | async-done | bytes 49184 | tf_op jit(solution)/shard_map/all_to_all | solution.py:379
  326.7 2.6 end.1
  (33 shorter events, 10.3 us)
Async XLA Ops:
  0.6 22.4 %copy-start = (bf16[1,1,32,128,128]{4,3,2,1,0:T(8,128)(2,1)S(1)}, bf16[1,1,32,128,128]{4,3,2,1,0:T(8,128)(2,1)}, u32[]{:S(2)}) copy-start(bf16[1,1,32,128,128]{4,3,2,1,0:T(8,128)(2,1)} %param.6) | copy-start | bytes 3145732
  0.6 0.8 copy-start.1
  2.4 20.6 %all-to-all-start = ((f32[16,48,128]{2,1,0:T(8,128)}), f32[16,48,128]{2,1,0:T(8,128)S(1)}, u32[]{:S(2)}, u32[]{:S(2)}) async-start(f32[16,48,128]{2,1,0:T(8,128)} %pack.1), calls=%async_computation | async-start | bytes 786432 | tf_op jit(solution)/shard_map/all_to_all | solution.py:379
  11.6 1.4 copy-start.2
  12.3 0.7 copy-start.4
  65.7 3.5 %copy-start.3 = (s32[2048]{0:T(1024)S(1)}, s32[2048]{0:T(1024)}, u32[]{:S(2)}) copy-start(s32[2048]{0:T(1024)} %param.9) | copy-start | bytes 24580
  65.7 9.0 %all-to-all-start.2 = ((f32[4,128,128]{2,1,0:T(8,128)}), f32[4,128,128]{2,1,0:T(8,128)S(1)}, u32[]{:S(2)}, u32[]{:S(2)}) async-start(f32[4,128,128]{2,1,0:T(8,128)} %fold.11), calls=%async_computation.2 | async-start | bytes 524288 | tf_op jit(solution)/shard_map/all_to_all | solution.py:379
  102.3 15.7 %all-to-all-start.4 = ((f32[16,48,128]{2,1,0:T(8,128)}), f32[16,48,128]{2,1,0:T(8,128)S(1)}, u32[]{:S(2)}, u32[]{:S(2)}) async-start(f32[16,48,128]{2,1,0:T(8,128)} %get-tuple-element.44), calls=%async_computation.4 | async-start | bytes 786432 | tf_op jit(solution)/shard_map/all_to_all | solution.py:379
  107.3 4.5 %collective-permute-start = (f32[16,128]{1,0:T(8,128)S(1)}, f32[16,128]{1,0:T(8,128)S(1)}, u32[]{:S(2)}, u32[]{:S(2)}) collective-permute-start(f32[16,128]{1,0:T(8,128)S(1)} %get-tuple-element.45.refs_1_), channel_id=1, source_target_pairs={{0,1},{1,0},{2,3},{3,2},{4,5},{5,4},{6,7},{7,6},{8,9},{9,8},{10,11... | collective-permute-start | bytes 24584 | tf_op jit(solution)/shard_map/ppermute | solution.py:397
  153.8 8.9 %all-to-all-start.6 = ((f32[4,128,128]{2,1,0:T(8,128)}), f32[4,128,128]{2,1,0:T(8,128)S(1)}, u32[]{:S(2)}, u32[]{:S(2)}) async-start(f32[4,128,128]{2,1,0:T(8,128)} %fold.14), calls=%async_computation.6 | async-start | bytes 524288 | tf_op jit(solution)/shard_map/all_to_all | solution.py:379
  190.9 15.7 %all-to-all-start.8 = ((f32[16,48,128]{2,1,0:T(8,128)}), f32[16,48,128]{2,1,0:T(8,128)S(1)}, u32[]{:S(2)}, u32[]{:S(2)}) async-start(f32[16,48,128]{2,1,0:T(8,128)} %get-tuple-element.54), calls=%async_computation.8 | async-start | bytes 786432 | tf_op jit(solution)/shard_map/all_to_all | solution.py:379
  195.8 4.5 %collective-permute-start.1 = (f32[16,128]{1,0:T(8,128)S(1)}, f32[16,128]{1,0:T(8,128)S(1)}, u32[]{:S(2)}, u32[]{:S(2)}) collective-permute-start(f32[16,128]{1,0:T(8,128)S(1)} %get-tuple-element.55.refs_1_), channel_id=1, source_target_pairs={{0,1},{1,0},{2,3},{3,2},{4,5},{5,4},{6,7},{7,6},{8,9},{9,8},{10,11... | collective-permute-start | bytes 24584 | tf_op jit(solution)/shard_map/ppermute | solution.py:397
  242.1 8.9 %all-to-all-start.10 = ((f32[4,128,128]{2,1,0:T(8,128)}), f32[4,128,128]{2,1,0:T(8,128)S(1)}, u32[]{:S(2)}, u32[]{:S(2)}) async-start(f32[4,128,128]{2,1,0:T(8,128)} %fold.17), calls=%async_computation.10 | async-start | bytes 524288 | tf_op jit(solution)/shard_map/all_to_all | solution.py:379
  279.0 15.7 %all-to-all-start.12 = ((f32[16,48,128]{2,1,0:T(8,128)}), f32[16,48,128]{2,1,0:T(8,128)S(1)}, u32[]{:S(2)}, u32[]{:S(2)}) async-start(f32[16,48,128]{2,1,0:T(8,128)} %get-tuple-element.64), calls=%async_computation.12 | async-start | bytes 786432 | tf_op jit(solution)/shard_map/all_to_all | solution.py:379
  284.0 4.5 %collective-permute-start.2 = (f32[16,128]{1,0:T(8,128)S(1)}, f32[16,128]{1,0:T(8,128)S(1)}, u32[]{:S(2)}, u32[]{:S(2)}) collective-permute-start(f32[16,128]{1,0:T(8,128)S(1)} %get-tuple-element.65.refs_1_), channel_id=1, source_target_pairs={{0,1},{1,0},{2,3},{3,2},{4,5},{5,4},{6,7},{7,6},{8,9},{9,8},{10,11... | collective-permute-start | bytes 24584 | tf_op jit(solution)/shard_map/ppermute | solution.py:397
  296.4 11.7 %all-to-all-start.13 = ((f32[8,24,128]{2,1,0:T(8,128)}), f32[8,24,128]{2,1,0:T(8,128)S(1)}, u32[]{:S(2)}, u32[]{:S(2)}) async-start(f32[8,24,128]{2,1,0:T(8,128)} %get-tuple-element.69), calls=%async_computation.13 | async-start | bytes 196608 | tf_op jit(solution)/shard_map/all_to_all | solution.py:379
  308.7 18.0 %all-to-all-start.14 = ((f32[4,24,128]{2,1,0:T(8,128)}), f32[4,24,128]{2,1,0:T(8,128)S(1)}, u32[]{:S(2)}, u32[]{:S(2)}) async-start(f32[4,24,128]{2,1,0:T(8,128)} %fold.19), calls=%async_computation.14 | async-start | bytes 98304 | tf_op jit(solution)/shard_map/all_to_all | solution.py:379

commit v6 on v5

--- a/solution.py
+++ b/solution.py
@@ -253,7 +253,7 @@
 
 
 def join_gram(table_ref, own_ref, other_ref):
-    first = table_ref[table_ref.shape[0] - 1] == 0
+    first = table_ref[table_ref.shape[0] - 2] == 0
     own, other = own_ref[...], other_ref[...]
     return unpack_gram(
         jnp.concatenate(
@@ -274,7 +274,7 @@
     return jnp.where(mask, lower, 0.0)
 
 
-def factor_kernel(*refs, with_old, halves):
+def factor_kernel(*refs, with_old, halves, left_size=None):
     refs = list(refs)
     if halves:
         gram, refs = join_gram(*refs[:3]), refs[3:]
@@ -283,9 +283,21 @@
     if not with_old:
         factor_rows(gram, refs[0])
         return
-    old_ref, old_factor_ref, factor_ref, part_ref, lower_ref = refs
-    factor_rows(gram, factor_ref)
-    lower_ref[...] = lower_factor(factor_ref)
+    old_ref, old_factor_ref = refs[:2]
+    if left_size is None:
+        factor_ref, part_ref, lower_ref = refs[2:]
+        factor_rows(gram, factor_ref)
+        lower_ref[...] = lower_factor(factor_ref)
+    else:
+        left_ref, first_ref, second_ref, factor_ref, part_ref, lower_ref, out_ref = refs[2:]
+        factor_rows(gram, factor_ref)
+        lower_ref[0] = first_ref[...]
+        lower_ref[1] = second_ref[...]
+        lower_ref[2] = lower_factor(factor_ref)
+        out_ref[...] = math.sqrt(left_size) * jnp.dot(
+            factor_ref[:, BLOCK:], left_ref[...], precision=HIGH,
+            preferred_element_type=jnp.float32,
+        )
     upper_mask = lax.broadcasted_iota(
         jnp.int32, (BLOCK, BLOCK), 0
     ) <= lax.broadcasted_iota(jnp.int32, (BLOCK, BLOCK), 1)
@@ -335,20 +347,30 @@
 
 
 def end_kernel(
-    got_ref, right_ref, left_ref, left_factor_ref, first_ref, second_ref,
-    out_right_ref, out_left_ref, lower_ref, factor_ref, *, left_size, right_size,
+    table_ref, got_ref, panel_ref, first_ref, second_ref, out_ref, lower_ref, factor_ref, *, right_size
 ):
     lower_ref[0] = first_ref[...]
     lower_ref[1] = second_ref[...]
     factor_rows(sum_gram(got_ref), factor_ref)
     lower_ref[2] = lower_factor(factor_ref)
-    out_right_ref[...] = math.sqrt(right_size) * jnp.dot(
-        factor_ref[:, BLOCK:], right_ref[...], precision=HIGH,
-        preferred_element_type=jnp.float32,
-    )
-    out_left_ref[...] = math.sqrt(left_size) * jnp.dot(
-        left_factor_ref[:, BLOCK:], left_ref[...], precision=HIGH,
-        preferred_element_type=jnp.float32,
+    width = out_ref.shape[1]
+    unit = (width // UNIT) * table_ref[table_ref.shape[0] - 1]
+    block = unit // (TILE // UNIT)
+    after = jnp.minimum(block + 1, panel_ref.shape[0] // BLOCK - 1)
+    wide = jnp.concatenate(
+        [
+            panel_ref[pl.ds(pl.multiple_of(BLOCK * b, BLOCK), BLOCK), :]
+            for b in (block, after)
+        ],
+        axis=1,
+    )
+    own = wide[:, :width]
+    for k in range(1, TILE // UNIT):
+        own = jnp.where(
+            unit % (TILE // UNIT) == k, wide[:, UNIT * k : UNIT * k + width], own
+        )
+    out_ref[...] = math.sqrt(right_size) * jnp.dot(
+        factor_ref[:, BLOCK:], own, precision=HIGH, preferred_element_type=jnp.float32
     )
 
 
@@ -398,15 +420,22 @@
     return [table, own, other], whole
 
 
+def left_chunk(panel, blocks):
+    group = blocks * TILE // lax.axis_size(COL)
+    flat = jnp.transpose(panel.reshape(blocks, BLOCK, TILE), (1, 0, 2))
+    flat = flat.reshape(BLOCK, blocks * TILE)
+    return lax.dynamic_slice_in_dim(flat, lax.axis_index(COL) * group, group, 1)
+
+
 def per_device(tiles, tile_slots, tile_counts, user_degree, item_degree, start_panel):
     tile_stack = tiles[0, 0]
     rb = user_degree.shape[0] // TILE
     cb = item_degree.shape[0] // TILE
     rows = lax.axis_size(ROW)
-    cols = lax.axis_size(COL)
     near = lax.axis_size(NEAR)
     core = lax.axis_index("core").astype(jnp.int32).reshape(1)
-    table = jnp.concatenate([tile_slots[0, 0], tile_counts[0], core])
+    row = lax.axis_index(ROW).astype(jnp.int32).reshape(1)
+    table = jnp.concatenate([tile_slots[0, 0], tile_counts[0], core, row])
     user_scale = lax.rsqrt(user_degree.astype(jnp.float32)).reshape(rb, TILE)
     item_scale = lax.rsqrt(item_degree.astype(jnp.float32)).reshape(cb, TILE)
 
@@ -452,17 +481,29 @@
         gram, whole = sum_col(sent) if users else sum_row(sent, table)
         panel_shape = f32((rb if users else cb) * BLOCK, TILE)
         old = [panels[half - 2], factors[half - 2]] if with_old else []
+        finished = [left_chunk(panels[-1], rb), lower[0], lower[2]] if last else []
+        shapes = [f32(BLOCK, 2 * BLOCK)]
+        if with_old:
+            shapes += [panel_shape, f32(*([STEPS] if last else []), BLOCK, BLOCK)]
+        if last:
+            shapes.append(f32(BLOCK, finished[0].shape[1]))
         factored = pl.pallas_call(
-            functools.partial(factor_kernel, with_old=with_old, halves=not users),
-            out_shape=[f32(BLOCK, 2 * BLOCK)]
-            + ([panel_shape, f32(BLOCK, BLOCK)] if with_old else []),
-            in_specs=([VMEM] if users else [SMEM, VMEM, VMEM]) + [VMEM] * len(old),
-            out_specs=[VMEM] * (3 if with_old else 1),
+            functools.partial(
+                factor_kernel, with_old=with_old, halves=not users,
+                left_size=rb * TILE * rows if last else None,
+            ),
+            out_shape=shapes,
+            in_specs=([VMEM] if users else [SMEM, VMEM, VMEM])
+            + [VMEM] * len(old + finished),
+            out_specs=[VMEM] * len(shapes),
             compiler_params=PARAMS,
             name=f"factor{half}",
-        )(*gram, *old)
+        )(*gram, *old, *finished)
         factors.append(factored[0])
-        lower += factored[2:]
+        if last:
+            left_factors, left_panel = factored[2:]
+        else:
+            lower += factored[2:]
         tables = [] if last else [table, tile_stack]
         table_specs = [] if last else [SMEM, VMEM]
         operands = [whole, user_scale if users else item_scale, *factored[:2]]
@@ -486,35 +527,19 @@
         )(*tables, *operands)
         panels.append(panel)
 
-    gram = fold(exchange(sent, NEAR), lax.axis_size("zh"), GRAM_ROWS)[0]
-    gram = exchange(gram, "zh")
-
-    user_group = rb * TILE // cols
-    item_group = cb * TILE // rows
-    left = jnp.transpose(panels[-2].reshape(rb, BLOCK, TILE), (1, 0, 2))
-    left = lax.dynamic_slice_in_dim(
-        left.reshape(BLOCK, rb * TILE), lax.axis_index(COL) * user_group, user_group, 1
-    )
-    right = jnp.transpose(panels[-1].reshape(cb, BLOCK, TILE), (1, 0, 2))
-    right = lax.dynamic_slice_in_dim(
-        right.reshape(BLOCK, cb * TILE), lax.axis_index(ROW) * item_group, item_group, 1
-    )
-    right_panel, left_panel, right_factors = pl.pallas_call(
-        functools.partial(
-            end_kernel, left_size=rb * TILE * rows, right_size=cb * TILE * cols
-        ),
-        out_shape=[
-            f32(BLOCK, item_group),
-            f32(BLOCK, user_group),
-            f32(STEPS, BLOCK, BLOCK),
-        ],
-        in_specs=[VMEM] * 6,
-        out_specs=[VMEM] * 3,
+    gram = fold(exchange(sent, NEAR), 1, GRAM_ROWS)[0][0]
+    gram = lax.all_gather(gram, "zh", axis=0, tiled=False)
+
+    right_panel, right_factors = pl.pallas_call(
+        functools.partial(end_kernel, right_size=cb * TILE * lax.axis_size(COL)),
+        out_shape=[f32(BLOCK, cb * TILE // rows), f32(STEPS, BLOCK, BLOCK)],
+        in_specs=[SMEM] + [VMEM] * 4,
+        out_specs=[VMEM] * 2,
         scratch_shapes=[pltpu.VMEM((BLOCK, 2 * BLOCK), jnp.float32)],
         compiler_params=PARAMS,
         name="end",
-    )(gram, right, left, factors[-1], lower[1], lower[3])
-    return left_panel, right_panel, jnp.stack(lower[::2]), right_factors
+    )(table, gram, panels[-1], lower[1], lower[3])
+    return left_panel, right_panel, left_factors, right_factors
 
 
 def solution(mesh):

time: 331 us -> 327 us (0.988)
  blocking collectives: 182 us -> 207 us
  waiting for transfers between devices: 47.1 us -> 31 us
  starting transfers between devices: 58.6 us -> 45.6 us
    all_to_all x9 -> x7, waiting for transfers between devices: 45.3 us -> 28.8 us  [exchange(): return lax.all_to_all(messages, axes, 0, 0, tiled=True)]
    all_gather x0 -> x1, blocking collectives: none -> 14.5 us  [per_device(): gram = lax.all_gather(gram, 'zh', axis=0, tiled=False)]
    all_to_all x9 -> x7, starting transfers between devices: 47.4 us -> 34.4 us  [exchange(): return lax.all_to_all(messages, axes, 0, 0, tiled=True)]
    all_to_all x6 -> x7, blocking collectives: 103 us -> 113 us  [exchange(): return lax.all_to_all(messages, axes, 0, 0, tiled=True)]
  transfers between devices with their start and end apart: 12 -> 10, of which waited for: 12 -> 10; matrix products, arithmetic and copies ran while one was open for 1% -> 0% of each run, Pallas kernels for 5% -> 5%
where the time goes in v6:
time: 327 us; the launch traced here: 324 us
  blocking collectives  207 us (63%)
  starting transfers between devices  45.6 us (14%)
  Pallas kernels  36.7 us (11%)
  waiting for transfers between devices  31 us (9%)
    all_to_all x7, blocking collectives, exchange(): return lax.all_to_all(messages, axes, 0, 0, tiled=True)  113 us
    all_gather x3, blocking collectives, sum_col(): got = lax.all_gather(own, 'zh', axis=0, tiled=False)  56.6 us
    all_to_all x7, starting transfers between devices, exchange(): return lax.all_to_all(messages, axes, 0, 0, tiled=True)  34.4 us
    all_to_all x7, waiting for transfers between devices, exchange(): return lax.all_to_all(messages, axes, 0, 0, tiled=True)  28.8 us
    all_gather x3, blocking collectives, sum_col(): return ([got], lax.all_gather(half, 'core', axis=0, tiled=True))  23 us
    pallas_call x6, Pallas kernels, per_device(): pl.pallas_call(functools.partial(factor_kernel, with_old=with_old, halves...  15.8 us
    all_gather x1, blocking collectives, per_device(): gram = lax.all_gather(gram, 'zh', axis=0, tiled=False)  14.5 us
    ppermute x3, starting transfers between devices, sum_row(): other = lax.ppermute(own, 'core', [(0, 1), (1, 0)])  11.3 us
  transfers between devices with their start and end apart: 10, of which 10 were waited for; matrix products, arithmetic and copies ran while one was open for 0% of the time, Pallas kernels for 5%

profile of v6, /device:TPU:1, one launch (start us, length us, event | category | flops | bytes accessed | tf_op | source)
XLA Modules:
  0.0 324.2 jit_solution(7722137988136426617)
XLA Ops:
  0.7 0.8 copy-done.1
  1.5 0.9 pack.1
  2.4 9.2 %all-to-all-start = ((f32[16,48,128]{2,1,0:T(8,128)}), f32[16,48,128]{2,1,0:T(8,128)S(1)}, u32[]{:S(2)}, u32[]{:S(2)}) async-start(f32[16,48,128]{2,1,0:T(8,128)} %pack.1), calls=%async_computation | async-start | bytes 786432 | tf_op jit(solution)/shard_map/all_to_all | solution.py:401
  13.0 10.0 %all-to-all-done.got_ref = f32[16,48,128]{2,1,0:T(8,128)S(1)} async-done(((f32[16,48,128]{2,1,0:T(8,128)}), f32[16,48,128]{2,1,0:T(8,128)S(1)}, u32[]{:S(2)}, u32[]{:S(2)}) %all-to-all-start) | async-done | bytes 393248 | tf_op jit(solution)/shard_map/all_to_all | solution.py:401
  23.0 1.7 start.1
  24.7 17.5 %all_to_all.70.got_ref = f32[8,152,128]{2,1,0:T(8,128)S(1)} all-to-all(f32[8,152,128]{2,1,0:T(8,128)S(1)} %get-tuple-element.42), channel_id=1, replica_groups=mesh['zl'=4,'y'=4,'x'=4,'zh'=4,'core'=2] {'core','x'}, dimensions={0} | all-to-all | bytes 1245184 | tf_op jit(solution)/shard_map/all_to_all | solution.py:401
  42.2 23.1 %all_gather.21.got_ref.refs_0_ = f32[4,152,128]{2,1,0:T(8,128)S(1)} all-gather(f32[1,152,128]{2,1,0:T(8,128)S(1)} %fold.10), channel_id=1, replica_groups=mesh['zl'=4,'y'=4,'x'=4,'zh'=4,'core'=2] {'zh'}, dimensions={0}, use_global_device_ids=true | all-gather | bytes 389120 | tf_op jit(solution)/shard_map/all_gather | solution.py:407
  66.0 3.5 %all-to-all-start.2 = ((f32[4,128,128]{2,1,0:T(8,128)}), f32[4,128,128]{2,1,0:T(8,128)S(1)}, u32[]{:S(2)}, u32[]{:S(2)}) async-start(f32[4,128,128]{2,1,0:T(8,128)} %fold.11), calls=%async_computation.2 | async-start | bytes 524288 | tf_op jit(solution)/shard_map/all_to_all | solution.py:401
  69.6 1.7 factor1.1.refs_4_
  71.3 3.7 %all-to-all-done.2 = f32[4,128,128]{2,1,0:T(8,128)S(1)} async-done(((f32[4,128,128]{2,1,0:T(8,128)}), f32[4,128,128]{2,1,0:T(8,128)S(1)}, u32[]{:S(2)}, u32[]{:S(2)}) %all-to-all-start.2) | async-done | bytes 262176 | tf_op jit(solution)/shard_map/all_to_all | solution.py:401
  75.1 7.3 %all_gather.22.refs_2_ = f32[1024,128]{1,0:T(8,128)S(1)} all-gather(f32[512,128]{1,0:T(8,128)S(1)} %bitcast.35), channel_id=1, replica_groups=mesh['zl'=4,'y'=4,'x'=4,'zh'=4,'core'=2] {'core'}, dimensions={0}, use_global_device_ids=true | all-gather | bytes 786432 | tf_op jit(solution)/shard_map/all_gather | solution.py:411
  82.4 1.9 half1.1
  84.3 17.2 %all_to_all.71.got_ref = f32[16,64,128]{2,1,0:T(8,128)S(1)} all-to-all(f32[16,64,128]{2,1,0:T(8,128)S(1)} %get-tuple-element.43), channel_id=1, replica_groups=mesh['zl'=4,'y'=4,'x'=4,'zh'=4,'core'=2] {'zl','y'}, dimensions={0} | all-to-all | bytes 1048576 | tf_op jit(solution)/shard_map/all_to_all | solution.py:401
  102.3 4.9 %all-to-all-start.4 = ((f32[16,48,128]{2,1,0:T(8,128)}), f32[16,48,128]{2,1,0:T(8,128)S(1)}, u32[]{:S(2)}, u32[]{:S(2)}) async-start(f32[16,48,128]{2,1,0:T(8,128)} %get-tuple-element.44), calls=%async_computation.4 | async-start | bytes 786432 | tf_op jit(solution)/shard_map/all_to_all | solution.py:401
  107.3 3.7 %collective-permute-start = (f32[16,128]{1,0:T(8,128)S(1)}, f32[16,128]{1,0:T(8,128)S(1)}, u32[]{:S(2)}, u32[]{:S(2)}) collective-permute-start(f32[16,128]{1,0:T(8,128)S(1)} %get-tuple-element.45.refs_1_), channel_id=1, source_target_pairs={{0,1},{1,0},{2,3},{3,2},{4,5},{5,4},{6,7},{7,6},{8,9},{9,8},{10,11... | collective-permute-start | bytes 24584 | tf_op jit(solution)/shard_map/ppermute | solution.py:419
  111.0 0.8 collective-permute-done.refs_2_
  111.8 2.9 factor2.1
  114.7 3.3 %all-to-all-done.4 = f32[16,48,128]{2,1,0:T(8,128)S(1)} async-done(((f32[16,48,128]{2,1,0:T(8,128)}), f32[16,48,128]{2,1,0:T(8,128)S(1)}, u32[]{:S(2)}, u32[]{:S(2)}) %all-to-all-start.4) | async-done | bytes 393248 | tf_op jit(solution)/shard_map/all_to_all | solution.py:401
  118.0 1.9 half2.1
  119.9 16.4 %all_to_all.72.got_ref = f32[8,152,128]{2,1,0:T(8,128)S(1)} all-to-all(f32[8,152,128]{2,1,0:T(8,128)S(1)} %get-tuple-element.49), channel_id=1, replica_groups=mesh['zl'=4,'y'=4,'x'=4,'zh'=4,'core'=2] {'core','x'}, dimensions={0} | all-to-all | bytes 1245184 | tf_op jit(solution)/shard_map/all_to_all | solution.py:401
  136.3 16.8 %all_gather.23.got_ref.refs_0_ = f32[4,152,128]{2,1,0:T(8,128)S(1)} all-gather(f32[1,152,128]{2,1,0:T(8,128)S(1)} %fold.13), channel_id=1, replica_groups=mesh['zl'=4,'y'=4,'x'=4,'zh'=4,'core'=2] {'zh'}, dimensions={0}, use_global_device_ids=true | all-gather | bytes 389120 | tf_op jit(solution)/shard_map/all_gather | solution.py:407
  153.8 3.4 %all-to-all-start.6 = ((f32[4,128,128]{2,1,0:T(8,128)}), f32[4,128,128]{2,1,0:T(8,128)S(1)}, u32[]{:S(2)}, u32[]{:S(2)}) async-start(f32[4,128,128]{2,1,0:T(8,128)} %fold.14), calls=%async_computation.6 | async-start | bytes 524288 | tf_op jit(solution)/shard_map/all_to_all | solution.py:401
  157.2 2.4 factor3.1
  159.7 3.0 all-to-all-done.6
  162.7 7.7 %all_gather.24.refs_2_ = f32[1024,128]{1,0:T(8,128)S(1)} all-gather(f32[512,128]{1,0:T(8,128)S(1)} %bitcast.33), channel_id=1, replica_groups=mesh['zl'=4,'y'=4,'x'=4,'zh'=4,'core'=2] {'core'}, dimensions={0}, use_global_device_ids=true | all-gather | bytes 786432 | tf_op jit(solution)/shard_map/all_gather | solution.py:411
  170.4 1.9 half3.1
  172.3 17.8 %all_to_all.73.got_ref = f32[16,64,128]{2,1,0:T(8,128)S(1)} all-to-all(f32[16,64,128]{2,1,0:T(8,128)S(1)} %get-tuple-element.53), channel_id=1, replica_groups=mesh['zl'=4,'y'=4,'x'=4,'zh'=4,'core'=2] {'zl','y'}, dimensions={0} | all-to-all | bytes 1048576 | tf_op jit(solution)/shard_map/all_to_all | solution.py:401
  190.9 4.9 %all-to-all-start.8 = ((f32[16,48,128]{2,1,0:T(8,128)}), f32[16,48,128]{2,1,0:T(8,128)S(1)}, u32[]{:S(2)}, u32[]{:S(2)}) async-start(f32[16,48,128]{2,1,0:T(8,128)} %get-tuple-element.54), calls=%async_computation.8 | async-start | bytes 786432 | tf_op jit(solution)/shard_map/all_to_all | solution.py:401
  195.8 3.9 %collective-permute-start.1 = (f32[16,128]{1,0:T(8,128)S(1)}, f32[16,128]{1,0:T(8,128)S(1)}, u32[]{:S(2)}, u32[]{:S(2)}) collective-permute-start(f32[16,128]{1,0:T(8,128)S(1)} %get-tuple-element.55.refs_1_), channel_id=1, source_target_pairs={{0,1},{1,0},{2,3},{3,2},{4,5},{5,4},{6,7},{7,6},{8,9},{9,8},{10,11... | collective-permute-start | bytes 24584 | tf_op jit(solution)/shard_map/ppermute | solution.py:419
  200.3 2.9 factor4.1
  203.2 3.3 %all-to-all-done.8 = f32[16,48,128]{2,1,0:T(8,128)S(1)} async-done(((f32[16,48,128]{2,1,0:T(8,128)}), f32[16,48,128]{2,1,0:T(8,128)S(1)}, u32[]{:S(2)}, u32[]{:S(2)}) %all-to-all-start.8) | async-done | bytes 393248 | tf_op jit(solution)/shard_map/all_to_all | solution.py:401
  206.5 1.9 half4.1
  208.4 16.4 %all_to_all.74.got_ref = f32[8,152,128]{2,1,0:T(8,128)S(1)} all-to-all(f32[8,152,128]{2,1,0:T(8,128)S(1)} %get-tuple-element.59), channel_id=1, replica_groups=mesh['zl'=4,'y'=4,'x'=4,'zh'=4,'core'=2] {'core','x'}, dimensions={0} | all-to-all | bytes 1245184 | tf_op jit(solution)/shard_map/all_to_all | solution.py:401
  224.9 16.7 %all_gather.25.got_ref.refs_0_ = f32[4,152,128]{2,1,0:T(8,128)S(1)} all-gather(f32[1,152,128]{2,1,0:T(8,128)S(1)} %fold.16), channel_id=1, replica_groups=mesh['zl'=4,'y'=4,'x'=4,'zh'=4,'core'=2] {'zh'}, dimensions={0}, use_global_device_ids=true | all-gather | bytes 389120 | tf_op jit(solution)/shard_map/all_gather | solution.py:407
  242.3 3.4 %all-to-all-start.10 = ((f32[4,128,128]{2,1,0:T(8,128)}), f32[4,128,128]{2,1,0:T(8,128)S(1)}, u32[]{:S(2)}, u32[]{:S(2)}) async-start(f32[4,128,128]{2,1,0:T(8,128)} %fold.17), calls=%async_computation.10 | async-start | bytes 524288 | tf_op jit(solution)/shard_map/all_to_all | solution.py:401
  245.7 2.4 factor5.1
  248.1 3.0 all-to-all-done.10
  251.2 8.0 %all_gather.26.refs_2_ = f32[1024,128]{1,0:T(8,128)S(1)} all-gather(f32[512,128]{1,0:T(8,128)S(1)} %bitcast.34), channel_id=1, replica_groups=mesh['zl'=4,'y'=4,'x'=4,'zh'=4,'core'=2] {'core'}, dimensions={0}, use_global_device_ids=true | all-gather | bytes 786432 | tf_op jit(solution)/shard_map/all_gather | solution.py:411
  259.1 1.9 half5.1
  261.0 17.2 %all_to_all.75.got_ref = f32[16,64,128]{2,1,0:T(8,128)S(1)} all-to-all(f32[16,64,128]{2,1,0:T(8,128)S(1)} %get-tuple-element.63), channel_id=1, replica_groups=mesh['zl'=4,'y'=4,'x'=4,'zh'=4,'core'=2] {'zl','y'}, dimensions={0} | all-to-all | bytes 1048576 | tf_op jit(solution)/shard_map/all_to_all | solution.py:401
  279.0 4.9 %all-to-all-start.12 = ((f32[16,48,128]{2,1,0:T(8,128)}), f32[16,48,128]{2,1,0:T(8,128)S(1)}, u32[]{:S(2)}, u32[]{:S(2)}) async-start(f32[16,48,128]{2,1,0:T(8,128)} %get-tuple-element.70), calls=%async_computation.12 | async-start | bytes 786432 | tf_op jit(solution)/shard_map/all_to_all | solution.py:401
  284.5 3.7 %collective-permute-start.2 = (f32[16,128]{1,0:T(8,128)S(1)}, f32[16,128]{1,0:T(8,128)S(1)}, u32[]{:S(2)}, u32[]{:S(2)}) collective-permute-start(f32[16,128]{1,0:T(8,128)S(1)} %get-tuple-element.64.refs_1_), channel_id=1, source_target_pairs={{0,1},{1,0},{2,3},{3,2},{4,5},{5,4},{6,7},{7,6},{8,9},{9,8},{10,11... | collective-permute-start | bytes 24584 | tf_op jit(solution)/shard_map/ppermute | solution.py:419
  289.0 3.4 %factor6.1 = (f32[64,128]{1,0:T(8,128)S(1)}, f32[768,128]{1,0:T(8,128)S(1)}, f32[3,64,64]{2,1,0:T(8,128)}, f32[64,64]{1,0:T(8,128)}) custom-call(s32[35]{0:T(128)S(1)} %pad_add_fusion.table_ref.refs_0_, f32[16,128]{1,0:T(8,128)S(1)} %get-tuple-element.64.refs_1_, f32[16,128]{1,0:T(8,128)S(1)} %collective-permute-done.2.refs_2_, ...), custom_call_target="tpu_custom_call" | custom-call | tf_op jit(solution)/shard_map/factor6/pallas_call | solution.py:490
  292.4 2.3 all-to-all-done.12
  294.7 1.0 half6.1
  295.8 10.8 %all_to_all.76.got_ref = f32[8,24,128]{2,1,0:T(8,128)S(1)} all-to-all(f32[8,24,128]{2,1,0:T(8,128)S(1)} %get-tuple-element.73), channel_id=1, replica_groups=mesh['zl'=4,'y'=4,'x'=4,'zh'=4,'core'=2] {'core','x'}, dimensions={0} | all-to-all | bytes 196608 | tf_op jit(solution)/shard_map/all_to_all | solution.py:401
  306.5 14.5 %all_gather.27.got_ref = f32[4,24,128]{2,1,0:T(8,128)S(1)} all-gather(f32[1,24,128]{2,1,0:T(8,128)S(1)} %fold.19), channel_id=1, replica_groups=mesh['zl'=4,'y'=4,'x'=4,'zh'=4,'core'=2] {'zh'}, dimensions={0}, use_global_device_ids=true | all-gather | bytes 61440 | tf_op jit(solution)/shard_map/all_gather | solution.py:531
  321.0 3.2 end.1
  (27 shorter events, 7.3 us)
Async XLA Ops:
  0.6 22.4 %copy-start = (bf16[1,1,32,128,128]{4,3,2,1,0:T(8,128)(2,1)S(1)}, bf16[1,1,32,128,128]{4,3,2,1,0:T(8,128)(2,1)}, u32[]{:S(2)}) copy-start(bf16[1,1,32,128,128]{4,3,2,1,0:T(8,128)(2,1)} %param.6) | copy-start | bytes 3145732
  0.6 0.8 copy-start.1
  2.4 20.6 %all-to-all-start = ((f32[16,48,128]{2,1,0:T(8,128)}), f32[16,48,128]{2,1,0:T(8,128)S(1)}, u32[]{:S(2)}, u32[]{:S(2)}) async-start(f32[16,48,128]{2,1,0:T(8,128)} %pack.1), calls=%async_computation | async-start | bytes 786432 | tf_op jit(solution)/shard_map/all_to_all | solution.py:401
  11.6 1.4 copy-start.2
  12.3 0.7 copy-start.4
  66.0 3.5 %copy-start.3 = (s32[2048]{0:T(1024)S(1)}, s32[2048]{0:T(1024)}, u32[]{:S(2)}) copy-start(s32[2048]{0:T(1024)} %param.9) | copy-start | bytes 24580
  66.0 9.0 %all-to-all-start.2 = ((f32[4,128,128]{2,1,0:T(8,128)}), f32[4,128,128]{2,1,0:T(8,128)S(1)}, u32[]{:S(2)}, u32[]{:S(2)}) async-start(f32[4,128,128]{2,1,0:T(8,128)} %fold.11), calls=%async_computation.2 | async-start | bytes 524288 | tf_op jit(solution)/shard_map/all_to_all | solution.py:401
  102.3 15.7 %all-to-all-start.4 = ((f32[16,48,128]{2,1,0:T(8,128)}), f32[16,48,128]{2,1,0:T(8,128)S(1)}, u32[]{:S(2)}, u32[]{:S(2)}) async-start(f32[16,48,128]{2,1,0:T(8,128)} %get-tuple-element.44), calls=%async_computation.4 | async-start | bytes 786432 | tf_op jit(solution)/shard_map/all_to_all | solution.py:401
  107.3 4.5 %collective-permute-start = (f32[16,128]{1,0:T(8,128)S(1)}, f32[16,128]{1,0:T(8,128)S(1)}, u32[]{:S(2)}, u32[]{:S(2)}) collective-permute-start(f32[16,128]{1,0:T(8,128)S(1)} %get-tuple-element.45.refs_1_), channel_id=1, source_target_pairs={{0,1},{1,0},{2,3},{3,2},{4,5},{5,4},{6,7},{7,6},{8,9},{9,8},{10,11... | collective-permute-start | bytes 24584 | tf_op jit(solution)/shard_map/ppermute | solution.py:419
  153.8 8.9 %all-to-all-start.6 = ((f32[4,128,128]{2,1,0:T(8,128)}), f32[4,128,128]{2,1,0:T(8,128)S(1)}, u32[]{:S(2)}, u32[]{:S(2)}) async-start(f32[4,128,128]{2,1,0:T(8,128)} %fold.14), calls=%async_computation.6 | async-start | bytes 524288 | tf_op jit(solution)/shard_map/all_to_all | solution.py:401
  190.9 15.7 %all-to-all-start.8 = ((f32[16,48,128]{2,1,0:T(8,128)}), f32[16,48,128]{2,1,0:T(8,128)S(1)}, u32[]{:S(2)}, u32[]{:S(2)}) async-start(f32[16,48,128]{2,1,0:T(8,128)} %get-tuple-element.54), calls=%async_computation.8 | async-start | bytes 786432 | tf_op jit(solution)/shard_map/all_to_all | solution.py:401
  195.8 4.5 %collective-permute-start.1 = (f32[16,128]{1,0:T(8,128)S(1)}, f32[16,128]{1,0:T(8,128)S(1)}, u32[]{:S(2)}, u32[]{:S(2)}) collective-permute-start(f32[16,128]{1,0:T(8,128)S(1)} %get-tuple-element.55.refs_1_), channel_id=1, source_target_pairs={{0,1},{1,0},{2,3},{3,2},{4,5},{5,4},{6,7},{7,6},{8,9},{9,8},{10,11... | collective-permute-start | bytes 24584 | tf_op jit(solution)/shard_map/ppermute | solution.py:419
  242.3 8.9 %all-to-all-start.10 = ((f32[4,128,128]{2,1,0:T(8,128)}), f32[4,128,128]{2,1,0:T(8,128)S(1)}, u32[]{:S(2)}, u32[]{:S(2)}) async-start(f32[4,128,128]{2,1,0:T(8,128)} %fold.17), calls=%async_computation.10 | async-start | bytes 524288 | tf_op jit(solution)/shard_map/all_to_all | solution.py:401
  279.0 15.7 %all-to-all-start.12 = ((f32[16,48,128]{2,1,0:T(8,128)}), f32[16,48,128]{2,1,0:T(8,128)S(1)}, u32[]{:S(2)}, u32[]{:S(2)}) async-start(f32[16,48,128]{2,1,0:T(8,128)} %get-tuple-element.70), calls=%async_computation.12 | async-start | bytes 786432 | tf_op jit(solution)/shard_map/all_to_all | solution.py:401
  284.5 4.5 %collective-permute-start.2 = (f32[16,128]{1,0:T(8,128)S(1)}, f32[16,128]{1,0:T(8,128)S(1)}, u32[]{:S(2)}, u32[]{:S(2)}) collective-permute-start(f32[16,128]{1,0:T(8,128)S(1)} %get-tuple-element.64.refs_1_), channel_id=1, source_target_pairs={{0,1},{1,0},{2,3},{3,2},{4,5},{5,4},{6,7},{7,6},{8,9},{9,8},{10,11... | collective-permute-start | bytes 24584 | tf_op jit(solution)/shard_map/ppermute | solution.py:419

commit v7 on v5

--- a/solution.py
+++ b/solution.py
@@ -20,6 +20,8 @@
 ROW = ("zl", "y")
 COL = ("x", "zh", "core")
 NEAR = ("core", "x")
+FLAT = ("core", "y", "x")
+LINE = ("zh", "zl")
 
 
 def pack_gram(gram):
@@ -158,7 +160,8 @@
 
 
 def send_panel(
-    table_ref, tiles_ref, panel_ref, scale_ref, sent_ref, parts_ref, sums_ref, *, forward, cb, ready=None
+    table_ref, tiles_ref, panel_ref, scale_ref, sent_ref, parts_ref, sums_ref, *, forward, cb, ready=None,
+    owned=False,
 ):
     sums_ref[...] = jnp.zeros_like(sums_ref)
     gram = no_gram()
@@ -172,7 +175,7 @@
         ready.wait()
     product(table_ref, tiles_ref, parts_ref, sums_ref, forward, cb)
     packed = pack_gram(whole_gram(gram))
-    if not forward:
+    if not (forward or owned):
         cross = packed[HALF_ROWS:]
         packed = jnp.where(
             table_ref[tiles_ref.shape[0] + 1] == 0, packed[:HALF_ROWS], jnp.concatenate([cross, cross], axis=0)
@@ -180,7 +183,20 @@
     count = sent_ref.shape[0]
     rows = (sums_ref.shape[0] - BLOCK) // count
     for k in range(count):
-        sent_ref[k, :rows, :] = sums_ref[rows * k : rows * k + rows, :]
+        if owned:
+            per_block = TILE // UNIT
+            units = rows * per_block // BLOCK
+            sent_ref[k, :rows, :] = pack_units(
+                [
+                    sums_ref[
+                        BLOCK * (u // per_block) : BLOCK * (u // per_block) + BLOCK,
+                        UNIT * (u % per_block) : UNIT * (u % per_block) + UNIT,
+                    ]
+                    for u in range(units * k, units * k + units)
+                ]
+            )
+        else:
+            sent_ref[k, :rows, :] = sums_ref[rows * k : rows * k + rows, :]
         sent_ref[k, rows:, :] = packed
 
 
@@ -190,15 +206,35 @@
         yield at % rows, UNIT * (at // rows)
 
 
-def pack_kernel(panel_ref, out_ref):
-    rows = out_ref.shape[1]
+def pack_units(units):
+    rows = len(units) * BLOCK * UNIT // TILE
     columns = [[] for _ in range(TILE // UNIT)]
-    for unit in range(panel_ref.shape[1] // UNIT):
-        value = panel_ref[:, UNIT * unit : UNIT * unit + UNIT]
+    for unit, value in enumerate(units):
         for piece, (_, lane) in enumerate(unit_rows(unit, rows)):
             columns[lane // UNIT].append(value[16 * piece : 16 * piece + 16])
-    packed = jnp.concatenate(
+    return jnp.concatenate(
         [jnp.concatenate(pieces, axis=0) for pieces in columns], axis=1
+    )
+
+
+def unpack_units(packed):
+    rows = packed.shape[0]
+    units = []
+    for unit in range(rows * TILE // (BLOCK * UNIT)):
+        pieces = [
+            packed[row : row + 16, lane : lane + UNIT]
+            for row, lane in unit_rows(unit, rows)
+        ]
+        units.append(jnp.concatenate(pieces, axis=0))
+    return jnp.concatenate(units, axis=1)
+
+
+def pack_kernel(panel_ref, out_ref):
+    packed = pack_units(
+        [
+            panel_ref[:, UNIT * unit : UNIT * unit + UNIT]
+            for unit in range(panel_ref.shape[1] // UNIT)
+        ]
     )
     for k in range(out_ref.shape[0]):
         out_ref[k] = packed
@@ -253,7 +289,7 @@
 
 
 def join_gram(table_ref, own_ref, other_ref):
-    first = table_ref[table_ref.shape[0] - 1] == 0
+    first = table_ref[table_ref.shape[0] - 2] == 0
     own, other = own_ref[...], other_ref[...]
     return unpack_gram(
         jnp.concatenate(
@@ -286,14 +322,7 @@
     old_ref, old_factor_ref, factor_ref, part_ref, lower_ref = refs
     factor_rows(gram, factor_ref)
     lower_ref[...] = lower_factor(factor_ref)
-    upper_mask = lax.broadcasted_iota(
-        jnp.int32, (BLOCK, BLOCK), 0
-    ) <= lax.broadcasted_iota(jnp.int32, (BLOCK, BLOCK), 1)
-    upper = jnp.where(upper_mask, factor_ref[:, :BLOCK], 0.0)
-    back = jnp.dot(
-        upper, -old_factor_ref[:, BLOCK:], precision=HIGH,
-        preferred_element_type=jnp.float32,
-    )
+    back = backward_weights(factor_ref, old_factor_ref)
     for b in range(old_ref.shape[0] // BLOCK):
         part_ref[64 * b : 64 * b + 64, :] = jnp.dot(
             back, old_ref[64 * b : 64 * b + 64, :], precision=HIGH,
@@ -301,18 +330,25 @@
         )
 
 
-def step_kernel(*refs, forward, cb, with_old, last):
+def backward_weights(factor_ref, old_factor_ref):
+    upper_mask = lax.broadcasted_iota(
+        jnp.int32, (BLOCK, BLOCK), 0
+    ) <= lax.broadcasted_iota(jnp.int32, (BLOCK, BLOCK), 1)
+    upper = jnp.where(upper_mask, factor_ref[:, :BLOCK], 0.0)
+    return jnp.dot(
+        upper, -old_factor_ref[:, BLOCK:], precision=HIGH,
+        preferred_element_type=jnp.float32,
+    )
+
+
+def step_kernel(*refs, forward, cb, with_old, owned):
     refs = list(refs)
-    tables = []
-    if not last:
-        tables, refs = refs[:2], refs[2:]
-    got_ref, scale_ref, factor_ref = refs[:3]
-    refs = refs[3:]
+    table_ref, tiles_ref, got_ref, scale_ref, factor_ref = refs[:5]
+    refs = refs[5:]
     if with_old:
         part_ref, refs = refs[0], refs[1:]
-    panel_ref, sent_ref = refs[:2]
+    panel_ref, sent_ref, parts_ref, sums_ref = refs
     inverse = split_three(factor_ref[:, BLOCK:])
-    gram = no_gram()
     for b in range(panel_ref.shape[0] // BLOCK):
         where = slice(64 * b, 64 * b + 64)
         value = exact_dot(
@@ -321,33 +357,62 @@
         if with_old:
             value += part_ref[where, :]
         panel_ref[where, :] = value
-        if last:
-            gram = add_gram(gram, value)
-    if last:
-        packed = pack_gram(whole_gram(gram))
-        for k in range(sent_ref.shape[0]):
-            sent_ref[k] = packed
-    else:
-        send_panel(
-            *tables, panel_ref, scale_ref, sent_ref, refs[2], refs[3],
-            forward=forward, cb=cb,
-        )
+    send_panel(
+        table_ref, tiles_ref, panel_ref, scale_ref, sent_ref, parts_ref, sums_ref,
+        forward=forward, cb=cb, owned=owned,
+    )
+
+
+def last_kernel(got_ref, old_ref, old_factor_ref, scale_ref, factor_ref, panel_ref, sent_ref):
+    rows = got_ref.shape[1] - GRAM_ROWS
+    total = got_ref[0, :rows, :]
+    for k in range(1, got_ref.shape[0]):
+        total += got_ref[k, :rows, :]
+    value = unpack_units(total) * scale_ref[...]
+    factor_rows(sum_gram(got_ref), factor_ref)
+    weights = jnp.concatenate(
+        [factor_ref[:, BLOCK:], backward_weights(factor_ref, old_factor_ref)], axis=1
+    )
+    value = jnp.dot(
+        weights, jnp.concatenate([value, old_ref[...]], axis=0), precision=HIGH,
+        preferred_element_type=jnp.float32,
+    )
+    panel_ref[...] = value
+    gram = lax.dot_general(
+        value, value, (((1,), (1,)), ((), ())), precision=HIGH,
+        preferred_element_type=jnp.float32,
+    )
+    packed = pack_gram(gram)
+    for k in range(sent_ref.shape[0]):
+        sent_ref[k] = packed
 
 
 def end_kernel(
-    got_ref, right_ref, left_ref, left_factor_ref, first_ref, second_ref,
-    out_right_ref, out_left_ref, lower_ref, factor_ref, *, left_size, right_size,
+    table_ref, got_ref, right_ref, left_ref, left_factor_ref, *refs, left_size, right_size
 ):
-    lower_ref[0] = first_ref[...]
-    lower_ref[1] = second_ref[...]
+    lower_refs, refs = refs[:4], refs[4:]
+    out_left_ref, out_right_ref, left_lower_ref, right_lower_ref, factor_ref = refs
+    width = out_left_ref.shape[1]
+    at = table_ref[table_ref.shape[0] - 1]
+    block = at // (TILE // width)
+    left = left_ref[pl.ds(pl.multiple_of(BLOCK * block, BLOCK), BLOCK), :]
+    own = left[:, :width]
+    for k in range(1, TILE // width):
+        part = left[:, width * k : width * k + width]
+        own = jnp.where(at - block * (TILE // width) == k, part, own)
+    out_left_ref[...] = math.sqrt(left_size) * jnp.dot(
+        left_factor_ref[:, BLOCK:], own, precision=HIGH,
+        preferred_element_type=jnp.float32,
+    )
+    left_lower_ref[0] = lower_refs[0][...]
+    right_lower_ref[0] = lower_refs[1][...]
+    left_lower_ref[1] = lower_refs[2][...]
+    right_lower_ref[1] = lower_refs[3][...]
+    left_lower_ref[2] = lower_factor(left_factor_ref)
     factor_rows(sum_gram(got_ref), factor_ref)
-    lower_ref[2] = lower_factor(factor_ref)
+    right_lower_ref[2] = lower_factor(factor_ref)
     out_right_ref[...] = math.sqrt(right_size) * jnp.dot(
         factor_ref[:, BLOCK:], right_ref[...], precision=HIGH,
-        preferred_element_type=jnp.float32,
-    )
-    out_left_ref[...] = math.sqrt(left_size) * jnp.dot(
-        left_factor_ref[:, BLOCK:], left_ref[...], precision=HIGH,
         preferred_element_type=jnp.float32,
     )
 
@@ -398,15 +463,23 @@
     return [table, own, other], whole
 
 
+def own_columns(panel, axes):
+    blocks = panel.shape[0] // BLOCK
+    group = blocks * TILE // lax.axis_size(axes)
+    flat = jnp.transpose(panel.reshape(blocks, BLOCK, TILE), (1, 0, 2))
+    flat = flat.reshape(BLOCK, blocks * TILE)
+    return lax.dynamic_slice_in_dim(flat, lax.axis_index(axes) * group, group, 1)
+
+
 def per_device(tiles, tile_slots, tile_counts, user_degree, item_degree, start_panel):
     tile_stack = tiles[0, 0]
     rb = user_degree.shape[0] // TILE
     cb = item_degree.shape[0] // TILE
     rows = lax.axis_size(ROW)
-    cols = lax.axis_size(COL)
     near = lax.axis_size(NEAR)
     core = lax.axis_index("core").astype(jnp.int32).reshape(1)
-    table = jnp.concatenate([tile_slots[0, 0], tile_counts[0], core])
+    col = lax.axis_index(COL).astype(jnp.int32).reshape(1)
+    table = jnp.concatenate([tile_slots[0, 0], tile_counts[0], core, col])
     user_scale = lax.rsqrt(user_degree.astype(jnp.float32)).reshape(rb, TILE)
     item_scale = lax.rsqrt(item_degree.astype(jnp.float32)).reshape(cb, TILE)
 
@@ -423,6 +496,7 @@
 
     user_messages = f32(near, rb * BLOCK // near + GRAM_ROWS, TILE)
     item_messages = f32(rows, cb * BLOCK // rows + HALF_ROWS, TILE)
+    owned_messages = f32(rows, cb * BLOCK // rows + GRAM_ROWS, TILE)
     user_sums = pltpu.VMEM((rb * BLOCK + BLOCK, TILE), jnp.float32)
     item_sums = pltpu.VMEM((cb * BLOCK + BLOCK, TILE), jnp.float32)
     user_parts = pltpu.VMEM((rb * 192, TILE), jnp.bfloat16)
@@ -442,79 +516,92 @@
         name="start",
     )(table, tile_stack, start, item_scale)
 
+    item_group = cb * TILE // rows
+    own_scale = lax.dynamic_slice_in_dim(
+        item_scale.reshape(1, cb * TILE), lax.axis_index(ROW) * item_group, item_group, 1
+    )
     panels = [start]
     factors = []
     lower = []
-    for half in range(1, 2 * STEPS + 1):
+    for half in range(1, 2 * STEPS):
         users = half % 2 == 1
-        last = half == 2 * STEPS
+        owned = half == 2 * STEPS - 1
         with_old = half > 1
         gram, whole = sum_col(sent) if users else sum_row(sent, table)
         panel_shape = f32((rb if users else cb) * BLOCK, TILE)
+        if owned:
+            old_items, gram[0] = lax.optimization_barrier((panels[-1], gram[0]))
+            own_old = own_columns(old_items, ROW)
         old = [panels[half - 2], factors[half - 2]] if with_old else []
+        shapes = [f32(BLOCK, 2 * BLOCK)]
+        if with_old:
+            shapes += [panel_shape, f32(BLOCK, BLOCK)]
         factored = pl.pallas_call(
             functools.partial(factor_kernel, with_old=with_old, halves=not users),
-            out_shape=[f32(BLOCK, 2 * BLOCK)]
-            + ([panel_shape, f32(BLOCK, BLOCK)] if with_old else []),
+            out_shape=shapes,
             in_specs=([VMEM] if users else [SMEM, VMEM, VMEM]) + [VMEM] * len(old),
-            out_specs=[VMEM] * (3 if with_old else 1),
+            out_specs=[VMEM] * len(shapes),
             compiler_params=PARAMS,
             name=f"factor{half}",
         )(*gram, *old)
         factors.append(factored[0])
         lower += factored[2:]
-        tables = [] if last else [table, tile_stack]
-        table_specs = [] if last else [SMEM, VMEM]
+        messages = user_messages
+        if users:
+            messages = owned_messages if owned else item_messages
         operands = [whole, user_scale if users else item_scale, *factored[:2]]
+        if owned:
+            operands[2:], own_old, own_scale = lax.optimization_barrier(
+                (operands[2:], own_old, own_scale)
+            )
         panel, sent = pl.pallas_call(
             functools.partial(
-                step_kernel, forward=not users, cb=cb, with_old=with_old, last=last
+                step_kernel, forward=not users, cb=cb, with_old=with_old, owned=owned
+            ),
+            out_shape=[panel_shape, messages],
+            in_specs=[SMEM, VMEM] + [VMEM] * len(operands),
+            out_specs=[VMEM, VMEM],
+            scratch_shapes=[user_parts, item_sums] if users else [item_parts, user_sums],
+            compiler_params=PARAMS,
+            name=f"half{half}",
+        )(table, tile_stack, *operands)
+        panels.append(panel)
+
+    factor, right, sent = pl.pallas_call(
+        last_kernel,
+        out_shape=[
+            f32(BLOCK, 2 * BLOCK),
+            f32(BLOCK, item_group),
+            f32(lax.axis_size(FLAT), GRAM_ROWS, TILE),
+        ],
+        in_specs=[VMEM] * 4,
+        out_specs=[VMEM] * 3,
+        compiler_params=PARAMS,
+        name="last",
+    )(exchange(sent, ROW), own_old, factors[-1], own_scale)
+    gram = exchange(
+        fold(exchange(sent, FLAT), lax.axis_size(LINE), GRAM_ROWS)[0], LINE
+    )
+    return tuple(
+        pl.pallas_call(
+            functools.partial(
+                end_kernel,
+                left_size=rb * TILE * rows,
+                right_size=cb * TILE * lax.axis_size(COL),
             ),
             out_shape=[
-                panel_shape,
-                f32(near, GRAM_ROWS, TILE)
-                if last
-                else (item_messages if users else user_messages),
+                f32(BLOCK, rb * TILE // lax.axis_size(COL)),
+                f32(BLOCK, item_group),
+                f32(STEPS, BLOCK, BLOCK),
+                f32(STEPS, BLOCK, BLOCK),
             ],
-            in_specs=table_specs + [VMEM] * len(operands),
-            out_specs=[VMEM, VMEM],
-            scratch_shapes=[]
-            if last
-            else ([user_parts, item_sums] if users else [item_parts, user_sums]),
+            in_specs=[SMEM] + [VMEM] * 8,
+            out_specs=[VMEM] * 4,
+            scratch_shapes=[pltpu.VMEM((BLOCK, 2 * BLOCK), jnp.float32)],
             compiler_params=PARAMS,
-            name=f"half{half}",
-        )(*tables, *operands)
-        panels.append(panel)
-
-    gram = fold(exchange(sent, NEAR), lax.axis_size("zh"), GRAM_ROWS)[0]
-    gram = exchange(gram, "zh")
-
-    user_group = rb * TILE // cols
-    item_group = cb * TILE // rows
-    left = jnp.transpose(panels[-2].reshape(rb, BLOCK, TILE), (1, 0, 2))
-    left = lax.dynamic_slice_in_dim(
-        left.reshape(BLOCK, rb * TILE), lax.axis_index(COL) * user_group, user_group, 1
-    )
-    right = jnp.transpose(panels[-1].reshape(cb, BLOCK, TILE), (1, 0, 2))
-    right = lax.dynamic_slice_in_dim(
-        right.reshape(BLOCK, cb * TILE), lax.axis_index(ROW) * item_group, item_group, 1
-    )
-    right_panel, left_panel, right_factors = pl.pallas_call(
-        functools.partial(
-            end_kernel, left_size=rb * TILE * rows, right_size=cb * TILE * cols
-        ),
-        out_shape=[
-            f32(BLOCK, item_group),
-            f32(BLOCK, user_group),
-            f32(STEPS, BLOCK, BLOCK),
-        ],
-        in_specs=[VMEM] * 6,
-        out_specs=[VMEM] * 3,
-        scratch_shapes=[pltpu.VMEM((BLOCK, 2 * BLOCK), jnp.float32)],
-        compiler_params=PARAMS,
-        name="end",
-    )(gram, right, left, factors[-1], lower[1], lower[3])
-    return left_panel, right_panel, jnp.stack(lower[::2]), right_factors
+            name="end",
+        )(table, gram, right, panels[-1], factor, *lower)
+    )
 
 
 def solution(mesh):

time: 331 us -> 327 us (0.988)
  blocking collectives: 182 us -> 202 us
  starting transfers between devices: 58.6 us -> 43.8 us
  waiting for transfers between devices: 47.1 us -> 37.9 us
    all_to_all x6 -> x7, blocking collectives: 103 us -> 122 us  [exchange(): return lax.all_to_all(messages, axes, 0, 0, tiled=True)]
    all_to_all x9 -> x7, starting transfers between devices: 47.4 us -> 36.2 us  [exchange(): return lax.all_to_all(messages, axes, 0, 0, tiled=True)]
    all_to_all x9 -> x7, waiting for transfers between devices: 45.3 us -> 36.4 us  [exchange(): return lax.all_to_all(messages, axes, 0, 0, tiled=True)]
    ppermute x3 -> x2, starting transfers between devices: 11.3 us -> 7.56 us  [sum_row(): other = lax.ppermute(own, 'core', [(0, 1), (1, 0)])]
    pallas_call x6 -> x5, Pallas kernels: 15.3 us -> 12.4 us  [per_device(): pl.pallas_call(functools.partial(factor_kernel, with_old=with_old, halves...]
    pallas_call x6 -> x5, Pallas kernels: 11.1 us -> 11 us  [per_device(): pl.pallas_call(functools.partial(step_kernel, forward=not users, cb=cb, w...]
  transfers between devices with their start and end apart: 12 -> 9, of which waited for: 12 -> 9; matrix products, arithmetic and copies ran while one was open for 1% -> 0% of each run, Pallas kernels for 5% -> 4%
where the time goes in v7:
time: 327 us; the launch traced here: 323 us
  blocking collectives  202 us (62%)
  starting transfers between devices  43.8 us (13%)
  waiting for transfers between devices  37.9 us (12%)
  Pallas kernels  35.5 us (11%)
    all_to_all x7, blocking collectives, exchange(): return lax.all_to_all(messages, axes, 0, 0, tiled=True)  122 us
    all_gather x3, blocking collectives, sum_col(): got = lax.all_gather(own, 'zh', axis=0, tiled=False)  57.1 us
    all_to_all x7, waiting for transfers between devices, exchange(): return lax.all_to_all(messages, axes, 0, 0, tiled=True)  36.4 us
    all_to_all x7, starting transfers between devices, exchange(): return lax.all_to_all(messages, axes, 0, 0, tiled=True)  36.2 us
    all_gather x3, blocking collectives, sum_col(): return ([got], lax.all_gather(half, 'core', axis=0, tiled=True))  22.3 us
    pallas_call x5, Pallas kernels, per_device(): pl.pallas_call(functools.partial(factor_kernel, with_old=with_old, halves...  12.4 us
    pallas_call x5, Pallas kernels, per_device(): pl.pallas_call(functools.partial(step_kernel, forward=not users, cb=cb, w...  11 us
    ppermute x2, starting transfers between devices, sum_row(): other = lax.ppermute(own, 'core', [(0, 1), (1, 0)])  7.56 us
  transfers between devices with their start and end apart: 9, of which 9 were waited for; matrix products, arithmetic and copies ran while one was open for 0% of the time, Pallas kernels for 4%

profile of v7, /device:TPU:1, one launch (start us, length us, event | category | flops | bytes accessed | tf_op | source)
XLA Modules:
  0.0 322.6 jit_solution(12292094312685183734)
XLA Ops:
  0.7 0.8 copy-done.1
  1.5 0.9 pack.1
  2.4 9.2 %all-to-all-start = ((f32[16,48,128]{2,1,0:T(8,128)}), f32[16,48,128]{2,1,0:T(8,128)S(1)}, u32[]{:S(2)}, u32[]{:S(2)}) async-start(f32[16,48,128]{2,1,0:T(8,128)} %pack.1), calls=%async_computation | async-start | bytes 786432 | tf_op jit(solution)/shard_map/all_to_all | solution.py:444
  13.0 10.0 %all-to-all-done.got_ref = f32[16,48,128]{2,1,0:T(8,128)S(1)} async-done(((f32[16,48,128]{2,1,0:T(8,128)}), f32[16,48,128]{2,1,0:T(8,128)S(1)}, u32[]{:S(2)}, u32[]{:S(2)}) %all-to-all-start) | async-done | bytes 393248 | tf_op jit(solution)/shard_map/all_to_all | solution.py:444
  23.0 1.7 start.1
  24.7 17.4 %all_to_all.70.got_ref = f32[8,152,128]{2,1,0:T(8,128)S(1)} all-to-all(f32[8,152,128]{2,1,0:T(8,128)S(1)} %get-tuple-element.41), channel_id=1, replica_groups=mesh['zl'=4,'y'=4,'x'=4,'zh'=4,'core'=2] {'core','x'}, dimensions={0} | all-to-all | bytes 1245184 | tf_op jit(solution)/shard_map/all_to_all | solution.py:444
  42.2 22.7 %all_gather.18.got_ref.refs_0_ = f32[4,152,128]{2,1,0:T(8,128)S(1)} all-gather(f32[1,152,128]{2,1,0:T(8,128)S(1)} %fold.9), channel_id=1, replica_groups=mesh['zl'=4,'y'=4,'x'=4,'zh'=4,'core'=2] {'zh'}, dimensions={0}, use_global_device_ids=true | all-gather | bytes 389120 | tf_op jit(solution)/shard_map/all_gather | solution.py:450
  64.9 0.7 fold.10
  65.6 3.5 %all-to-all-start.2 = ((f32[4,128,128]{2,1,0:T(8,128)}), f32[4,128,128]{2,1,0:T(8,128)S(1)}, u32[]{:S(2)}, u32[]{:S(2)}) async-start(f32[4,128,128]{2,1,0:T(8,128)} %fold.10), calls=%async_computation.2 | async-start | bytes 524288 | tf_op jit(solution)/shard_map/all_to_all | solution.py:444
  69.2 1.7 factor1.1.refs_4_
  70.9 3.7 %all-to-all-done.2 = f32[4,128,128]{2,1,0:T(8,128)S(1)} async-done(((f32[4,128,128]{2,1,0:T(8,128)}), f32[4,128,128]{2,1,0:T(8,128)S(1)}, u32[]{:S(2)}, u32[]{:S(2)}) %all-to-all-start.2) | async-done | bytes 262176 | tf_op jit(solution)/shard_map/all_to_all | solution.py:444
  74.7 7.7 %all_gather.19.refs_2_ = f32[1024,128]{1,0:T(8,128)S(1)} all-gather(f32[512,128]{1,0:T(8,128)S(1)} %bitcast.35), channel_id=1, replica_groups=mesh['zl'=4,'y'=4,'x'=4,'zh'=4,'core'=2] {'core'}, dimensions={0}, use_global_device_ids=true | all-gather | bytes 786432 | tf_op jit(solution)/shard_map/all_gather | solution.py:454
  82.4 1.9 half1.1
  84.3 17.2 %all_to_all.71.got_ref = f32[16,64,128]{2,1,0:T(8,128)S(1)} all-to-all(f32[16,64,128]{2,1,0:T(8,128)S(1)} %get-tuple-element.42), channel_id=1, replica_groups=mesh['zl'=4,'y'=4,'x'=4,'zh'=4,'core'=2] {'zl','y'}, dimensions={0} | all-to-all | bytes 1048576 | tf_op jit(solution)/shard_map/all_to_all | solution.py:444
  101.5 0.8 fold.11
  102.3 4.9 %all-to-all-start.4 = ((f32[16,48,128]{2,1,0:T(8,128)}), f32[16,48,128]{2,1,0:T(8,128)S(1)}, u32[]{:S(2)}, u32[]{:S(2)}) async-start(f32[16,48,128]{2,1,0:T(8,128)} %get-tuple-element.43), calls=%async_computation.4 | async-start | bytes 786432 | tf_op jit(solution)/shard_map/all_to_all | solution.py:444
  107.3 3.7 %collective-permute-start = (f32[16,128]{1,0:T(8,128)S(1)}, f32[16,128]{1,0:T(8,128)S(1)}, u32[]{:S(2)}, u32[]{:S(2)}) collective-permute-start(f32[16,128]{1,0:T(8,128)S(1)} %get-tuple-element.44.refs_1_), channel_id=1, source_target_pairs={{0,1},{1,0},{2,3},{3,2},{4,5},{5,4},{6,7},{7,6},{8,9},{9,8},{10,11... | collective-permute-start | bytes 24584 | tf_op jit(solution)/shard_map/ppermute | solution.py:462
  111.0 0.8 collective-permute-done.refs_2_
  111.8 2.9 factor2.1
  114.6 3.4 %all-to-all-done.4 = f32[16,48,128]{2,1,0:T(8,128)S(1)} async-done(((f32[16,48,128]{2,1,0:T(8,128)}), f32[16,48,128]{2,1,0:T(8,128)S(1)}, u32[]{:S(2)}, u32[]{:S(2)}) %all-to-all-start.4) | async-done | bytes 393248 | tf_op jit(solution)/shard_map/all_to_all | solution.py:444
  118.0 1.9 half2.1
  119.9 16.4 %all_to_all.72.got_ref = f32[8,152,128]{2,1,0:T(8,128)S(1)} all-to-all(f32[8,152,128]{2,1,0:T(8,128)S(1)} %get-tuple-element.48), channel_id=1, replica_groups=mesh['zl'=4,'y'=4,'x'=4,'zh'=4,'core'=2] {'core','x'}, dimensions={0} | all-to-all | bytes 1245184 | tf_op jit(solution)/shard_map/all_to_all | solution.py:444
  136.3 16.8 %all_gather.20.got_ref.refs_0_ = f32[4,152,128]{2,1,0:T(8,128)S(1)} all-gather(f32[1,152,128]{2,1,0:T(8,128)S(1)} %fold.12), channel_id=1, replica_groups=mesh['zl'=4,'y'=4,'x'=4,'zh'=4,'core'=2] {'zh'}, dimensions={0}, use_global_device_ids=true | all-gather | bytes 389120 | tf_op jit(solution)/shard_map/all_gather | solution.py:450
  153.8 3.4 %all-to-all-start.6 = ((f32[4,128,128]{2,1,0:T(8,128)}), f32[4,128,128]{2,1,0:T(8,128)S(1)}, u32[]{:S(2)}, u32[]{:S(2)}) async-start(f32[4,128,128]{2,1,0:T(8,128)} %fold.13), calls=%async_computation.6 | async-start | bytes 524288 | tf_op jit(solution)/shard_map/all_to_all | solution.py:444
  157.2 2.4 factor3.1
  159.7 3.0 all-to-all-done.6
  162.7 7.6 %all_gather.21.refs_2_ = f32[1024,128]{1,0:T(8,128)S(1)} all-gather(f32[512,128]{1,0:T(8,128)S(1)} %bitcast.34), channel_id=1, replica_groups=mesh['zl'=4,'y'=4,'x'=4,'zh'=4,'core'=2] {'core'}, dimensions={0}, use_global_device_ids=true | all-gather | bytes 786432 | tf_op jit(solution)/shard_map/all_gather | solution.py:454
  170.3 1.9 half3.1
  172.2 17.9 %all_to_all.73.got_ref = f32[16,64,128]{2,1,0:T(8,128)S(1)} all-to-all(f32[16,64,128]{2,1,0:T(8,128)S(1)} %get-tuple-element.52), channel_id=1, replica_groups=mesh['zl'=4,'y'=4,'x'=4,'zh'=4,'core'=2] {'zl','y'}, dimensions={0} | all-to-all | bytes 1048576 | tf_op jit(solution)/shard_map/all_to_all | solution.py:444
  190.1 0.8 fold.14
  190.8 4.9 %all-to-all-start.8 = ((f32[16,48,128]{2,1,0:T(8,128)}), f32[16,48,128]{2,1,0:T(8,128)S(1)}, u32[]{:S(2)}, u32[]{:S(2)}) async-start(f32[16,48,128]{2,1,0:T(8,128)} %get-tuple-element.53), calls=%async_computation.8 | async-start | bytes 786432 | tf_op jit(solution)/shard_map/all_to_all | solution.py:444
  195.8 3.9 %collective-permute-start.1 = (f32[16,128]{1,0:T(8,128)S(1)}, f32[16,128]{1,0:T(8,128)S(1)}, u32[]{:S(2)}, u32[]{:S(2)}) collective-permute-start(f32[16,128]{1,0:T(8,128)S(1)} %get-tuple-element.54.refs_1_), channel_id=1, source_target_pairs={{0,1},{1,0},{2,3},{3,2},{4,5},{5,4},{6,7},{7,6},{8,9},{9,8},{10,11... | collective-permute-start | bytes 24584 | tf_op jit(solution)/shard_map/ppermute | solution.py:462
  200.3 2.9 factor4.1
  203.2 3.4 %all-to-all-done.8 = f32[16,48,128]{2,1,0:T(8,128)S(1)} async-done(((f32[16,48,128]{2,1,0:T(8,128)}), f32[16,48,128]{2,1,0:T(8,128)S(1)}, u32[]{:S(2)}, u32[]{:S(2)}) %all-to-all-start.8) | async-done | bytes 393248 | tf_op jit(solution)/shard_map/all_to_all | solution.py:444
  206.5 2.7 half4.1
  209.3 6.8 %all-to-all-start.9 = ((f32[8,152,128]{2,1,0:T(8,128)}), f32[8,152,128]{2,1,0:T(8,128)S(1)}, u32[]{:S(2)}, u32[]{:S(2)}) async-start(f32[8,152,128]{2,1,0:T(8,128)} %get-tuple-element.58), calls=%async_computation.9 | async-start | bytes 1245184 | tf_op jit(solution)/shard_map/all_to_all | solution.py:444
  216.1 10.4 %all-to-all-done.9.got_ref = f32[8,152,128]{2,1,0:T(8,128)S(1)} async-done(((f32[8,152,128]{2,1,0:T(8,128)}), f32[8,152,128]{2,1,0:T(8,128)S(1)}, u32[]{:S(2)}, u32[]{:S(2)}) %all-to-all-start.9) | async-done | bytes 622624 | tf_op jit(solution)/shard_map/all_to_all | solution.py:444
  226.5 17.6 %all_gather.22.got_ref.refs_0_ = f32[4,152,128]{2,1,0:T(8,128)S(1)} all-gather(f32[1,152,128]{2,1,0:T(8,128)S(1)} %fold.15), channel_id=1, replica_groups=mesh['zl'=4,'y'=4,'x'=4,'zh'=4,'core'=2] {'zh'}, dimensions={0}, use_global_device_ids=true | all-gather | bytes 389120 | tf_op jit(solution)/shard_map/all_gather | solution.py:450
  244.9 3.4 %all-to-all-start.10 = ((f32[4,128,128]{2,1,0:T(8,128)}), f32[4,128,128]{2,1,0:T(8,128)S(1)}, u32[]{:S(2)}, u32[]{:S(2)}) async-start(f32[4,128,128]{2,1,0:T(8,128)} %fold.16), calls=%async_computation.10 | async-start | bytes 524288 | tf_op jit(solution)/shard_map/all_to_all | solution.py:444
  248.7 2.4 factor5.1
  251.3 2.5 all-to-all-done.10
  253.8 7.0 %all_gather.23.refs_2_ = f32[1024,128]{1,0:T(8,128)S(1)} all-gather(f32[512,128]{1,0:T(8,128)S(1)} %bitcast.33), channel_id=1, replica_groups=mesh['zl'=4,'y'=4,'x'=4,'zh'=4,'core'=2] {'core'}, dimensions={0}, use_global_device_ids=true | all-gather | bytes 786432 | tf_op jit(solution)/shard_map/all_gather | solution.py:454
  260.8 2.6 half5.1
  263.4 20.0 %all_to_all.74.got_ref = f32[16,72,128]{2,1,0:T(8,128)S(1)} all-to-all(f32[16,72,128]{2,1,0:T(8,128)S(1)} %get-tuple-element.67), channel_id=1, replica_groups=mesh['zl'=4,'y'=4,'x'=4,'zh'=4,'core'=2] {'zl','y'}, dimensions={0} | all-to-all | bytes 1179648 | tf_op jit(solution)/shard_map/all_to_all | solution.py:444
  283.4 2.5 last.1
  285.9 14.7 %all_to_all.75.got_ref = f32[32,24,128]{2,1,0:T(8,128)S(1)} all-to-all(f32[32,24,128]{2,1,0:T(8,128)S(1)} %get-tuple-element.70), channel_id=1, replica_groups=mesh['zl'=4,'y'=4,'x'=4,'zh'=4,'core'=2] {'core','y','x'}, dimensions={0} | all-to-all | bytes 786432 | tf_op jit(solution)/shard_map/all_to_all | solution.py:444
  300.7 18.7 %all_to_all.76.got_ref = f32[16,24,128]{2,1,0:T(8,128)S(1)} all-to-all(f32[16,24,128]{2,1,0:T(8,128)S(1)} %fold.17), channel_id=1, replica_groups=mesh['zl'=4,'y'=4,'x'=4,'zh'=4,'core'=2] {'zh','zl'}, dimensions={0} | all-to-all | bytes 393216 | tf_op jit(solution)/shard_map/all_to_all | solution.py:444
  319.4 3.2 end.1
  (23 shorter events, 3.5 us)
Async XLA Ops:
  0.6 22.4 %copy-start = (bf16[1,1,32,128,128]{4,3,2,1,0:T(8,128)(2,1)S(1)}, bf16[1,1,32,128,128]{4,3,2,1,0:T(8,128)(2,1)}, u32[]{:S(2)}) copy-start(bf16[1,1,32,128,128]{4,3,2,1,0:T(8,128)(2,1)} %param.6) | copy-start | bytes 3145732
  0.6 0.8 copy-start.1
  2.4 20.6 %all-to-all-start = ((f32[16,48,128]{2,1,0:T(8,128)}), f32[16,48,128]{2,1,0:T(8,128)S(1)}, u32[]{:S(2)}, u32[]{:S(2)}) async-start(f32[16,48,128]{2,1,0:T(8,128)} %pack.1), calls=%async_computation | async-start | bytes 786432 | tf_op jit(solution)/shard_map/all_to_all | solution.py:444
  12.2 0.8 copy-start.2
  12.2 0.7 copy-start.4
  65.6 3.5 %copy-start.3 = (s32[2048]{0:T(1024)S(1)}, s32[2048]{0:T(1024)}, u32[]{:S(2)}) copy-start(s32[2048]{0:T(1024)} %param.9) | copy-start | bytes 24580
  65.6 9.0 %all-to-all-start.2 = ((f32[4,128,128]{2,1,0:T(8,128)}), f32[4,128,128]{2,1,0:T(8,128)S(1)}, u32[]{:S(2)}, u32[]{:S(2)}) async-start(f32[4,128,128]{2,1,0:T(8,128)} %fold.10), calls=%async_computation.2 | async-start | bytes 524288 | tf_op jit(solution)/shard_map/all_to_all | solution.py:444
  102.3 15.7 %all-to-all-start.4 = ((f32[16,48,128]{2,1,0:T(8,128)}), f32[16,48,128]{2,1,0:T(8,128)S(1)}, u32[]{:S(2)}, u32[]{:S(2)}) async-start(f32[16,48,128]{2,1,0:T(8,128)} %get-tuple-element.43), calls=%async_computation.4 | async-start | bytes 786432 | tf_op jit(solution)/shard_map/all_to_all | solution.py:444
  107.3 4.5 %collective-permute-start = (f32[16,128]{1,0:T(8,128)S(1)}, f32[16,128]{1,0:T(8,128)S(1)}, u32[]{:S(2)}, u32[]{:S(2)}) collective-permute-start(f32[16,128]{1,0:T(8,128)S(1)} %get-tuple-element.44.refs_1_), channel_id=1, source_target_pairs={{0,1},{1,0},{2,3},{3,2},{4,5},{5,4},{6,7},{7,6},{8,9},{9,8},{10,11... | collective-permute-start | bytes 24584 | tf_op jit(solution)/shard_map/ppermute | solution.py:462
  153.8 8.9 %all-to-all-start.6 = ((f32[4,128,128]{2,1,0:T(8,128)}), f32[4,128,128]{2,1,0:T(8,128)S(1)}, u32[]{:S(2)}, u32[]{:S(2)}) async-start(f32[4,128,128]{2,1,0:T(8,128)} %fold.13), calls=%async_computation.6 | async-start | bytes 524288 | tf_op jit(solution)/shard_map/all_to_all | solution.py:444
  190.8 15.7 %all-to-all-start.8 = ((f32[16,48,128]{2,1,0:T(8,128)}), f32[16,48,128]{2,1,0:T(8,128)S(1)}, u32[]{:S(2)}, u32[]{:S(2)}) async-start(f32[16,48,128]{2,1,0:T(8,128)} %get-tuple-element.53), calls=%async_computation.8 | async-start | bytes 786432 | tf_op jit(solution)/shard_map/all_to_all | solution.py:444
  195.8 4.5 %collective-permute-start.1 = (f32[16,128]{1,0:T(8,128)S(1)}, f32[16,128]{1,0:T(8,128)S(1)}, u32[]{:S(2)}, u32[]{:S(2)}) collective-permute-start(f32[16,128]{1,0:T(8,128)S(1)} %get-tuple-element.54.refs_1_), channel_id=1, source_target_pairs={{0,1},{1,0},{2,3},{3,2},{4,5},{5,4},{6,7},{7,6},{8,9},{9,8},{10,11... | collective-permute-start | bytes 24584 | tf_op jit(solution)/shard_map/ppermute | solution.py:462
  209.3 17.2 %all-to-all-start.9 = ((f32[8,152,128]{2,1,0:T(8,128)}), f32[8,152,128]{2,1,0:T(8,128)S(1)}, u32[]{:S(2)}, u32[]{:S(2)}) async-start(f32[8,152,128]{2,1,0:T(8,128)} %get-tuple-element.58), calls=%async_computation.9 | async-start | bytes 1245184 | tf_op jit(solution)/shard_map/all_to_all | solution.py:444
  244.9 8.9 %all-to-all-start.10 = ((f32[4,128,128]{2,1,0:T(8,128)}), f32[4,128,128]{2,1,0:T(8,128)S(1)}, u32[]{:S(2)}, u32[]{:S(2)}) async-start(f32[4,128,128]{2,1,0:T(8,128)} %fold.16), calls=%async_computation.10 | async-start | bytes 524288 | tf_op jit(solution)/shard_map/all_to_all | solution.py:444

commit v8 on v7

--- a/solution.py
+++ b/solution.py
@@ -289,7 +289,7 @@
 
 
 def join_gram(table_ref, own_ref, other_ref):
-    first = table_ref[table_ref.shape[0] - 2] == 0
+    first = table_ref[table_ref.shape[0] - 3] == 0
     own, other = own_ref[...], other_ref[...]
     return unpack_gram(
         jnp.concatenate(
@@ -310,8 +310,35 @@
     return jnp.where(mask, lower, 0.0)
 
 
-def factor_kernel(*refs, with_old, halves):
+def cut(ref, height, start, width):
+    per_block = TILE // UNIT
+    block = start // per_block
+    after = jnp.minimum(block + 1, ref.shape[0] // height - 1)
+    wide = jnp.concatenate(
+        [
+            ref[pl.ds(pl.multiple_of(height * b, height), height), :]
+            for b in (block, after)
+        ],
+        axis=1,
+    )
+    own = wide[:, :width]
+    for k in range(1, per_block):
+        own = jnp.where(
+            start - block * per_block == k, wide[:, UNIT * k : UNIT * k + width], own
+        )
+    return own
+
+
+def factor_kernel(*refs, with_old, halves, owned=False):
     refs = list(refs)
+    if owned:
+        table_ref, items_ref, scale_ref = refs[3:6]
+        own_items_ref, own_scale_ref = refs[-2:]
+        width = own_items_ref.shape[1]
+        start = (width // UNIT) * table_ref[table_ref.shape[0] - 1]
+        own_items_ref[...] = cut(items_ref, BLOCK, start, width)
+        own_scale_ref[...] = cut(scale_ref, 1, start, width)
+        refs = refs[:3] + refs[6:-2]
     if halves:
         gram, refs = join_gram(*refs[:3]), refs[3:]
     else:
@@ -347,7 +374,11 @@
     refs = refs[5:]
     if with_old:
         part_ref, refs = refs[0], refs[1:]
-    panel_ref, sent_ref, parts_ref, sums_ref = refs
+    if owned:
+        sent_ref, own_ref, panel_ref = refs[:3]
+    else:
+        panel_ref, sent_ref = refs[:2]
+    parts_ref, sums_ref = refs[-2:]
     inverse = split_three(factor_ref[:, BLOCK:])
     for b in range(panel_ref.shape[0] // BLOCK):
         where = slice(64 * b, 64 * b + 64)
@@ -361,6 +392,10 @@
         table_ref, tiles_ref, panel_ref, scale_ref, sent_ref, parts_ref, sums_ref,
         forward=forward, cb=cb, owned=owned,
     )
+    if owned:
+        width = own_ref.shape[1]
+        start = (width // UNIT) * table_ref[table_ref.shape[0] - 2]
+        own_ref[...] = cut(panel_ref, BLOCK, start, width)
 
 
 def last_kernel(got_ref, old_ref, old_factor_ref, scale_ref, factor_ref, panel_ref, sent_ref):
@@ -388,20 +423,12 @@
 
 
 def end_kernel(
-    table_ref, got_ref, right_ref, left_ref, left_factor_ref, *refs, left_size, right_size
+    got_ref, right_ref, left_ref, left_factor_ref, *refs, left_size, right_size
 ):
     lower_refs, refs = refs[:4], refs[4:]
     out_left_ref, out_right_ref, left_lower_ref, right_lower_ref, factor_ref = refs
-    width = out_left_ref.shape[1]
-    at = table_ref[table_ref.shape[0] - 1]
-    block = at // (TILE // width)
-    left = left_ref[pl.ds(pl.multiple_of(BLOCK * block, BLOCK), BLOCK), :]
-    own = left[:, :width]
-    for k in range(1, TILE // width):
-        part = left[:, width * k : width * k + width]
-        own = jnp.where(at - block * (TILE // width) == k, part, own)
     out_left_ref[...] = math.sqrt(left_size) * jnp.dot(
-        left_factor_ref[:, BLOCK:], own, precision=HIGH,
+        left_factor_ref[:, BLOCK:], left_ref[...], precision=HIGH,
         preferred_element_type=jnp.float32,
     )
     left_lower_ref[0] = lower_refs[0][...]
@@ -463,14 +490,6 @@
     return [table, own, other], whole
 
 
-def own_columns(panel, axes):
-    blocks = panel.shape[0] // BLOCK
-    group = blocks * TILE // lax.axis_size(axes)
-    flat = jnp.transpose(panel.reshape(blocks, BLOCK, TILE), (1, 0, 2))
-    flat = flat.reshape(BLOCK, blocks * TILE)
-    return lax.dynamic_slice_in_dim(flat, lax.axis_index(axes) * group, group, 1)
-
-
 def per_device(tiles, tile_slots, tile_counts, user_degree, item_degree, start_panel):
     tile_stack = tiles[0, 0]
     rb = user_degree.shape[0] // TILE
@@ -479,7 +498,8 @@
     near = lax.axis_size(NEAR)
     core = lax.axis_index("core").astype(jnp.int32).reshape(1)
     col = lax.axis_index(COL).astype(jnp.int32).reshape(1)
-    table = jnp.concatenate([tile_slots[0, 0], tile_counts[0], core, col])
+    row = lax.axis_index(ROW).astype(jnp.int32).reshape(1)
+    table = jnp.concatenate([tile_slots[0, 0], tile_counts[0], core, col, row])
     user_scale = lax.rsqrt(user_degree.astype(jnp.float32)).reshape(rb, TILE)
     item_scale = lax.rsqrt(item_degree.astype(jnp.float32)).reshape(cb, TILE)
 
@@ -517,9 +537,6 @@
     )(table, tile_stack, start, item_scale)
 
     item_group = cb * TILE // rows
-    own_scale = lax.dynamic_slice_in_dim(
-        item_scale.reshape(1, cb * TILE), lax.axis_index(ROW) * item_group, item_group, 1
-    )
     panels = [start]
     factors = []
     lower = []
@@ -529,43 +546,53 @@
         with_old = half > 1
         gram, whole = sum_col(sent) if users else sum_row(sent, table)
         panel_shape = f32((rb if users else cb) * BLOCK, TILE)
-        if owned:
-            old_items, gram[0] = lax.optimization_barrier((panels[-1], gram[0]))
-            own_old = own_columns(old_items, ROW)
         old = [panels[half - 2], factors[half - 2]] if with_old else []
         shapes = [f32(BLOCK, 2 * BLOCK)]
         if with_old:
             shapes += [panel_shape, f32(BLOCK, BLOCK)]
+        wanted = []
+        if owned:
+            wanted = [table, panels[-1], item_scale]
+            shapes += [f32(BLOCK, item_group), f32(1, item_group)]
         factored = pl.pallas_call(
-            functools.partial(factor_kernel, with_old=with_old, halves=not users),
+            functools.partial(
+                factor_kernel, with_old=with_old, halves=not users, owned=owned
+            ),
             out_shape=shapes,
-            in_specs=([VMEM] if users else [SMEM, VMEM, VMEM]) + [VMEM] * len(old),
+            in_specs=([VMEM] if users else [SMEM, VMEM, VMEM])
+            + [VMEM] * len(old)
+            + ([SMEM, VMEM, VMEM] if owned else []),
             out_specs=[VMEM] * len(shapes),
             compiler_params=PARAMS,
             name=f"factor{half}",
-        )(*gram, *old)
+        )(*gram, *old, *wanted)
         factors.append(factored[0])
-        lower += factored[2:]
+        lower += factored[2:3]
         messages = user_messages
         if users:
             messages = owned_messages if owned else item_messages
         operands = [whole, user_scale if users else item_scale, *factored[:2]]
+        scratch = [user_parts, item_sums] if users else [item_parts, user_sums]
+        shapes = [panel_shape, messages]
         if owned:
-            operands[2:], own_old, own_scale = lax.optimization_barrier(
-                (operands[2:], own_old, own_scale)
-            )
-        panel, sent = pl.pallas_call(
+            shapes = [messages, f32(BLOCK, rb * TILE // lax.axis_size(COL))]
+            scratch = [pltpu.VMEM(panel_shape.shape, jnp.float32), *scratch]
+        results = pl.pallas_call(
             functools.partial(
                 step_kernel, forward=not users, cb=cb, with_old=with_old, owned=owned
             ),
-            out_shape=[panel_shape, messages],
+            out_shape=shapes,
             in_specs=[SMEM, VMEM] + [VMEM] * len(operands),
             out_specs=[VMEM, VMEM],
-            scratch_shapes=[user_parts, item_sums] if users else [item_parts, user_sums],
+            scratch_shapes=scratch,
             compiler_params=PARAMS,
             name=f"half{half}",
         )(table, tile_stack, *operands)
-        panels.append(panel)
+        if owned:
+            sent, left = results
+        else:
+            panel, sent = results
+            panels.append(panel)
 
     factor, right, sent = pl.pallas_call(
         last_kernel,
@@ -578,7 +605,7 @@
         out_specs=[VMEM] * 3,
         compiler_params=PARAMS,
         name="last",
-    )(exchange(sent, ROW), own_old, factors[-1], own_scale)
+    )(exchange(sent, ROW), factored[3], factors[-1], factored[4])
     gram = exchange(
         fold(exchange(sent, FLAT), lax.axis_size(LINE), GRAM_ROWS)[0], LINE
     )
@@ -595,12 +622,12 @@
                 f32(STEPS, BLOCK, BLOCK),
                 f32(STEPS, BLOCK, BLOCK),
             ],
-            in_specs=[SMEM] + [VMEM] * 8,
+            in_specs=[VMEM] * 8,
             out_specs=[VMEM] * 4,
             scratch_shapes=[pltpu.VMEM((BLOCK, 2 * BLOCK), jnp.float32)],
             compiler_params=PARAMS,
             name="end",
-        )(table, gram, right, panels[-1], factor, *lower)
+        )(gram, right, left, factor, *lower)
     )
 
 

time: 327 us -> 325 us (level)
  blocking collectives: 202 us -> 218 us
  waiting for transfers between devices: 37.9 us -> 27.4 us
  starting transfers between devices: 43.8 us -> 37 us
    all_to_all x7 -> x8, blocking collectives: 122 us -> 139 us  [exchange(): return lax.all_to_all(messages, axes, 0, 0, tiled=True)]
    all_to_all x7 -> x6, waiting for transfers between devices: 36.4 us -> 26 us  [exchange(): return lax.all_to_all(messages, axes, 0, 0, tiled=True)]
    all_to_all x7 -> x6, starting transfers between devices: 36.2 us -> 29.4 us  [exchange(): return lax.all_to_all(messages, axes, 0, 0, tiled=True)]
  transfers between devices with their start and end apart: 9 -> 8, of which waited for: 9 -> 8; matrix products, arithmetic and copies ran while one was open for 0% -> 0% of each run, Pallas kernels for 4% -> 4%
where the time goes in v8:
time: 325 us; the launch traced here: 320 us
  blocking collectives  218 us (67%)
  starting transfers between devices  37 us (11%)
  Pallas kernels  34.8 us (11%)
  waiting for transfers between devices  27.4 us (8%)
    all_to_all x8, blocking collectives, exchange(): return lax.all_to_all(messages, axes, 0, 0, tiled=True)  139 us
    all_gather x3, blocking collectives, sum_col(): got = lax.all_gather(own, 'zh', axis=0, tiled=False)  56.3 us
    all_to_all x6, starting transfers between devices, exchange(): return lax.all_to_all(messages, axes, 0, 0, tiled=True)  29.4 us
    all_to_all x6, waiting for transfers between devices, exchange(): return lax.all_to_all(messages, axes, 0, 0, tiled=True)  26 us
    all_gather x3, blocking collectives, sum_col(): return ([got], lax.all_gather(half, 'core', axis=0, tiled=True))  22.9 us
    pallas_call x5, Pallas kernels, per_device(): pl.pallas_call(functools.partial(factor_kernel, with_old=with_old, halves...  12.9 us
    pallas_call x5, Pallas kernels, per_device(): pl.pallas_call(functools.partial(step_kernel, forward=not users, cb=cb, w...  10.2 us
    ppermute x2, starting transfers between devices, sum_row(): other = lax.ppermute(own, 'core', [(0, 1), (1, 0)])  7.57 us
  transfers between devices with their start and end apart: 8, of which 8 were waited for; matrix products, arithmetic and copies ran while one was open for 0% of the time, Pallas kernels for 4%

profile of v8, /device:TPU:1, one launch (start us, length us, event | category | flops | bytes accessed | tf_op | source)
XLA Modules:
  0.0 320.4 jit_solution(15194362399492207951)
XLA Ops:
  0.7 0.8 copy-done.1
  1.5 0.9 pack.1
  2.4 9.2 %all-to-all-start = ((f32[16,48,128]{2,1,0:T(8,128)}), f32[16,48,128]{2,1,0:T(8,128)S(1)}, u32[]{:S(2)}, u32[]{:S(2)}) async-start(f32[16,48,128]{2,1,0:T(8,128)} %pack.1), calls=%async_computation | async-start | bytes 786432 | tf_op jit(solution)/shard_map/all_to_all | solution.py:471
  13.0 10.0 %all-to-all-done.got_ref = f32[16,48,128]{2,1,0:T(8,128)S(1)} async-done(((f32[16,48,128]{2,1,0:T(8,128)}), f32[16,48,128]{2,1,0:T(8,128)S(1)}, u32[]{:S(2)}, u32[]{:S(2)}) %all-to-all-start) | async-done | bytes 393248 | tf_op jit(solution)/shard_map/all_to_all | solution.py:471
  23.0 1.7 start.1
  24.7 17.4 %all_to_all.70.got_ref = f32[8,152,128]{2,1,0:T(8,128)S(1)} all-to-all(f32[8,152,128]{2,1,0:T(8,128)S(1)} %get-tuple-element.37), channel_id=1, replica_groups=mesh['zl'=4,'y'=4,'x'=4,'zh'=4,'core'=2] {'core','x'}, dimensions={0} | all-to-all | bytes 1245184 | tf_op jit(solution)/shard_map/all_to_all | solution.py:471
  42.2 22.7 %all_gather.18.got_ref.refs_0_ = f32[4,152,128]{2,1,0:T(8,128)S(1)} all-gather(f32[1,152,128]{2,1,0:T(8,128)S(1)} %fold.9), channel_id=1, replica_groups=mesh['zl'=4,'y'=4,'x'=4,'zh'=4,'core'=2] {'zh'}, dimensions={0}, use_global_device_ids=true | all-gather | bytes 389120 | tf_op jit(solution)/shard_map/all_gather | solution.py:477
  64.9 0.7 fold.10
  65.7 3.5 %all-to-all-start.2 = ((f32[4,128,128]{2,1,0:T(8,128)}), f32[4,128,128]{2,1,0:T(8,128)S(1)}, u32[]{:S(2)}, u32[]{:S(2)}) async-start(f32[4,128,128]{2,1,0:T(8,128)} %fold.10), calls=%async_computation.2 | async-start | bytes 524288 | tf_op jit(solution)/shard_map/all_to_all | solution.py:471
  69.2 1.7 factor1.1.refs_4_
  71.0 3.7 %all-to-all-done.2 = f32[4,128,128]{2,1,0:T(8,128)S(1)} async-done(((f32[4,128,128]{2,1,0:T(8,128)}), f32[4,128,128]{2,1,0:T(8,128)S(1)}, u32[]{:S(2)}, u32[]{:S(2)}) %all-to-all-start.2) | async-done | bytes 262176 | tf_op jit(solution)/shard_map/all_to_all | solution.py:471
  74.7 7.7 %all_gather.19.refs_2_ = f32[1024,128]{1,0:T(8,128)S(1)} all-gather(f32[512,128]{1,0:T(8,128)S(1)} %bitcast.26), channel_id=1, replica_groups=mesh['zl'=4,'y'=4,'x'=4,'zh'=4,'core'=2] {'core'}, dimensions={0}, use_global_device_ids=true | all-gather | bytes 786432 | tf_op jit(solution)/shard_map/all_gather | solution.py:481
  82.4 1.9 half1.1
  84.3 17.2 %all_to_all.71.got_ref = f32[16,64,128]{2,1,0:T(8,128)S(1)} all-to-all(f32[16,64,128]{2,1,0:T(8,128)S(1)} %get-tuple-element.38), channel_id=1, replica_groups=mesh['zl'=4,'y'=4,'x'=4,'zh'=4,'core'=2] {'zl','y'}, dimensions={0} | all-to-all | bytes 1048576 | tf_op jit(solution)/shard_map/all_to_all | solution.py:471
  101.5 0.8 fold.11
  102.3 5.0 %all-to-all-start.4 = ((f32[16,48,128]{2,1,0:T(8,128)}), f32[16,48,128]{2,1,0:T(8,128)S(1)}, u32[]{:S(2)}, u32[]{:S(2)}) async-start(f32[16,48,128]{2,1,0:T(8,128)} %get-tuple-element.39), calls=%async_computation.4 | async-start | bytes 786432 | tf_op jit(solution)/shard_map/all_to_all | solution.py:471
  107.3 3.7 %collective-permute-start = (f32[16,128]{1,0:T(8,128)S(1)}, f32[16,128]{1,0:T(8,128)S(1)}, u32[]{:S(2)}, u32[]{:S(2)}) collective-permute-start(f32[16,128]{1,0:T(8,128)S(1)} %get-tuple-element.40.refs_1_), channel_id=1, source_target_pairs={{0,1},{1,0},{2,3},{3,2},{4,5},{5,4},{6,7},{7,6},{8,9},{9,8},{10,11... | collective-permute-start | bytes 24584 | tf_op jit(solution)/shard_map/ppermute | solution.py:489
  111.0 0.8 collective-permute-done.refs_2_
  111.8 2.9 factor2.1
  114.7 3.3 %all-to-all-done.4 = f32[16,48,128]{2,1,0:T(8,128)S(1)} async-done(((f32[16,48,128]{2,1,0:T(8,128)}), f32[16,48,128]{2,1,0:T(8,128)S(1)}, u32[]{:S(2)}, u32[]{:S(2)}) %all-to-all-start.4) | async-done | bytes 393248 | tf_op jit(solution)/shard_map/all_to_all | solution.py:471
  118.0 1.9 half2.1
  119.9 16.4 %all_to_all.72.got_ref = f32[8,152,128]{2,1,0:T(8,128)S(1)} all-to-all(f32[8,152,128]{2,1,0:T(8,128)S(1)} %get-tuple-element.44), channel_id=1, replica_groups=mesh['zl'=4,'y'=4,'x'=4,'zh'=4,'core'=2] {'core','x'}, dimensions={0} | all-to-all | bytes 1245184 | tf_op jit(solution)/shard_map/all_to_all | solution.py:471
  136.3 16.9 %all_gather.20.got_ref.refs_0_ = f32[4,152,128]{2,1,0:T(8,128)S(1)} all-gather(f32[1,152,128]{2,1,0:T(8,128)S(1)} %fold.12), channel_id=1, replica_groups=mesh['zl'=4,'y'=4,'x'=4,'zh'=4,'core'=2] {'zh'}, dimensions={0}, use_global_device_ids=true | all-gather | bytes 389120 | tf_op jit(solution)/shard_map/all_gather | solution.py:477
  153.2 0.7 fold.13
  153.9 3.4 %all-to-all-start.6 = ((f32[4,128,128]{2,1,0:T(8,128)}), f32[4,128,128]{2,1,0:T(8,128)S(1)}, u32[]{:S(2)}, u32[]{:S(2)}) async-start(f32[4,128,128]{2,1,0:T(8,128)} %fold.13), calls=%async_computation.6 | async-start | bytes 524288 | tf_op jit(solution)/shard_map/all_to_all | solution.py:471
  157.3 2.4 factor3.1
  159.8 3.0 all-to-all-done.6
  162.8 7.6 %all_gather.21.refs_2_ = f32[1024,128]{1,0:T(8,128)S(1)} all-gather(f32[512,128]{1,0:T(8,128)S(1)} %bitcast.25), channel_id=1, replica_groups=mesh['zl'=4,'y'=4,'x'=4,'zh'=4,'core'=2] {'core'}, dimensions={0}, use_global_device_ids=true | all-gather | bytes 786432 | tf_op jit(solution)/shard_map/all_gather | solution.py:481
  170.4 1.9 half3.1
  172.3 17.8 %all_to_all.73.got_ref = f32[16,64,128]{2,1,0:T(8,128)S(1)} all-to-all(f32[16,64,128]{2,1,0:T(8,128)S(1)} %get-tuple-element.48), channel_id=1, replica_groups=mesh['zl'=4,'y'=4,'x'=4,'zh'=4,'core'=2] {'zl','y'}, dimensions={0} | all-to-all | bytes 1048576 | tf_op jit(solution)/shard_map/all_to_all | solution.py:471
  190.1 0.8 fold.14
  190.9 4.9 %all-to-all-start.8 = ((f32[16,48,128]{2,1,0:T(8,128)}), f32[16,48,128]{2,1,0:T(8,128)S(1)}, u32[]{:S(2)}, u32[]{:S(2)}) async-start(f32[16,48,128]{2,1,0:T(8,128)} %get-tuple-element.49), calls=%async_computation.8 | async-start | bytes 786432 | tf_op jit(solution)/shard_map/all_to_all | solution.py:471
  195.8 3.9 %collective-permute-start.1 = (f32[16,128]{1,0:T(8,128)S(1)}, f32[16,128]{1,0:T(8,128)S(1)}, u32[]{:S(2)}, u32[]{:S(2)}) collective-permute-start(f32[16,128]{1,0:T(8,128)S(1)} %get-tuple-element.50.refs_1_), channel_id=1, source_target_pairs={{0,1},{1,0},{2,3},{3,2},{4,5},{5,4},{6,7},{7,6},{8,9},{9,8},{10,11... | collective-permute-start | bytes 24584 | tf_op jit(solution)/shard_map/ppermute | solution.py:489
  200.3 2.9 factor4.1
  203.2 3.4 %all-to-all-done.8 = f32[16,48,128]{2,1,0:T(8,128)S(1)} async-done(((f32[16,48,128]{2,1,0:T(8,128)}), f32[16,48,128]{2,1,0:T(8,128)S(1)}, u32[]{:S(2)}, u32[]{:S(2)}) %all-to-all-start.8) | async-done | bytes 393248 | tf_op jit(solution)/shard_map/all_to_all | solution.py:471
  206.6 1.9 half4.1
  208.5 16.4 %all_to_all.74.got_ref = f32[8,152,128]{2,1,0:T(8,128)S(1)} all-to-all(f32[8,152,128]{2,1,0:T(8,128)S(1)} %get-tuple-element.54), channel_id=1, replica_groups=mesh['zl'=4,'y'=4,'x'=4,'zh'=4,'core'=2] {'core','x'}, dimensions={0} | all-to-all | bytes 1245184 | tf_op jit(solution)/shard_map/all_to_all | solution.py:471
  224.9 16.7 %all_gather.22.got_ref.refs_0_ = f32[4,152,128]{2,1,0:T(8,128)S(1)} all-gather(f32[1,152,128]{2,1,0:T(8,128)S(1)} %fold.15), channel_id=1, replica_groups=mesh['zl'=4,'y'=4,'x'=4,'zh'=4,'core'=2] {'zh'}, dimensions={0}, use_global_device_ids=true | all-gather | bytes 389120 | tf_op jit(solution)/shard_map/all_gather | solution.py:477
  242.3 3.4 %all-to-all-start.10 = ((f32[4,128,128]{2,1,0:T(8,128)}), f32[4,128,128]{2,1,0:T(8,128)S(1)}, u32[]{:S(2)}, u32[]{:S(2)}) async-start(f32[4,128,128]{2,1,0:T(8,128)} %fold.16), calls=%async_computation.10 | async-start | bytes 524288 | tf_op jit(solution)/shard_map/all_to_all | solution.py:471
  245.7 3.0 factor5.1
  248.7 2.5 all-to-all-done.10
  251.2 7.6 %all_gather.23.refs_2_ = f32[1024,128]{1,0:T(8,128)S(1)} all-gather(f32[512,128]{1,0:T(8,128)S(1)} %bitcast.24), channel_id=1, replica_groups=mesh['zl'=4,'y'=4,'x'=4,'zh'=4,'core'=2] {'core'}, dimensions={0}, use_global_device_ids=true | all-gather | bytes 786432 | tf_op jit(solution)/shard_map/all_gather | solution.py:481
  258.8 2.7 half5.1
  261.5 20.4 %all_to_all.75.got_ref = f32[16,72,128]{2,1,0:T(8,128)S(1)} all-to-all(f32[16,72,128]{2,1,0:T(8,128)S(1)} %get-tuple-element.59), channel_id=1, replica_groups=mesh['zl'=4,'y'=4,'x'=4,'zh'=4,'core'=2] {'zl','y'}, dimensions={0} | all-to-all | bytes 1179648 | tf_op jit(solution)/shard_map/all_to_all | solution.py:471
  281.9 2.5 last.1
  284.4 14.7 %all_to_all.76.got_ref = f32[32,24,128]{2,1,0:T(8,128)S(1)} all-to-all(f32[32,24,128]{2,1,0:T(8,128)S(1)} %get-tuple-element.62), channel_id=1, replica_groups=mesh['zl'=4,'y'=4,'x'=4,'zh'=4,'core'=2] {'core','y','x'}, dimensions={0} | all-to-all | bytes 786432 | tf_op jit(solution)/shard_map/all_to_all | solution.py:471
  299.2 18.5 %all_to_all.77.got_ref = f32[16,24,128]{2,1,0:T(8,128)S(1)} all-to-all(f32[16,24,128]{2,1,0:T(8,128)S(1)} %fold.17), channel_id=1, replica_groups=mesh['zl'=4,'y'=4,'x'=4,'zh'=4,'core'=2] {'zh','zl'}, dimensions={0} | all-to-all | bytes 393216 | tf_op jit(solution)/shard_map/all_to_all | solution.py:471
  317.7 2.6 end.1
  (18 shorter events, 2.3 us)
Async XLA Ops:
  0.6 22.4 %copy-start = (bf16[1,1,32,128,128]{4,3,2,1,0:T(8,128)(2,1)S(1)}, bf16[1,1,32,128,128]{4,3,2,1,0:T(8,128)(2,1)}, u32[]{:S(2)}) copy-start(bf16[1,1,32,128,128]{4,3,2,1,0:T(8,128)(2,1)} %param.6) | copy-start | bytes 3145732
  0.6 0.8 copy-start.1
  2.4 20.6 %all-to-all-start = ((f32[16,48,128]{2,1,0:T(8,128)}), f32[16,48,128]{2,1,0:T(8,128)S(1)}, u32[]{:S(2)}, u32[]{:S(2)}) async-start(f32[16,48,128]{2,1,0:T(8,128)} %pack.1), calls=%async_computation | async-start | bytes 786432 | tf_op jit(solution)/shard_map/all_to_all | solution.py:471
  12.3 0.8 copy-start.2
  12.3 0.7 copy-start.4
  65.7 3.5 %copy-start.3 = (s32[2048]{0:T(1024)S(1)}, s32[2048]{0:T(1024)}, u32[]{:S(2)}) copy-start(s32[2048]{0:T(1024)} %param.9) | copy-start | bytes 24580
  65.7 9.0 %all-to-all-start.2 = ((f32[4,128,128]{2,1,0:T(8,128)}), f32[4,128,128]{2,1,0:T(8,128)S(1)}, u32[]{:S(2)}, u32[]{:S(2)}) async-start(f32[4,128,128]{2,1,0:T(8,128)} %fold.10), calls=%async_computation.2 | async-start | bytes 524288 | tf_op jit(solution)/shard_map/all_to_all | solution.py:471
  102.3 15.7 %all-to-all-start.4 = ((f32[16,48,128]{2,1,0:T(8,128)}), f32[16,48,128]{2,1,0:T(8,128)S(1)}, u32[]{:S(2)}, u32[]{:S(2)}) async-start(f32[16,48,128]{2,1,0:T(8,128)} %get-tuple-element.39), calls=%async_computation.4 | async-start | bytes 786432 | tf_op jit(solution)/shard_map/all_to_all | solution.py:471
  107.3 4.5 %collective-permute-start = (f32[16,128]{1,0:T(8,128)S(1)}, f32[16,128]{1,0:T(8,128)S(1)}, u32[]{:S(2)}, u32[]{:S(2)}) collective-permute-start(f32[16,128]{1,0:T(8,128)S(1)} %get-tuple-element.40.refs_1_), channel_id=1, source_target_pairs={{0,1},{1,0},{2,3},{3,2},{4,5},{5,4},{6,7},{7,6},{8,9},{9,8},{10,11... | collective-permute-start | bytes 24584 | tf_op jit(solution)/shard_map/ppermute | solution.py:489
  153.9 8.9 %all-to-all-start.6 = ((f32[4,128,128]{2,1,0:T(8,128)}), f32[4,128,128]{2,1,0:T(8,128)S(1)}, u32[]{:S(2)}, u32[]{:S(2)}) async-start(f32[4,128,128]{2,1,0:T(8,128)} %fold.13), calls=%async_computation.6 | async-start | bytes 524288 | tf_op jit(solution)/shard_map/all_to_all | solution.py:471
  190.9 15.7 %all-to-all-start.8 = ((f32[16,48,128]{2,1,0:T(8,128)}), f32[16,48,128]{2,1,0:T(8,128)S(1)}, u32[]{:S(2)}, u32[]{:S(2)}) async-start(f32[16,48,128]{2,1,0:T(8,128)} %get-tuple-element.49), calls=%async_computation.8 | async-start | bytes 786432 | tf_op jit(solution)/shard_map/all_to_all | solution.py:471
  195.8 4.5 %collective-permute-start.1 = (f32[16,128]{1,0:T(8,128)S(1)}, f32[16,128]{1,0:T(8,128)S(1)}, u32[]{:S(2)}, u32[]{:S(2)}) collective-permute-start(f32[16,128]{1,0:T(8,128)S(1)} %get-tuple-element.50.refs_1_), channel_id=1, source_target_pairs={{0,1},{1,0},{2,3},{3,2},{4,5},{5,4},{6,7},{7,6},{8,9},{9,8},{10,11... | collective-permute-start | bytes 24584 | tf_op jit(solution)/shard_map/ppermute | solution.py:489
  242.3 8.9 %all-to-all-start.10 = ((f32[4,128,128]{2,1,0:T(8,128)}), f32[4,128,128]{2,1,0:T(8,128)S(1)}, u32[]{:S(2)}, u32[]{:S(2)}) async-start(f32[4,128,128]{2,1,0:T(8,128)} %fold.16), calls=%async_computation.10 | async-start | bytes 524288 | tf_op jit(solution)/shard_map/all_to_all | solution.py:471

commit v9 on v8

--- a/solution.py
+++ b/solution.py
@@ -15,6 +15,8 @@
 GRAM_ROWS = 24
 HALF_ROWS = 16
 UNIT = 32
+COUNT_AT, CORE_AT, COL_AT, ROW_AT, SLOTS_AT = range(5)
+TABLE = 128
 HIGH = lax.Precision.HIGHEST
 
 ROW = ("zl", "y")
@@ -104,8 +106,7 @@
 
 
 def product(table_ref, tiles_ref, parts_ref, sums_ref, forward, cb):
-    slot_count = tiles_ref.shape[0]
-    count = table_ref[slot_count]
+    count = table_ref[COUNT_AT]
     spare = sums_ref.shape[0] // BLOCK - 1
     group = 16
 
@@ -113,7 +114,7 @@
         added = []
         for g in range(group):
             t = step * group + g
-            slot = table_ref[t]
+            slot = table_ref[SLOTS_AT + t]
             local_row = slot // cb
             local_col = slot - local_row * cb
             source, target = (
@@ -160,7 +161,7 @@
 
 
 def send_panel(
-    table_ref, tiles_ref, panel_ref, scale_ref, sent_ref, parts_ref, sums_ref, *, forward, cb, ready=None,
+    table_ref, tiles_ref, panel_ref, scale_ref, sent_ref, parts_ref, sums_ref, *, forward, cb, ready=(),
     owned=False,
 ):
     sums_ref[...] = jnp.zeros_like(sums_ref)
@@ -171,14 +172,14 @@
         parts_ref[192 * b : 192 * b + 192, :] = jnp.concatenate(
             split_three(value * scale_ref[b : b + 1, :]), axis=0
         )
-    if ready is not None:
-        ready.wait()
+    for copy in ready:
+        copy.wait()
     product(table_ref, tiles_ref, parts_ref, sums_ref, forward, cb)
     packed = pack_gram(whole_gram(gram))
     if not (forward or owned):
         cross = packed[HALF_ROWS:]
         packed = jnp.where(
-            table_ref[tiles_ref.shape[0] + 1] == 0, packed[:HALF_ROWS], jnp.concatenate([cross, cross], axis=0)
+            table_ref[CORE_AT] == 0, packed[:HALF_ROWS], jnp.concatenate([cross, cross], axis=0)
         )
     count = sent_ref.shape[0]
     rows = (sums_ref.shape[0] - BLOCK) // count
@@ -241,11 +242,13 @@
 
 
 def start_kernel(
-    table_ref, tiles_ref, got_ref, scale_ref, panel_ref, sent_ref,
-    parts_ref, sums_ref, near_tiles_ref, sem, *, cb, units,
+    far_table_ref, tiles_ref, got_ref, scale_ref, panel_ref, sent_ref,
+    parts_ref, sums_ref, near_tiles_ref, sem, table_ref, table_sem, *, cb, units,
 ):
     copy = pltpu.make_async_copy(tiles_ref, near_tiles_ref, sem)
     copy.start()
+    table_copy = pltpu.make_async_copy(far_table_ref, table_ref, table_sem)
+    table_copy.start()
     rows = got_ref.shape[1]
     for b in range(cb):
         found = []
@@ -263,7 +266,7 @@
             )
     send_panel(
         table_ref, near_tiles_ref, panel_ref, scale_ref, sent_ref, parts_ref, sums_ref,
-        forward=True, cb=cb, ready=copy,
+        forward=True, cb=cb, ready=(copy, table_copy),
     )
 
 
@@ -289,7 +292,7 @@
 
 
 def join_gram(table_ref, own_ref, other_ref):
-    first = table_ref[table_ref.shape[0] - 3] == 0
+    first = table_ref[CORE_AT] == 0
     own, other = own_ref[...], other_ref[...]
     return unpack_gram(
         jnp.concatenate(
@@ -335,7 +338,7 @@
         table_ref, items_ref, scale_ref = refs[3:6]
         own_items_ref, own_scale_ref = refs[-2:]
         width = own_items_ref.shape[1]
-        start = (width // UNIT) * table_ref[table_ref.shape[0] - 1]
+        start = (width // UNIT) * table_ref[ROW_AT]
         own_items_ref[...] = cut(items_ref, BLOCK, start, width)
         own_scale_ref[...] = cut(scale_ref, 1, start, width)
         refs = refs[:3] + refs[6:-2]
@@ -370,8 +373,11 @@
 
 def step_kernel(*refs, forward, cb, with_old, owned):
     refs = list(refs)
-    table_ref, tiles_ref, got_ref, scale_ref, factor_ref = refs[:5]
-    refs = refs[5:]
+    far_table_ref, tiles_ref, got_ref, scale_ref, factor_ref = refs[:5]
+    table_ref, table_sem = refs[-2:]
+    refs = refs[5:-2]
+    table_copy = pltpu.make_async_copy(far_table_ref, table_ref, table_sem)
+    table_copy.start()
     if with_old:
         part_ref, refs = refs[0], refs[1:]
     if owned:
@@ -390,11 +396,11 @@
         panel_ref[where, :] = value
     send_panel(
         table_ref, tiles_ref, panel_ref, scale_ref, sent_ref, parts_ref, sums_ref,
-        forward=forward, cb=cb, owned=owned,
+        forward=forward, cb=cb, owned=owned, ready=(table_copy,),
     )
     if owned:
         width = own_ref.shape[1]
-        start = (width // UNIT) * table_ref[table_ref.shape[0] - 2]
+        start = (width // UNIT) * table_ref[COL_AT]
         own_ref[...] = cut(panel_ref, BLOCK, start, width)
 
 
@@ -446,6 +452,7 @@
 
 SMEM = pl.BlockSpec(memory_space=pltpu.SMEM)
 VMEM = pl.BlockSpec(memory_space=pltpu.VMEM)
+FAR = pl.BlockSpec(memory_space=pltpu.HBM)
 PARAMS = pltpu.CompilerParams(vmem_limit_bytes=8 * 1024 * 1024)
 
 
@@ -499,7 +506,8 @@
     core = lax.axis_index("core").astype(jnp.int32).reshape(1)
     col = lax.axis_index(COL).astype(jnp.int32).reshape(1)
     row = lax.axis_index(ROW).astype(jnp.int32).reshape(1)
-    table = jnp.concatenate([tile_slots[0, 0], tile_counts[0], core, col, row])
+    table = jnp.concatenate([tile_counts[0], core, col, row, tile_slots[0, 0]])
+    table = jnp.pad(table, (0, TABLE - table.shape[0]))
     user_scale = lax.rsqrt(user_degree.astype(jnp.float32)).reshape(rb, TILE)
     item_scale = lax.rsqrt(item_degree.astype(jnp.float32)).reshape(cb, TILE)
 
@@ -521,16 +529,18 @@
     item_sums = pltpu.VMEM((cb * BLOCK + BLOCK, TILE), jnp.float32)
     user_parts = pltpu.VMEM((rb * 192, TILE), jnp.bfloat16)
     item_parts = pltpu.VMEM((cb * 192, TILE), jnp.bfloat16)
+    near_table = [pltpu.SMEM((TABLE,), jnp.int32), pltpu.SemaphoreType.DMA]
     start, sent = pl.pallas_call(
         functools.partial(start_kernel, cb=cb, units=units),
         out_shape=[f32(cb * BLOCK, TILE), user_messages],
-        in_specs=[SMEM, pl.BlockSpec(memory_space=pltpu.HBM), VMEM, VMEM],
+        in_specs=[FAR, FAR, VMEM, VMEM],
         out_specs=[VMEM, VMEM],
         scratch_shapes=[
             item_parts,
             user_sums,
             pltpu.VMEM(tile_stack.shape, tile_stack.dtype),
             pltpu.SemaphoreType.DMA,
+            *near_table,
         ],
         compiler_params=PARAMS,
         name="start",
@@ -582,9 +592,9 @@
                 step_kernel, forward=not users, cb=cb, with_old=with_old, owned=owned
             ),
             out_shape=shapes,
-            in_specs=[SMEM, VMEM] + [VMEM] * len(operands),
+            in_specs=[FAR, VMEM] + [VMEM] * len(operands),
             out_specs=[VMEM, VMEM],
-            scratch_shapes=scratch,
+            scratch_shapes=[*scratch, *near_table],
             compiler_params=PARAMS,
             name=f"half{half}",
         )(table, tile_stack, *operands)

time: 325 us -> 322 us (level)
  no operation moved by 1% of the time
where the time goes in v9:
time: 322 us; the launch traced here: 317 us
  blocking collectives  218 us (68%)
  starting transfers between devices  37 us (11%)
  Pallas kernels  31.9 us (10%)
  waiting for transfers between devices  27.4 us (9%)
    all_to_all x8, blocking collectives, exchange(): return lax.all_to_all(messages, axes, 0, 0, tiled=True)  138 us
    all_gather x3, blocking collectives, sum_col(): got = lax.all_gather(own, 'zh', axis=0, tiled=False)  56.2 us
    all_to_all x6, starting transfers between devices, exchange(): return lax.all_to_all(messages, axes, 0, 0, tiled=True)  29.4 us
    all_to_all x6, waiting for transfers between devices, exchange(): return lax.all_to_all(messages, axes, 0, 0, tiled=True)  26 us
    all_gather x3, blocking collectives, sum_col(): return ([got], lax.all_gather(half, 'core', axis=0, tiled=True))  23.5 us
    pallas_call x5, Pallas kernels, per_device(): pl.pallas_call(functools.partial(factor_kernel, with_old=with_old, halves...  12.9 us
    pallas_call x5, Pallas kernels, per_device(): pl.pallas_call(functools.partial(step_kernel, forward=not users, cb=cb, w...  7.74 us
    ppermute x2, starting transfers between devices, sum_row(): other = lax.ppermute(own, 'core', [(0, 1), (1, 0)])  7.56 us
  transfers between devices with their start and end apart: 8, of which 8 were waited for; matrix products, arithmetic and copies ran while one was open for 0% of the time, Pallas kernels for 4%

profile of v9, /device:TPU:1, one launch (start us, length us, event | category | flops | bytes accessed | tf_op | source)
XLA Modules:
  0.0 317.5 jit_solution(261565151711324642)
XLA Ops:
  0.7 0.8 copy-done.1
  1.5 0.9 pack.1
  2.4 9.2 %all-to-all-start = ((f32[16,48,128]{2,1,0:T(8,128)}), f32[16,48,128]{2,1,0:T(8,128)S(1)}, u32[]{:S(2)}, u32[]{:S(2)}) async-start(f32[16,48,128]{2,1,0:T(8,128)} %pack.1), calls=%async_computation | async-start | bytes 786432 | tf_op jit(solution)/shard_map/all_to_all | solution.py:478
  13.0 10.0 %all-to-all-done.got_ref = f32[16,48,128]{2,1,0:T(8,128)S(1)} async-done(((f32[16,48,128]{2,1,0:T(8,128)}), f32[16,48,128]{2,1,0:T(8,128)S(1)}, u32[]{:S(2)}, u32[]{:S(2)}) %all-to-all-start) | async-done | bytes 393248 | tf_op jit(solution)/shard_map/all_to_all | solution.py:478
  23.0 1.3 start.1
  24.3 17.5 %all_to_all.70.got_ref = f32[8,152,128]{2,1,0:T(8,128)S(1)} all-to-all(f32[8,152,128]{2,1,0:T(8,128)S(1)} %get-tuple-element.37), channel_id=1, replica_groups=mesh['zl'=4,'y'=4,'x'=4,'zh'=4,'core'=2] {'core','x'}, dimensions={0} | all-to-all | bytes 1245184 | tf_op jit(solution)/shard_map/all_to_all | solution.py:478
  41.8 22.7 %all_gather.18.got_ref.refs_0_ = f32[4,152,128]{2,1,0:T(8,128)S(1)} all-gather(f32[1,152,128]{2,1,0:T(8,128)S(1)} %fold.9), channel_id=1, replica_groups=mesh['zl'=4,'y'=4,'x'=4,'zh'=4,'core'=2] {'zh'}, dimensions={0}, use_global_device_ids=true | all-gather | bytes 389120 | tf_op jit(solution)/shard_map/all_gather | solution.py:484
  64.5 0.7 fold.10
  65.2 3.5 %all-to-all-start.2 = ((f32[4,128,128]{2,1,0:T(8,128)}), f32[4,128,128]{2,1,0:T(8,128)S(1)}, u32[]{:S(2)}, u32[]{:S(2)}) async-start(f32[4,128,128]{2,1,0:T(8,128)} %fold.10), calls=%async_computation.2 | async-start | bytes 524288 | tf_op jit(solution)/shard_map/all_to_all | solution.py:478
  68.8 1.7 factor1.1.refs_4_
  70.5 3.7 %all-to-all-done.2 = f32[4,128,128]{2,1,0:T(8,128)S(1)} async-done(((f32[4,128,128]{2,1,0:T(8,128)}), f32[4,128,128]{2,1,0:T(8,128)S(1)}, u32[]{:S(2)}, u32[]{:S(2)}) %all-to-all-start.2) | async-done | bytes 262176 | tf_op jit(solution)/shard_map/all_to_all | solution.py:478
  74.3 7.7 %all_gather.19.refs_2_ = f32[1024,128]{1,0:T(8,128)S(1)} all-gather(f32[512,128]{1,0:T(8,128)S(1)} %bitcast.26), channel_id=1, replica_groups=mesh['zl'=4,'y'=4,'x'=4,'zh'=4,'core'=2] {'core'}, dimensions={0}, use_global_device_ids=true | all-gather | bytes 786432 | tf_op jit(solution)/shard_map/all_gather | solution.py:488
  82.0 1.4 half1.1
  83.4 17.2 %all_to_all.71.got_ref = f32[16,64,128]{2,1,0:T(8,128)S(1)} all-to-all(f32[16,64,128]{2,1,0:T(8,128)S(1)} %get-tuple-element.38), channel_id=1, replica_groups=mesh['zl'=4,'y'=4,'x'=4,'zh'=4,'core'=2] {'zl','y'}, dimensions={0} | all-to-all | bytes 1048576 | tf_op jit(solution)/shard_map/all_to_all | solution.py:478
  100.6 0.8 fold.11
  101.4 4.9 %all-to-all-start.4 = ((f32[16,48,128]{2,1,0:T(8,128)}), f32[16,48,128]{2,1,0:T(8,128)S(1)}, u32[]{:S(2)}, u32[]{:S(2)}) async-start(f32[16,48,128]{2,1,0:T(8,128)} %get-tuple-element.39), calls=%async_computation.4 | async-start | bytes 786432 | tf_op jit(solution)/shard_map/all_to_all | solution.py:478
  106.4 3.7 %collective-permute-start = (f32[16,128]{1,0:T(8,128)S(1)}, f32[16,128]{1,0:T(8,128)S(1)}, u32[]{:S(2)}, u32[]{:S(2)}) collective-permute-start(f32[16,128]{1,0:T(8,128)S(1)} %get-tuple-element.40.refs_1_), channel_id=1, source_target_pairs={{0,1},{1,0},{2,3},{3,2},{4,5},{5,4},{6,7},{7,6},{8,9},{9,8},{10,11... | collective-permute-start | bytes 24584 | tf_op jit(solution)/shard_map/ppermute | solution.py:496
  110.1 0.8 collective-permute-done.refs_2_
  110.9 2.9 factor2.1
  113.8 3.4 %all-to-all-done.4 = f32[16,48,128]{2,1,0:T(8,128)S(1)} async-done(((f32[16,48,128]{2,1,0:T(8,128)}), f32[16,48,128]{2,1,0:T(8,128)S(1)}, u32[]{:S(2)}, u32[]{:S(2)}) %all-to-all-start.4) | async-done | bytes 393248 | tf_op jit(solution)/shard_map/all_to_all | solution.py:478
  117.1 1.4 half2.1
  118.5 16.4 %all_to_all.72.got_ref = f32[8,152,128]{2,1,0:T(8,128)S(1)} all-to-all(f32[8,152,128]{2,1,0:T(8,128)S(1)} %get-tuple-element.44), channel_id=1, replica_groups=mesh['zl'=4,'y'=4,'x'=4,'zh'=4,'core'=2] {'core','x'}, dimensions={0} | all-to-all | bytes 1245184 | tf_op jit(solution)/shard_map/all_to_all | solution.py:478
  134.9 16.8 %all_gather.20.got_ref.refs_0_ = f32[4,152,128]{2,1,0:T(8,128)S(1)} all-gather(f32[1,152,128]{2,1,0:T(8,128)S(1)} %fold.12), channel_id=1, replica_groups=mesh['zl'=4,'y'=4,'x'=4,'zh'=4,'core'=2] {'zh'}, dimensions={0}, use_global_device_ids=true | all-gather | bytes 389120 | tf_op jit(solution)/shard_map/all_gather | solution.py:484
  151.7 0.7 fold.13
  152.5 3.4 %all-to-all-start.6 = ((f32[4,128,128]{2,1,0:T(8,128)}), f32[4,128,128]{2,1,0:T(8,128)S(1)}, u32[]{:S(2)}, u32[]{:S(2)}) async-start(f32[4,128,128]{2,1,0:T(8,128)} %fold.13), calls=%async_computation.6 | async-start | bytes 524288 | tf_op jit(solution)/shard_map/all_to_all | solution.py:478
  155.9 2.4 factor3.1
  158.3 3.0 all-to-all-done.6
  161.4 7.6 %all_gather.21.refs_2_ = f32[1024,128]{1,0:T(8,128)S(1)} all-gather(f32[512,128]{1,0:T(8,128)S(1)} %bitcast.25), channel_id=1, replica_groups=mesh['zl'=4,'y'=4,'x'=4,'zh'=4,'core'=2] {'core'}, dimensions={0}, use_global_device_ids=true | all-gather | bytes 786432 | tf_op jit(solution)/shard_map/all_gather | solution.py:488
  169.0 1.4 half3.1
  170.4 17.8 %all_to_all.73.got_ref = f32[16,64,128]{2,1,0:T(8,128)S(1)} all-to-all(f32[16,64,128]{2,1,0:T(8,128)S(1)} %get-tuple-element.48), channel_id=1, replica_groups=mesh['zl'=4,'y'=4,'x'=4,'zh'=4,'core'=2] {'zl','y'}, dimensions={0} | all-to-all | bytes 1048576 | tf_op jit(solution)/shard_map/all_to_all | solution.py:478
  188.2 0.8 fold.14
  189.0 4.9 %all-to-all-start.8 = ((f32[16,48,128]{2,1,0:T(8,128)}), f32[16,48,128]{2,1,0:T(8,128)S(1)}, u32[]{:S(2)}, u32[]{:S(2)}) async-start(f32[16,48,128]{2,1,0:T(8,128)} %get-tuple-element.49), calls=%async_computation.8 | async-start | bytes 786432 | tf_op jit(solution)/shard_map/all_to_all | solution.py:478
  193.9 3.9 %collective-permute-start.1 = (f32[16,128]{1,0:T(8,128)S(1)}, f32[16,128]{1,0:T(8,128)S(1)}, u32[]{:S(2)}, u32[]{:S(2)}) collective-permute-start(f32[16,128]{1,0:T(8,128)S(1)} %get-tuple-element.50.refs_1_), channel_id=1, source_target_pairs={{0,1},{1,0},{2,3},{3,2},{4,5},{5,4},{6,7},{7,6},{8,9},{9,8},{10,11... | collective-permute-start | bytes 24584 | tf_op jit(solution)/shard_map/ppermute | solution.py:496
  198.4 2.9 factor4.1
  201.3 3.4 %all-to-all-done.8 = f32[16,48,128]{2,1,0:T(8,128)S(1)} async-done(((f32[16,48,128]{2,1,0:T(8,128)}), f32[16,48,128]{2,1,0:T(8,128)S(1)}, u32[]{:S(2)}, u32[]{:S(2)}) %all-to-all-start.8) | async-done | bytes 393248 | tf_op jit(solution)/shard_map/all_to_all | solution.py:478
  204.7 1.4 half4.1
  206.1 16.4 %all_to_all.74.got_ref = f32[8,152,128]{2,1,0:T(8,128)S(1)} all-to-all(f32[8,152,128]{2,1,0:T(8,128)S(1)} %get-tuple-element.54), channel_id=1, replica_groups=mesh['zl'=4,'y'=4,'x'=4,'zh'=4,'core'=2] {'core','x'}, dimensions={0} | all-to-all | bytes 1245184 | tf_op jit(solution)/shard_map/all_to_all | solution.py:478
  222.5 16.7 %all_gather.22.got_ref.refs_0_ = f32[4,152,128]{2,1,0:T(8,128)S(1)} all-gather(f32[1,152,128]{2,1,0:T(8,128)S(1)} %fold.15), channel_id=1, replica_groups=mesh['zl'=4,'y'=4,'x'=4,'zh'=4,'core'=2] {'zh'}, dimensions={0}, use_global_device_ids=true | all-gather | bytes 389120 | tf_op jit(solution)/shard_map/all_gather | solution.py:484
  239.9 3.4 %all-to-all-start.10 = ((f32[4,128,128]{2,1,0:T(8,128)}), f32[4,128,128]{2,1,0:T(8,128)S(1)}, u32[]{:S(2)}, u32[]{:S(2)}) async-start(f32[4,128,128]{2,1,0:T(8,128)} %fold.16), calls=%async_computation.10 | async-start | bytes 524288 | tf_op jit(solution)/shard_map/all_to_all | solution.py:478
  243.3 3.0 factor5.1
  246.3 2.5 all-to-all-done.10
  248.8 8.1 %all_gather.23.refs_2_ = f32[1024,128]{1,0:T(8,128)S(1)} all-gather(f32[512,128]{1,0:T(8,128)S(1)} %bitcast.24), channel_id=1, replica_groups=mesh['zl'=4,'y'=4,'x'=4,'zh'=4,'core'=2] {'core'}, dimensions={0}, use_global_device_ids=true | all-gather | bytes 786432 | tf_op jit(solution)/shard_map/all_gather | solution.py:488
  256.9 2.2 half5.1
  259.1 19.9 %all_to_all.75.got_ref = f32[16,72,128]{2,1,0:T(8,128)S(1)} all-to-all(f32[16,72,128]{2,1,0:T(8,128)S(1)} %get-tuple-element.59), channel_id=1, replica_groups=mesh['zl'=4,'y'=4,'x'=4,'zh'=4,'core'=2] {'zl','y'}, dimensions={0} | all-to-all | bytes 1179648 | tf_op jit(solution)/shard_map/all_to_all | solution.py:478
  279.0 2.5 last.1
  281.5 14.7 %all_to_all.76.got_ref = f32[32,24,128]{2,1,0:T(8,128)S(1)} all-to-all(f32[32,24,128]{2,1,0:T(8,128)S(1)} %get-tuple-element.62), channel_id=1, replica_groups=mesh['zl'=4,'y'=4,'x'=4,'zh'=4,'core'=2] {'core','y','x'}, dimensions={0} | all-to-all | bytes 786432 | tf_op jit(solution)/shard_map/all_to_all | solution.py:478
  296.3 18.5 %all_to_all.77.got_ref = f32[16,24,128]{2,1,0:T(8,128)S(1)} all-to-all(f32[16,24,128]{2,1,0:T(8,128)S(1)} %fold.17), channel_id=1, replica_groups=mesh['zl'=4,'y'=4,'x'=4,'zh'=4,'core'=2] {'zh','zl'}, dimensions={0} | all-to-all | bytes 393216 | tf_op jit(solution)/shard_map/all_to_all | solution.py:478
  314.8 2.6 end.1
  (19 shorter events, 2.3 us)
Async XLA Ops:
  0.6 22.4 %copy-start = (bf16[1,1,32,128,128]{4,3,2,1,0:T(8,128)(2,1)S(1)}, bf16[1,1,32,128,128]{4,3,2,1,0:T(8,128)(2,1)}, u32[]{:S(2)}) copy-start(bf16[1,1,32,128,128]{4,3,2,1,0:T(8,128)(2,1)} %param.6) | copy-start | bytes 3145732
  0.6 0.8 copy-start.1
  2.4 20.6 %all-to-all-start = ((f32[16,48,128]{2,1,0:T(8,128)}), f32[16,48,128]{2,1,0:T(8,128)S(1)}, u32[]{:S(2)}, u32[]{:S(2)}) async-start(f32[16,48,128]{2,1,0:T(8,128)} %pack.1), calls=%async_computation | async-start | bytes 786432 | tf_op jit(solution)/shard_map/all_to_all | solution.py:478
  12.3 0.8 copy-start.2
  12.3 0.7 copy-start.4
  65.2 3.5 %copy-start.3 = (s32[2048]{0:T(1024)S(1)}, s32[2048]{0:T(1024)}, u32[]{:S(2)}) copy-start(s32[2048]{0:T(1024)} %param.9) | copy-start | bytes 24580
  65.2 9.0 %all-to-all-start.2 = ((f32[4,128,128]{2,1,0:T(8,128)}), f32[4,128,128]{2,1,0:T(8,128)S(1)}, u32[]{:S(2)}, u32[]{:S(2)}) async-start(f32[4,128,128]{2,1,0:T(8,128)} %fold.10), calls=%async_computation.2 | async-start | bytes 524288 | tf_op jit(solution)/shard_map/all_to_all | solution.py:478
  101.4 15.7 %all-to-all-start.4 = ((f32[16,48,128]{2,1,0:T(8,128)}), f32[16,48,128]{2,1,0:T(8,128)S(1)}, u32[]{:S(2)}, u32[]{:S(2)}) async-start(f32[16,48,128]{2,1,0:T(8,128)} %get-tuple-element.39), calls=%async_computation.4 | async-start | bytes 786432 | tf_op jit(solution)/shard_map/all_to_all | solution.py:478
  106.4 4.5 %collective-permute-start = (f32[16,128]{1,0:T(8,128)S(1)}, f32[16,128]{1,0:T(8,128)S(1)}, u32[]{:S(2)}, u32[]{:S(2)}) collective-permute-start(f32[16,128]{1,0:T(8,128)S(1)} %get-tuple-element.40.refs_1_), channel_id=1, source_target_pairs={{0,1},{1,0},{2,3},{3,2},{4,5},{5,4},{6,7},{7,6},{8,9},{9,8},{10,11... | collective-permute-start | bytes 24584 | tf_op jit(solution)/shard_map/ppermute | solution.py:496
  152.5 8.9 %all-to-all-start.6 = ((f32[4,128,128]{2,1,0:T(8,128)}), f32[4,128,128]{2,1,0:T(8,128)S(1)}, u32[]{:S(2)}, u32[]{:S(2)}) async-start(f32[4,128,128]{2,1,0:T(8,128)} %fold.13), calls=%async_computation.6 | async-start | bytes 524288 | tf_op jit(solution)/shard_map/all_to_all | solution.py:478
  189.0 15.7 %all-to-all-start.8 = ((f32[16,48,128]{2,1,0:T(8,128)}), f32[16,48,128]{2,1,0:T(8,128)S(1)}, u32[]{:S(2)}, u32[]{:S(2)}) async-start(f32[16,48,128]{2,1,0:T(8,128)} %get-tuple-element.49), calls=%async_computation.8 | async-start | bytes 786432 | tf_op jit(solution)/shard_map/all_to_all | solution.py:478
  193.9 4.5 %collective-permute-start.1 = (f32[16,128]{1,0:T(8,128)S(1)}, f32[16,128]{1,0:T(8,128)S(1)}, u32[]{:S(2)}, u32[]{:S(2)}) collective-permute-start(f32[16,128]{1,0:T(8,128)S(1)} %get-tuple-element.50.refs_1_), channel_id=1, source_target_pairs={{0,1},{1,0},{2,3},{3,2},{4,5},{5,4},{6,7},{7,6},{8,9},{9,8},{10,11... | collective-permute-start | bytes 24584 | tf_op jit(solution)/shard_map/ppermute | solution.py:496
  239.9 8.9 %all-to-all-start.10 = ((f32[4,128,128]{2,1,0:T(8,128)}), f32[4,128,128]{2,1,0:T(8,128)S(1)}, u32[]{:S(2)}, u32[]{:S(2)}) async-start(f32[4,128,128]{2,1,0:T(8,128)} %fold.16), calls=%async_computation.10 | async-start | bytes 524288 | tf_op jit(solution)/shard_map/all_to_all | solution.py:478

commit v10 on v9

--- a/solution.py
+++ b/solution.py
@@ -26,31 +26,18 @@
 LINE = ("zh", "zl")
 
 
-def pack_gram(gram):
+def flat_rows(block):
+    return jnp.concatenate([block[8 * i : 8 * i + 8] for i in range(4)], axis=1)
+
+
+def square_block(rows):
     half = BLOCK // 2
-
-    def rows(block):
-        return jnp.concatenate([block[8 * i : 8 * i + 8] for i in range(4)], axis=1)
-
     return jnp.concatenate(
-        [
-            rows(gram[:half, :half]),
-            rows(gram[half:, half:]),
-            rows(gram[half:, :half]),
-        ],
-        axis=0,
-    )
-
-
-def unpack_gram(packed):
-    half = BLOCK // 2
-
-    def block(rows):
-        return jnp.concatenate(
-            [rows[:, half * i : half * i + half] for i in range(4)], axis=0
-        )
-
-    upper, lower, cross = (block(packed[8 * i : 8 * i + 8]) for i in range(3))
+        [rows[:, half * i : half * i + half] for i in range(4)], axis=0
+    )
+
+
+def symmetric(upper, lower, cross):
     return jnp.concatenate(
         [
             jnp.concatenate([upper, jnp.transpose(cross)], axis=1),
@@ -58,6 +45,16 @@
         ],
         axis=0,
     )
+
+
+def pack_gram(gram):
+    half = BLOCK // 2
+    blocks = gram[:half, :half], gram[half:, half:], gram[half:, :half]
+    return jnp.concatenate([flat_rows(block) for block in blocks], axis=0)
+
+
+def unpack_gram(packed):
+    return symmetric(*(square_block(packed[8 * i : 8 * i + 8]) for i in range(3)))
 
 
 def factor_rows(gram, out_ref):
@@ -175,8 +172,12 @@
     for copy in ready:
         copy.wait()
     product(table_ref, tiles_ref, parts_ref, sums_ref, forward, cb)
-    packed = pack_gram(whole_gram(gram))
-    if not (forward or owned):
+    gram = whole_gram(gram)
+    if owned:
+        send_owned(sums_ref, gram, sent_ref)
+        return
+    packed = pack_gram(gram)
+    if not forward:
         cross = packed[HALF_ROWS:]
         packed = jnp.where(
             table_ref[CORE_AT] == 0, packed[:HALF_ROWS], jnp.concatenate([cross, cross], axis=0)
@@ -184,21 +185,26 @@
     count = sent_ref.shape[0]
     rows = (sums_ref.shape[0] - BLOCK) // count
     for k in range(count):
-        if owned:
-            per_block = TILE // UNIT
-            units = rows * per_block // BLOCK
-            sent_ref[k, :rows, :] = pack_units(
-                [
-                    sums_ref[
-                        BLOCK * (u // per_block) : BLOCK * (u // per_block) + BLOCK,
-                        UNIT * (u % per_block) : UNIT * (u % per_block) + UNIT,
-                    ]
-                    for u in range(units * k, units * k + units)
-                ]
+        sent_ref[k, :rows, :] = sums_ref[rows * k : rows * k + rows, :]
+        sent_ref[k, rows:, :] = packed
+
+
+def send_owned(sums_ref, gram, sent_ref):
+    half = BLOCK // 2
+    side = jnp.concatenate([gram[:half, :half], gram[half:, half:]], axis=0)
+    cross = flat_rows(gram[half:, :half])
+    width = TILE - half
+    for k in range(sent_ref.shape[0]):
+        pieces, at = [], width * k
+        while at < width * k + width:
+            block, lane = divmod(at, TILE)
+            lanes = min(TILE - lane, width * k + width - at)
+            pieces.append(
+                sums_ref[BLOCK * block : BLOCK * block + BLOCK, lane : lane + lanes]
             )
-        else:
-            sent_ref[k, :rows, :] = sums_ref[rows * k : rows * k + rows, :]
-        sent_ref[k, rows:, :] = packed
+            at += lanes
+        sent_ref[k, :BLOCK, :] = jnp.concatenate([*pieces, side], axis=1)
+        sent_ref[k, BLOCK:, :] = cross
 
 
 def unit_rows(unit, rows):
@@ -216,18 +222,6 @@
     return jnp.concatenate(
         [jnp.concatenate(pieces, axis=0) for pieces in columns], axis=1
     )
-
-
-def unpack_units(packed):
-    rows = packed.shape[0]
-    units = []
-    for unit in range(rows * TILE // (BLOCK * UNIT)):
-        pieces = [
-            packed[row : row + 16, lane : lane + UNIT]
-            for row, lane in unit_rows(unit, rows)
-        ]
-        units.append(jnp.concatenate(pieces, axis=0))
-    return jnp.concatenate(units, axis=1)
 
 
 def pack_kernel(panel_ref, out_ref):
@@ -405,12 +399,16 @@
 
 
 def last_kernel(got_ref, old_ref, old_factor_ref, scale_ref, factor_ref, panel_ref, sent_ref):
-    rows = got_ref.shape[1] - GRAM_ROWS
-    total = got_ref[0, :rows, :]
+    total = got_ref[0]
     for k in range(1, got_ref.shape[0]):
-        total += got_ref[k, :rows, :]
-    value = unpack_units(total) * scale_ref[...]
-    factor_rows(sum_gram(got_ref), factor_ref)
+        total += got_ref[k]
+    half = BLOCK // 2
+    width = TILE - half
+    value = total[:BLOCK, :width] * scale_ref[...]
+    gram = symmetric(
+        total[:half, width:], total[half:BLOCK, width:], square_block(total[BLOCK:])
+    )
+    factor_rows(gram, factor_ref)
     weights = jnp.concatenate(
         [factor_ref[:, BLOCK:], backward_weights(factor_ref, old_factor_ref)], axis=1
     )
@@ -524,7 +522,7 @@
 
     user_messages = f32(near, rb * BLOCK // near + GRAM_ROWS, TILE)
     item_messages = f32(rows, cb * BLOCK // rows + HALF_ROWS, TILE)
-    owned_messages = f32(rows, cb * BLOCK // rows + GRAM_ROWS, TILE)
+    owned_messages = f32(rows, BLOCK + GRAM_ROWS - HALF_ROWS, TILE)
     user_sums = pltpu.VMEM((rb * BLOCK + BLOCK, TILE), jnp.float32)
     item_sums = pltpu.VMEM((cb * BLOCK + BLOCK, TILE), jnp.float32)
     user_parts = pltpu.VMEM((rb * 192, TILE), jnp.bfloat16)

time: 322 us -> 322 us (level)
  no operation moved by 1% of the time
where the time goes in v10:
time: 322 us; the launch traced here: 317 us
  blocking collectives  218 us (68%)
  starting transfers between devices  37 us (11%)
  Pallas kernels  31.3 us (10%)
  waiting for transfers between devices  27.4 us (9%)
    all_to_all x8, blocking collectives, exchange(): return lax.all_to_all(messages, axes, 0, 0, tiled=True)  139 us
    all_gather x3, blocking collectives, sum_col(): got = lax.all_gather(own, 'zh', axis=0, tiled=False)  56.8 us
    all_to_all x6, starting transfers between devices, exchange(): return lax.all_to_all(messages, axes, 0, 0, tiled=True)  29.4 us
    all_to_all x6, waiting for transfers between devices, exchange(): return lax.all_to_all(messages, axes, 0, 0, tiled=True)  26 us
    all_gather x3, blocking collectives, sum_col(): return ([got], lax.all_gather(half, 'core', axis=0, tiled=True))  22.6 us
    pallas_call x5, Pallas kernels, per_device(): pl.pallas_call(functools.partial(factor_kernel, with_old=with_old, halves...  12.9 us
    ppermute x2, starting transfers between devices, sum_row(): other = lax.ppermute(own, 'core', [(0, 1), (1, 0)])  7.57 us
    pallas_call x5, Pallas kernels, per_device(): pl.pallas_call(functools.partial(step_kernel, forward=not users, cb=cb, w...  7.18 us
  transfers between devices with their start and end apart: 8, of which 8 were waited for; matrix products, arithmetic and copies ran while one was open for 0% of the time, Pallas kernels for 4%

profile of v10, /device:TPU:1, one launch (start us, length us, event | category | flops | bytes accessed | tf_op | source)
XLA Modules:
  0.0 316.8 jit_solution(9617150538090973780)
XLA Ops:
  0.7 0.8 copy-done.1
  1.5 0.9 pack.1
  2.4 9.2 %all-to-all-start = ((f32[16,48,128]{2,1,0:T(8,128)}), f32[16,48,128]{2,1,0:T(8,128)S(1)}, u32[]{:S(2)}, u32[]{:S(2)}) async-start(f32[16,48,128]{2,1,0:T(8,128)} %pack.1), calls=%async_computation | async-start | bytes 786432 | tf_op jit(solution)/shard_map/all_to_all | solution.py:476
  13.0 10.0 %all-to-all-done.got_ref = f32[16,48,128]{2,1,0:T(8,128)S(1)} async-done(((f32[16,48,128]{2,1,0:T(8,128)}), f32[16,48,128]{2,1,0:T(8,128)S(1)}, u32[]{:S(2)}, u32[]{:S(2)}) %all-to-all-start) | async-done | bytes 393248 | tf_op jit(solution)/shard_map/all_to_all | solution.py:476
  23.0 1.3 start.1
  24.3 17.5 %all_to_all.70.got_ref = f32[8,152,128]{2,1,0:T(8,128)S(1)} all-to-all(f32[8,152,128]{2,1,0:T(8,128)S(1)} %get-tuple-element.37), channel_id=1, replica_groups=mesh['zl'=4,'y'=4,'x'=4,'zh'=4,'core'=2] {'core','x'}, dimensions={0} | all-to-all | bytes 1245184 | tf_op jit(solution)/shard_map/all_to_all | solution.py:476
  41.8 23.0 %all_gather.18.got_ref.refs_0_ = f32[4,152,128]{2,1,0:T(8,128)S(1)} all-gather(f32[1,152,128]{2,1,0:T(8,128)S(1)} %fold.9), channel_id=1, replica_groups=mesh['zl'=4,'y'=4,'x'=4,'zh'=4,'core'=2] {'zh'}, dimensions={0}, use_global_device_ids=true | all-gather | bytes 389120 | tf_op jit(solution)/shard_map/all_gather | solution.py:482
  64.8 0.7 fold.10
  65.5 3.5 %all-to-all-start.2 = ((f32[4,128,128]{2,1,0:T(8,128)}), f32[4,128,128]{2,1,0:T(8,128)S(1)}, u32[]{:S(2)}, u32[]{:S(2)}) async-start(f32[4,128,128]{2,1,0:T(8,128)} %fold.10), calls=%async_computation.2 | async-start | bytes 524288 | tf_op jit(solution)/shard_map/all_to_all | solution.py:476
  69.1 1.7 factor1.1.refs_4_
  70.8 3.7 %all-to-all-done.2 = f32[4,128,128]{2,1,0:T(8,128)S(1)} async-done(((f32[4,128,128]{2,1,0:T(8,128)}), f32[4,128,128]{2,1,0:T(8,128)S(1)}, u32[]{:S(2)}, u32[]{:S(2)}) %all-to-all-start.2) | async-done | bytes 262176 | tf_op jit(solution)/shard_map/all_to_all | solution.py:476
  74.5 7.5 %all_gather.19.refs_2_ = f32[1024,128]{1,0:T(8,128)S(1)} all-gather(f32[512,128]{1,0:T(8,128)S(1)} %bitcast.26), channel_id=1, replica_groups=mesh['zl'=4,'y'=4,'x'=4,'zh'=4,'core'=2] {'core'}, dimensions={0}, use_global_device_ids=true | all-gather | bytes 786432 | tf_op jit(solution)/shard_map/all_gather | solution.py:486
  82.0 1.4 half1.1
  83.4 17.1 %all_to_all.71.got_ref = f32[16,64,128]{2,1,0:T(8,128)S(1)} all-to-all(f32[16,64,128]{2,1,0:T(8,128)S(1)} %get-tuple-element.38), channel_id=1, replica_groups=mesh['zl'=4,'y'=4,'x'=4,'zh'=4,'core'=2] {'zl','y'}, dimensions={0} | all-to-all | bytes 1048576 | tf_op jit(solution)/shard_map/all_to_all | solution.py:476
  100.5 0.8 fold.11
  101.3 4.9 %all-to-all-start.4 = ((f32[16,48,128]{2,1,0:T(8,128)}), f32[16,48,128]{2,1,0:T(8,128)S(1)}, u32[]{:S(2)}, u32[]{:S(2)}) async-start(f32[16,48,128]{2,1,0:T(8,128)} %get-tuple-element.39), calls=%async_computation.4 | async-start | bytes 786432 | tf_op jit(solution)/shard_map/all_to_all | solution.py:476
  106.2 3.7 %collective-permute-start = (f32[16,128]{1,0:T(8,128)S(1)}, f32[16,128]{1,0:T(8,128)S(1)}, u32[]{:S(2)}, u32[]{:S(2)}) collective-permute-start(f32[16,128]{1,0:T(8,128)S(1)} %get-tuple-element.40.refs_1_), channel_id=1, source_target_pairs={{0,1},{1,0},{2,3},{3,2},{4,5},{5,4},{6,7},{7,6},{8,9},{9,8},{10,11... | collective-permute-start | bytes 24584 | tf_op jit(solution)/shard_map/ppermute | solution.py:494
  109.9 0.8 collective-permute-done.refs_2_
  110.7 2.9 factor2.1
  113.6 3.3 %all-to-all-done.4 = f32[16,48,128]{2,1,0:T(8,128)S(1)} async-done(((f32[16,48,128]{2,1,0:T(8,128)}), f32[16,48,128]{2,1,0:T(8,128)S(1)}, u32[]{:S(2)}, u32[]{:S(2)}) %all-to-all-start.4) | async-done | bytes 393248 | tf_op jit(solution)/shard_map/all_to_all | solution.py:476
  117.0 1.4 half2.1
  118.4 16.4 %all_to_all.72.got_ref = f32[8,152,128]{2,1,0:T(8,128)S(1)} all-to-all(f32[8,152,128]{2,1,0:T(8,128)S(1)} %get-tuple-element.44), channel_id=1, replica_groups=mesh['zl'=4,'y'=4,'x'=4,'zh'=4,'core'=2] {'core','x'}, dimensions={0} | all-to-all | bytes 1245184 | tf_op jit(solution)/shard_map/all_to_all | solution.py:476
  134.8 16.9 %all_gather.20.got_ref.refs_0_ = f32[4,152,128]{2,1,0:T(8,128)S(1)} all-gather(f32[1,152,128]{2,1,0:T(8,128)S(1)} %fold.12), channel_id=1, replica_groups=mesh['zl'=4,'y'=4,'x'=4,'zh'=4,'core'=2] {'zh'}, dimensions={0}, use_global_device_ids=true | all-gather | bytes 389120 | tf_op jit(solution)/shard_map/all_gather | solution.py:482
  151.7 0.7 fold.13
  152.4 3.4 %all-to-all-start.6 = ((f32[4,128,128]{2,1,0:T(8,128)}), f32[4,128,128]{2,1,0:T(8,128)S(1)}, u32[]{:S(2)}, u32[]{:S(2)}) async-start(f32[4,128,128]{2,1,0:T(8,128)} %fold.13), calls=%async_computation.6 | async-start | bytes 524288 | tf_op jit(solution)/shard_map/all_to_all | solution.py:476
  155.9 2.4 factor3.1
  158.3 3.0 all-to-all-done.6
  161.3 7.7 %all_gather.21.refs_2_ = f32[1024,128]{1,0:T(8,128)S(1)} all-gather(f32[512,128]{1,0:T(8,128)S(1)} %bitcast.25), channel_id=1, replica_groups=mesh['zl'=4,'y'=4,'x'=4,'zh'=4,'core'=2] {'core'}, dimensions={0}, use_global_device_ids=true | all-gather | bytes 786432 | tf_op jit(solution)/shard_map/all_gather | solution.py:486
  169.0 1.4 half3.1
  170.4 17.3 %all_to_all.73.got_ref = f32[16,64,128]{2,1,0:T(8,128)S(1)} all-to-all(f32[16,64,128]{2,1,0:T(8,128)S(1)} %get-tuple-element.48), channel_id=1, replica_groups=mesh['zl'=4,'y'=4,'x'=4,'zh'=4,'core'=2] {'zl','y'}, dimensions={0} | all-to-all | bytes 1048576 | tf_op jit(solution)/shard_map/all_to_all | solution.py:476
  187.7 0.8 fold.14
  188.5 4.9 %all-to-all-start.8 = ((f32[16,48,128]{2,1,0:T(8,128)}), f32[16,48,128]{2,1,0:T(8,128)S(1)}, u32[]{:S(2)}, u32[]{:S(2)}) async-start(f32[16,48,128]{2,1,0:T(8,128)} %get-tuple-element.49), calls=%async_computation.8 | async-start | bytes 786432 | tf_op jit(solution)/shard_map/all_to_all | solution.py:476
  193.5 3.9 %collective-permute-start.1 = (f32[16,128]{1,0:T(8,128)S(1)}, f32[16,128]{1,0:T(8,128)S(1)}, u32[]{:S(2)}, u32[]{:S(2)}) collective-permute-start(f32[16,128]{1,0:T(8,128)S(1)} %get-tuple-element.50.refs_1_), channel_id=1, source_target_pairs={{0,1},{1,0},{2,3},{3,2},{4,5},{5,4},{6,7},{7,6},{8,9},{9,8},{10,11... | collective-permute-start | bytes 24584 | tf_op jit(solution)/shard_map/ppermute | solution.py:494
  198.0 2.9 factor4.1
  200.9 3.3 %all-to-all-done.8 = f32[16,48,128]{2,1,0:T(8,128)S(1)} async-done(((f32[16,48,128]{2,1,0:T(8,128)}), f32[16,48,128]{2,1,0:T(8,128)S(1)}, u32[]{:S(2)}, u32[]{:S(2)}) %all-to-all-start.8) | async-done | bytes 393248 | tf_op jit(solution)/shard_map/all_to_all | solution.py:476
  204.2 1.4 half4.1
  205.6 16.4 %all_to_all.74.got_ref = f32[8,152,128]{2,1,0:T(8,128)S(1)} all-to-all(f32[8,152,128]{2,1,0:T(8,128)S(1)} %get-tuple-element.54), channel_id=1, replica_groups=mesh['zl'=4,'y'=4,'x'=4,'zh'=4,'core'=2] {'core','x'}, dimensions={0} | all-to-all | bytes 1245184 | tf_op jit(solution)/shard_map/all_to_all | solution.py:476
  222.0 16.9 %all_gather.22.got_ref.refs_0_ = f32[4,152,128]{2,1,0:T(8,128)S(1)} all-gather(f32[1,152,128]{2,1,0:T(8,128)S(1)} %fold.15), channel_id=1, replica_groups=mesh['zl'=4,'y'=4,'x'=4,'zh'=4,'core'=2] {'zh'}, dimensions={0}, use_global_device_ids=true | all-gather | bytes 389120 | tf_op jit(solution)/shard_map/all_gather | solution.py:482
  239.7 3.4 %all-to-all-start.10 = ((f32[4,128,128]{2,1,0:T(8,128)}), f32[4,128,128]{2,1,0:T(8,128)S(1)}, u32[]{:S(2)}, u32[]{:S(2)}) async-start(f32[4,128,128]{2,1,0:T(8,128)} %fold.16), calls=%async_computation.10 | async-start | bytes 524288 | tf_op jit(solution)/shard_map/all_to_all | solution.py:476
  243.1 3.0 factor5.1
  246.1 2.5 all-to-all-done.10
  248.6 7.4 %all_gather.23.refs_2_ = f32[1024,128]{1,0:T(8,128)S(1)} all-gather(f32[512,128]{1,0:T(8,128)S(1)} %bitcast.24), channel_id=1, replica_groups=mesh['zl'=4,'y'=4,'x'=4,'zh'=4,'core'=2] {'core'}, dimensions={0}, use_global_device_ids=true | all-gather | bytes 786432 | tf_op jit(solution)/shard_map/all_gather | solution.py:486
  256.0 1.6 half5.1
  257.6 20.6 %all_to_all.75.got_ref = f32[16,72,128]{2,1,0:T(8,128)S(1)} all-to-all(f32[16,72,128]{2,1,0:T(8,128)S(1)} %get-tuple-element.59), channel_id=1, replica_groups=mesh['zl'=4,'y'=4,'x'=4,'zh'=4,'core'=2] {'zl','y'}, dimensions={0} | all-to-all | bytes 1179648 | tf_op jit(solution)/shard_map/all_to_all | solution.py:476
  278.2 2.5 last.1
  280.7 14.7 %all_to_all.76.got_ref = f32[32,24,128]{2,1,0:T(8,128)S(1)} all-to-all(f32[32,24,128]{2,1,0:T(8,128)S(1)} %get-tuple-element.62), channel_id=1, replica_groups=mesh['zl'=4,'y'=4,'x'=4,'zh'=4,'core'=2] {'core','y','x'}, dimensions={0} | all-to-all | bytes 786432 | tf_op jit(solution)/shard_map/all_to_all | solution.py:476
  295.5 18.7 %all_to_all.77.got_ref = f32[16,24,128]{2,1,0:T(8,128)S(1)} all-to-all(f32[16,24,128]{2,1,0:T(8,128)S(1)} %fold.17), channel_id=1, replica_groups=mesh['zl'=4,'y'=4,'x'=4,'zh'=4,'core'=2] {'zh','zl'}, dimensions={0} | all-to-all | bytes 393216 | tf_op jit(solution)/shard_map/all_to_all | solution.py:476
  314.2 2.6 end.1
  (19 shorter events, 2.3 us)
Async XLA Ops:
  0.6 22.4 %copy-start = (bf16[1,1,32,128,128]{4,3,2,1,0:T(8,128)(2,1)S(1)}, bf16[1,1,32,128,128]{4,3,2,1,0:T(8,128)(2,1)}, u32[]{:S(2)}) copy-start(bf16[1,1,32,128,128]{4,3,2,1,0:T(8,128)(2,1)} %param.6) | copy-start | bytes 3145732
  0.6 0.8 copy-start.1
  2.4 20.6 %all-to-all-start = ((f32[16,48,128]{2,1,0:T(8,128)}), f32[16,48,128]{2,1,0:T(8,128)S(1)}, u32[]{:S(2)}, u32[]{:S(2)}) async-start(f32[16,48,128]{2,1,0:T(8,128)} %pack.1), calls=%async_computation | async-start | bytes 786432 | tf_op jit(solution)/shard_map/all_to_all | solution.py:476
  12.3 0.8 copy-start.2
  12.3 0.7 copy-start.4
  65.5 3.5 %copy-start.3 = (s32[2048]{0:T(1024)S(1)}, s32[2048]{0:T(1024)}, u32[]{:S(2)}) copy-start(s32[2048]{0:T(1024)} %param.9) | copy-start | bytes 24580
  65.5 9.0 %all-to-all-start.2 = ((f32[4,128,128]{2,1,0:T(8,128)}), f32[4,128,128]{2,1,0:T(8,128)S(1)}, u32[]{:S(2)}, u32[]{:S(2)}) async-start(f32[4,128,128]{2,1,0:T(8,128)} %fold.10), calls=%async_computation.2 | async-start | bytes 524288 | tf_op jit(solution)/shard_map/all_to_all | solution.py:476
  101.3 15.7 %all-to-all-start.4 = ((f32[16,48,128]{2,1,0:T(8,128)}), f32[16,48,128]{2,1,0:T(8,128)S(1)}, u32[]{:S(2)}, u32[]{:S(2)}) async-start(f32[16,48,128]{2,1,0:T(8,128)} %get-tuple-element.39), calls=%async_computation.4 | async-start | bytes 786432 | tf_op jit(solution)/shard_map/all_to_all | solution.py:476
  106.2 4.5 %collective-permute-start = (f32[16,128]{1,0:T(8,128)S(1)}, f32[16,128]{1,0:T(8,128)S(1)}, u32[]{:S(2)}, u32[]{:S(2)}) collective-permute-start(f32[16,128]{1,0:T(8,128)S(1)} %get-tuple-element.40.refs_1_), channel_id=1, source_target_pairs={{0,1},{1,0},{2,3},{3,2},{4,5},{5,4},{6,7},{7,6},{8,9},{9,8},{10,11... | collective-permute-start | bytes 24584 | tf_op jit(solution)/shard_map/ppermute | solution.py:494
  152.4 8.9 %all-to-all-start.6 = ((f32[4,128,128]{2,1,0:T(8,128)}), f32[4,128,128]{2,1,0:T(8,128)S(1)}, u32[]{:S(2)}, u32[]{:S(2)}) async-start(f32[4,128,128]{2,1,0:T(8,128)} %fold.13), calls=%async_computation.6 | async-start | bytes 524288 | tf_op jit(solution)/shard_map/all_to_all | solution.py:476
  188.5 15.7 %all-to-all-start.8 = ((f32[16,48,128]{2,1,0:T(8,128)}), f32[16,48,128]{2,1,0:T(8,128)S(1)}, u32[]{:S(2)}, u32[]{:S(2)}) async-start(f32[16,48,128]{2,1,0:T(8,128)} %get-tuple-element.49), calls=%async_computation.8 | async-start | bytes 786432 | tf_op jit(solution)/shard_map/all_to_all | solution.py:476
  193.5 4.5 %collective-permute-start.1 = (f32[16,128]{1,0:T(8,128)S(1)}, f32[16,128]{1,0:T(8,128)S(1)}, u32[]{:S(2)}, u32[]{:S(2)}) collective-permute-start(f32[16,128]{1,0:T(8,128)S(1)} %get-tuple-element.50.refs_1_), channel_id=1, source_target_pairs={{0,1},{1,0},{2,3},{3,2},{4,5},{5,4},{6,7},{7,6},{8,9},{9,8},{10,11... | collective-permute-start | bytes 24584 | tf_op jit(solution)/shard_map/ppermute | solution.py:494
  239.7 8.9 %all-to-all-start.10 = ((f32[4,128,128]{2,1,0:T(8,128)}), f32[4,128,128]{2,1,0:T(8,128)S(1)}, u32[]{:S(2)}, u32[]{:S(2)}) async-start(f32[4,128,128]{2,1,0:T(8,128)} %fold.16), calls=%async_computation.10 | async-start | bytes 524288 | tf_op jit(solution)/shard_map/all_to_all | solution.py:476

commit v11 on v10

--- a/solution.py
+++ b/solution.py
@@ -380,14 +380,21 @@
         panel_ref, sent_ref = refs[:2]
     parts_ref, sums_ref = refs[-2:]
     inverse = split_three(factor_ref[:, BLOCK:])
-    for b in range(panel_ref.shape[0] // BLOCK):
-        where = slice(64 * b, 64 * b + 64)
-        value = exact_dot(
-            inverse, split_three(got_ref[where, :] * scale_ref[b : b + 1, :])
+    for b in range(0, panel_ref.shape[0] // BLOCK, 2):
+        wheres = [slice(64 * c, 64 * c + 64) for c in (b, b + 1)]
+        pair = jnp.concatenate(
+            [
+                got_ref[where, :] * scale_ref[c : c + 1, :]
+                for c, where in zip((b, b + 1), wheres)
+            ],
+            axis=1,
         )
-        if with_old:
-            value += part_ref[where, :]
-        panel_ref[where, :] = value
+        pair = exact_dot(inverse, split_three(pair))
+        for i, where in enumerate(wheres):
+            value = pair[:, TILE * i : TILE * i + TILE]
+            if with_old:
+                value += part_ref[where, :]
+            panel_ref[where, :] = value
     send_panel(
         table_ref, tiles_ref, panel_ref, scale_ref, sent_ref, parts_ref, sums_ref,
         forward=forward, cb=cb, owned=owned, ready=(table_copy,),

time: 322 us -> 322 us (level)
  no operation moved by 1% of the time
where the time goes in v11:
time: 322 us; the launch traced here: 318 us
  blocking collectives  219 us (68%)
  starting transfers between devices  36 us (11%)
  Pallas kernels  31.3 us (10%)
  waiting for transfers between devices  27.8 us (9%)
    all_to_all x8, blocking collectives, exchange(): return lax.all_to_all(messages, axes, 0, 0, tiled=True)  141 us
    all_gather x3, blocking collectives, sum_col(): got = lax.all_gather(own, 'zh', axis=0, tiled=False)  58.2 us
    all_to_all x6, starting transfers between devices, exchange(): return lax.all_to_all(messages, axes, 0, 0, tiled=True)  28.8 us
    all_to_all x6, waiting for transfers between devices, exchange(): return lax.all_to_all(messages, axes, 0, 0, tiled=True)  26.2 us
    all_gather x3, blocking collectives, sum_col(): return ([got], lax.all_gather(half, 'core', axis=0, tiled=True))  20.5 us
    pallas_call x5, Pallas kernels, per_device(): pl.pallas_call(functools.partial(factor_kernel, with_old=with_old, halves...  12.9 us
    ppermute x2, starting transfers between devices, sum_row(): other = lax.ppermute(own, 'core', [(0, 1), (1, 0)])  7.28 us
    pallas_call x5, Pallas kernels, per_device(): pl.pallas_call(functools.partial(step_kernel, forward=not users, cb=cb, w...  7.14 us
  transfers between devices with their start and end apart: 8, of which 8 were waited for; matrix products, arithmetic and copies ran while one was open for 0% of the time, Pallas kernels for 4%

profile of v11, /device:TPU:1, one launch (start us, length us, event | category | flops | bytes accessed | tf_op | source)
XLA Modules:
  0.0 317.6 jit_solution(5751557505993310683)
XLA Ops:
  0.7 0.8 copy-done.1
  1.5 0.9 pack.1
  2.4 9.2 %all-to-all-start = ((f32[16,48,128]{2,1,0:T(8,128)}), f32[16,48,128]{2,1,0:T(8,128)S(1)}, u32[]{:S(2)}, u32[]{:S(2)}) async-start(f32[16,48,128]{2,1,0:T(8,128)} %pack.1), calls=%async_computation | async-start | bytes 786432 | tf_op jit(solution)/shard_map/all_to_all | solution.py:483
  13.0 10.0 %all-to-all-done.got_ref = f32[16,48,128]{2,1,0:T(8,128)S(1)} async-done(((f32[16,48,128]{2,1,0:T(8,128)}), f32[16,48,128]{2,1,0:T(8,128)S(1)}, u32[]{:S(2)}, u32[]{:S(2)}) %all-to-all-start) | async-done | bytes 393248 | tf_op jit(solution)/shard_map/all_to_all | solution.py:483
  23.0 1.3 start.1
  24.3 17.5 %all_to_all.70.got_ref = f32[8,152,128]{2,1,0:T(8,128)S(1)} all-to-all(f32[8,152,128]{2,1,0:T(8,128)S(1)} %get-tuple-element.37), channel_id=1, replica_groups=mesh['zl'=4,'y'=4,'x'=4,'zh'=4,'core'=2] {'core','x'}, dimensions={0} | all-to-all | bytes 1245184 | tf_op jit(solution)/shard_map/all_to_all | solution.py:483
  41.8 22.7 %all_gather.18.got_ref.refs_0_ = f32[4,152,128]{2,1,0:T(8,128)S(1)} all-gather(f32[1,152,128]{2,1,0:T(8,128)S(1)} %fold.9), channel_id=1, replica_groups=mesh['zl'=4,'y'=4,'x'=4,'zh'=4,'core'=2] {'zh'}, dimensions={0}, use_global_device_ids=true | all-gather | bytes 389120 | tf_op jit(solution)/shard_map/all_gather | solution.py:489
  64.5 0.7 fold.10
  65.2 3.5 %all-to-all-start.2 = ((f32[4,128,128]{2,1,0:T(8,128)}), f32[4,128,128]{2,1,0:T(8,128)S(1)}, u32[]{:S(2)}, u32[]{:S(2)}) async-start(f32[4,128,128]{2,1,0:T(8,128)} %fold.10), calls=%async_computation.2 | async-start | bytes 524288 | tf_op jit(solution)/shard_map/all_to_all | solution.py:483
  68.8 1.7 factor1.1.refs_4_
  70.5 3.7 %all-to-all-done.2 = f32[4,128,128]{2,1,0:T(8,128)S(1)} async-done(((f32[4,128,128]{2,1,0:T(8,128)}), f32[4,128,128]{2,1,0:T(8,128)S(1)}, u32[]{:S(2)}, u32[]{:S(2)}) %all-to-all-start.2) | async-done | bytes 262176 | tf_op jit(solution)/shard_map/all_to_all | solution.py:483
  74.3 7.7 %all_gather.19.refs_2_ = f32[1024,128]{1,0:T(8,128)S(1)} all-gather(f32[512,128]{1,0:T(8,128)S(1)} %bitcast.26), channel_id=1, replica_groups=mesh['zl'=4,'y'=4,'x'=4,'zh'=4,'core'=2] {'core'}, dimensions={0}, use_global_device_ids=true | all-gather | bytes 786432 | tf_op jit(solution)/shard_map/all_gather | solution.py:493
  82.0 1.4 half1.1
  83.4 18.0 %all_to_all.71.got_ref = f32[16,64,128]{2,1,0:T(8,128)S(1)} all-to-all(f32[16,64,128]{2,1,0:T(8,128)S(1)} %get-tuple-element.38), channel_id=1, replica_groups=mesh['zl'=4,'y'=4,'x'=4,'zh'=4,'core'=2] {'zl','y'}, dimensions={0} | all-to-all | bytes 1048576 | tf_op jit(solution)/shard_map/all_to_all | solution.py:483
  101.3 0.8 fold.11
  102.1 4.6 %all-to-all-start.4 = ((f32[16,48,128]{2,1,0:T(8,128)}), f32[16,48,128]{2,1,0:T(8,128)S(1)}, u32[]{:S(2)}, u32[]{:S(2)}) async-start(f32[16,48,128]{2,1,0:T(8,128)} %get-tuple-element.39), calls=%async_computation.4 | async-start | bytes 786432 | tf_op jit(solution)/shard_map/all_to_all | solution.py:483
  106.8 3.6 %collective-permute-start = (f32[16,128]{1,0:T(8,128)S(1)}, f32[16,128]{1,0:T(8,128)S(1)}, u32[]{:S(2)}, u32[]{:S(2)}) collective-permute-start(f32[16,128]{1,0:T(8,128)S(1)} %get-tuple-element.40.refs_1_), channel_id=1, source_target_pairs={{0,1},{1,0},{2,3},{3,2},{4,5},{5,4},{6,7},{7,6},{8,9},{9,8},{10,11... | collective-permute-start | bytes 24584 | tf_op jit(solution)/shard_map/ppermute | solution.py:501
  110.4 0.8 collective-permute-done.refs_2_
  111.2 2.9 factor2.1
  114.1 3.4 %all-to-all-done.4 = f32[16,48,128]{2,1,0:T(8,128)S(1)} async-done(((f32[16,48,128]{2,1,0:T(8,128)}), f32[16,48,128]{2,1,0:T(8,128)S(1)}, u32[]{:S(2)}, u32[]{:S(2)}) %all-to-all-start.4) | async-done | bytes 393248 | tf_op jit(solution)/shard_map/all_to_all | solution.py:483
  117.6 1.3 half2.1
  118.9 16.3 %all_to_all.72.got_ref = f32[8,152,128]{2,1,0:T(8,128)S(1)} all-to-all(f32[8,152,128]{2,1,0:T(8,128)S(1)} %get-tuple-element.44), channel_id=1, replica_groups=mesh['zl'=4,'y'=4,'x'=4,'zh'=4,'core'=2] {'core','x'}, dimensions={0} | all-to-all | bytes 1245184 | tf_op jit(solution)/shard_map/all_to_all | solution.py:483
  135.2 17.7 %all_gather.20.got_ref.refs_0_ = f32[4,152,128]{2,1,0:T(8,128)S(1)} all-gather(f32[1,152,128]{2,1,0:T(8,128)S(1)} %fold.12), channel_id=1, replica_groups=mesh['zl'=4,'y'=4,'x'=4,'zh'=4,'core'=2] {'zh'}, dimensions={0}, use_global_device_ids=true | all-gather | bytes 389120 | tf_op jit(solution)/shard_map/all_gather | solution.py:489
  153.7 3.4 %all-to-all-start.6 = ((f32[4,128,128]{2,1,0:T(8,128)}), f32[4,128,128]{2,1,0:T(8,128)S(1)}, u32[]{:S(2)}, u32[]{:S(2)}) async-start(f32[4,128,128]{2,1,0:T(8,128)} %fold.13), calls=%async_computation.6 | async-start | bytes 524288 | tf_op jit(solution)/shard_map/all_to_all | solution.py:483
  157.1 2.4 factor3.1
  159.6 3.0 all-to-all-done.6
  162.6 6.5 %all_gather.21.refs_2_ = f32[1024,128]{1,0:T(8,128)S(1)} all-gather(f32[512,128]{1,0:T(8,128)S(1)} %bitcast.25), channel_id=1, replica_groups=mesh['zl'=4,'y'=4,'x'=4,'zh'=4,'core'=2] {'core'}, dimensions={0}, use_global_device_ids=true | all-gather | bytes 786432 | tf_op jit(solution)/shard_map/all_gather | solution.py:493
  169.1 1.3 half3.1
  170.4 18.4 %all_to_all.73.got_ref = f32[16,64,128]{2,1,0:T(8,128)S(1)} all-to-all(f32[16,64,128]{2,1,0:T(8,128)S(1)} %get-tuple-element.48), channel_id=1, replica_groups=mesh['zl'=4,'y'=4,'x'=4,'zh'=4,'core'=2] {'zl','y'}, dimensions={0} | all-to-all | bytes 1048576 | tf_op jit(solution)/shard_map/all_to_all | solution.py:483
  188.8 0.8 fold.14
  189.6 4.6 %all-to-all-start.8 = ((f32[16,48,128]{2,1,0:T(8,128)}), f32[16,48,128]{2,1,0:T(8,128)S(1)}, u32[]{:S(2)}, u32[]{:S(2)}) async-start(f32[16,48,128]{2,1,0:T(8,128)} %get-tuple-element.49), calls=%async_computation.8 | async-start | bytes 786432 | tf_op jit(solution)/shard_map/all_to_all | solution.py:483
  194.3 3.6 %collective-permute-start.1 = (f32[16,128]{1,0:T(8,128)S(1)}, f32[16,128]{1,0:T(8,128)S(1)}, u32[]{:S(2)}, u32[]{:S(2)}) collective-permute-start(f32[16,128]{1,0:T(8,128)S(1)} %get-tuple-element.50.refs_1_), channel_id=1, source_target_pairs={{0,1},{1,0},{2,3},{3,2},{4,5},{5,4},{6,7},{7,6},{8,9},{9,8},{10,11... | collective-permute-start | bytes 24584 | tf_op jit(solution)/shard_map/ppermute | solution.py:501
  197.9 0.8 collective-permute-done.1.refs_2_
  198.7 2.9 factor4.1
  201.6 3.4 %all-to-all-done.8 = f32[16,48,128]{2,1,0:T(8,128)S(1)} async-done(((f32[16,48,128]{2,1,0:T(8,128)}), f32[16,48,128]{2,1,0:T(8,128)S(1)}, u32[]{:S(2)}, u32[]{:S(2)}) %all-to-all-start.8) | async-done | bytes 393248 | tf_op jit(solution)/shard_map/all_to_all | solution.py:483
  205.1 1.5 half4.1
  206.6 16.3 %all_to_all.74.got_ref = f32[8,152,128]{2,1,0:T(8,128)S(1)} all-to-all(f32[8,152,128]{2,1,0:T(8,128)S(1)} %get-tuple-element.54), channel_id=1, replica_groups=mesh['zl'=4,'y'=4,'x'=4,'zh'=4,'core'=2] {'core','x'}, dimensions={0} | all-to-all | bytes 1245184 | tf_op jit(solution)/shard_map/all_to_all | solution.py:483
  222.9 17.8 %all_gather.22.got_ref.refs_0_ = f32[4,152,128]{2,1,0:T(8,128)S(1)} all-gather(f32[1,152,128]{2,1,0:T(8,128)S(1)} %fold.15), channel_id=1, replica_groups=mesh['zl'=4,'y'=4,'x'=4,'zh'=4,'core'=2] {'zh'}, dimensions={0}, use_global_device_ids=true | all-gather | bytes 389120 | tf_op jit(solution)/shard_map/all_gather | solution.py:489
  241.4 3.4 %all-to-all-start.10 = ((f32[4,128,128]{2,1,0:T(8,128)}), f32[4,128,128]{2,1,0:T(8,128)S(1)}, u32[]{:S(2)}, u32[]{:S(2)}) async-start(f32[4,128,128]{2,1,0:T(8,128)} %fold.16), calls=%async_computation.10 | async-start | bytes 524288 | tf_op jit(solution)/shard_map/all_to_all | solution.py:483
  244.8 3.0 factor5.1
  247.8 2.5 all-to-all-done.10
  250.3 6.3 %all_gather.23.refs_2_ = f32[1024,128]{1,0:T(8,128)S(1)} all-gather(f32[512,128]{1,0:T(8,128)S(1)} %bitcast.24), channel_id=1, replica_groups=mesh['zl'=4,'y'=4,'x'=4,'zh'=4,'core'=2] {'core'}, dimensions={0}, use_global_device_ids=true | all-gather | bytes 786432 | tf_op jit(solution)/shard_map/all_gather | solution.py:493
  256.6 1.6 half5.1
  258.2 21.5 %all_to_all.75.got_ref = f32[16,72,128]{2,1,0:T(8,128)S(1)} all-to-all(f32[16,72,128]{2,1,0:T(8,128)S(1)} %get-tuple-element.59), channel_id=1, replica_groups=mesh['zl'=4,'y'=4,'x'=4,'zh'=4,'core'=2] {'zl','y'}, dimensions={0} | all-to-all | bytes 1179648 | tf_op jit(solution)/shard_map/all_to_all | solution.py:483
  279.7 2.5 last.1
  282.2 14.1 %all_to_all.76.got_ref = f32[32,24,128]{2,1,0:T(8,128)S(1)} all-to-all(f32[32,24,128]{2,1,0:T(8,128)S(1)} %get-tuple-element.62), channel_id=1, replica_groups=mesh['zl'=4,'y'=4,'x'=4,'zh'=4,'core'=2] {'core','y','x'}, dimensions={0} | all-to-all | bytes 786432 | tf_op jit(solution)/shard_map/all_to_all | solution.py:483
  296.3 18.6 %all_to_all.77.got_ref = f32[16,24,128]{2,1,0:T(8,128)S(1)} all-to-all(f32[16,24,128]{2,1,0:T(8,128)S(1)} %fold.17), channel_id=1, replica_groups=mesh['zl'=4,'y'=4,'x'=4,'zh'=4,'core'=2] {'zh','zl'}, dimensions={0} | all-to-all | bytes 393216 | tf_op jit(solution)/shard_map/all_to_all | solution.py:483
  314.9 2.6 end.1
  (19 shorter events, 2.4 us)
Async XLA Ops:
  0.6 22.4 %copy-start = (bf16[1,1,32,128,128]{4,3,2,1,0:T(8,128)(2,1)S(1)}, bf16[1,1,32,128,128]{4,3,2,1,0:T(8,128)(2,1)}, u32[]{:S(2)}) copy-start(bf16[1,1,32,128,128]{4,3,2,1,0:T(8,128)(2,1)} %param.6) | copy-start | bytes 3145732
  0.6 0.8 copy-start.1
  2.4 20.6 %all-to-all-start = ((f32[16,48,128]{2,1,0:T(8,128)}), f32[16,48,128]{2,1,0:T(8,128)S(1)}, u32[]{:S(2)}, u32[]{:S(2)}) async-start(f32[16,48,128]{2,1,0:T(8,128)} %pack.1), calls=%async_computation | async-start | bytes 786432 | tf_op jit(solution)/shard_map/all_to_all | solution.py:483
  12.3 0.8 copy-start.2
  12.3 0.7 copy-start.4
  65.2 3.5 %copy-start.3 = (s32[2048]{0:T(1024)S(1)}, s32[2048]{0:T(1024)}, u32[]{:S(2)}) copy-start(s32[2048]{0:T(1024)} %param.9) | copy-start | bytes 24580
  65.2 9.0 %all-to-all-start.2 = ((f32[4,128,128]{2,1,0:T(8,128)}), f32[4,128,128]{2,1,0:T(8,128)S(1)}, u32[]{:S(2)}, u32[]{:S(2)}) async-start(f32[4,128,128]{2,1,0:T(8,128)} %fold.10), calls=%async_computation.2 | async-start | bytes 524288 | tf_op jit(solution)/shard_map/all_to_all | solution.py:483
  102.1 15.4 %all-to-all-start.4 = ((f32[16,48,128]{2,1,0:T(8,128)}), f32[16,48,128]{2,1,0:T(8,128)S(1)}, u32[]{:S(2)}, u32[]{:S(2)}) async-start(f32[16,48,128]{2,1,0:T(8,128)} %get-tuple-element.39), calls=%async_computation.4 | async-start | bytes 786432 | tf_op jit(solution)/shard_map/all_to_all | solution.py:483
  106.8 4.5 %collective-permute-start = (f32[16,128]{1,0:T(8,128)S(1)}, f32[16,128]{1,0:T(8,128)S(1)}, u32[]{:S(2)}, u32[]{:S(2)}) collective-permute-start(f32[16,128]{1,0:T(8,128)S(1)} %get-tuple-element.40.refs_1_), channel_id=1, source_target_pairs={{0,1},{1,0},{2,3},{3,2},{4,5},{5,4},{6,7},{7,6},{8,9},{9,8},{10,11... | collective-permute-start | bytes 24584 | tf_op jit(solution)/shard_map/ppermute | solution.py:501
  153.7 8.9 %all-to-all-start.6 = ((f32[4,128,128]{2,1,0:T(8,128)}), f32[4,128,128]{2,1,0:T(8,128)S(1)}, u32[]{:S(2)}, u32[]{:S(2)}) async-start(f32[4,128,128]{2,1,0:T(8,128)} %fold.13), calls=%async_computation.6 | async-start | bytes 524288 | tf_op jit(solution)/shard_map/all_to_all | solution.py:483
  189.6 15.4 %all-to-all-start.8 = ((f32[16,48,128]{2,1,0:T(8,128)}), f32[16,48,128]{2,1,0:T(8,128)S(1)}, u32[]{:S(2)}, u32[]{:S(2)}) async-start(f32[16,48,128]{2,1,0:T(8,128)} %get-tuple-element.49), calls=%async_computation.8 | async-start | bytes 786432 | tf_op jit(solution)/shard_map/all_to_all | solution.py:483
  194.3 4.5 %collective-permute-start.1 = (f32[16,128]{1,0:T(8,128)S(1)}, f32[16,128]{1,0:T(8,128)S(1)}, u32[]{:S(2)}, u32[]{:S(2)}) collective-permute-start(f32[16,128]{1,0:T(8,128)S(1)} %get-tuple-element.50.refs_1_), channel_id=1, source_target_pairs={{0,1},{1,0},{2,3},{3,2},{4,5},{5,4},{6,7},{7,6},{8,9},{9,8},{10,11... | collective-permute-start | bytes 24584 | tf_op jit(solution)/shard_map/ppermute | solution.py:501
  241.4 8.9 %all-to-all-start.10 = ((f32[4,128,128]{2,1,0:T(8,128)}), f32[4,128,128]{2,1,0:T(8,128)S(1)}, u32[]{:S(2)}, u32[]{:S(2)}) async-start(f32[4,128,128]{2,1,0:T(8,128)} %fold.16), calls=%async_computation.10 | async-start | bytes 524288 | tf_op jit(solution)/shard_map/all_to_all | solution.py:483
